TPU v7x, 128 devices: a whole 4x4x4 slice. The times are simulated.
128 devices in a mesh: agg: 8 (over y, core), blk: 16 (over x, z).
Axes of the slice: x: 4, y: 4, z: 4, core: 2. Of those that a mesh axis runs over, the one named last changes fastest.
Arguments:
- right_side: float32 [256, 512, 128], P('blk', 'agg'), may hold values from -8 to 8
- coefficient: float32 [256, 512, 128], P('blk', 'agg'), may hold values from 0.05 to 2
Outputs:
- pressure: float32 [256, 512, 128], P('blk', 'agg')
All inputs are finite; a program needn't handle non-finite values.
Results may differ from a plain program's by a relative error of at most 0.0001.
Values sent between devices are 32-bit elements; how exact they have to be, the bound alone decides.
No kernel may reach another device: no remote copies, remote signals or barrier semaphores. Data moves between devices by JAX's collectives and lax.ppermute only.
A program may use at most 128 MiB of HBM per device.

v0:
```python
import jax
import jax.numpy as jnp
from jax import lax
from jax.sharding import PartitionSpec as P

OMEGA = 0.8


def padded_2(x, sides, width):
    for axis, dim in sides:
        size, length = (lax.axis_size(axis), x.shape[dim])
        up = [(i, (i + 1) % size) for i in range(size - 1)]
        down = [(j, i) for i, j in up]
        last = lax.slice_in_dim(x, length - width, length, axis=dim)
        first = lax.slice_in_dim(x, 0, width, axis=dim)
        before = lax.ppermute(last, axis, up)
        after = lax.ppermute(first, axis, down)
        x = jnp.concatenate([before, x, after], axis=dim)
    return x


def from_partner(block, axis, apart):
    count = lax.axis_size(axis)
    route = []
    for low in range(count):
        high = low | 1 << apart
        if high != low and high < count:
            route += [(low, high), (high, low)]
    return lax.ppermute(block, axis, route)


def depth_pair(field):
    depth = field.shape[2]
    column = lax.broadcasted_iota(jnp.int32, field.shape, 2)
    ahead = jnp.where(column < depth - 1, jnp.roll(field, -1, axis=2), 0.0)
    behind = jnp.where(column > 0, jnp.roll(field, 1, axis=2), 0.0)
    return ahead + behind


def fine_apply(field, coef):
    padded = padded_2(field, (("blk", 0), ("agg", 1)), 1)
    total = padded[2:, 1:-1] + padded[:-2, 1:-1]
    total = total + padded[1:-1, 2:] + padded[1:-1, :-2]
    total = total + depth_pair(field)
    return (6.0 + coef) * field - total


def coarse_apply(field, coef, window):
    nx, ny, nz = field.shape
    padded = padded_2(field, (("blk", 0),), 1)
    total = padded[2:] + padded[:-2] + depth_pair(field)
    shaped = field.reshape(nx, ny // window, window, nz)
    edged = jnp.pad(shaped, ((0, 0), (0, 0), (1, 1), (0, 0)))
    total = total + (edged[:, :, 2:] + edged[:, :, :-2]).reshape(nx, ny, nz)
    return (6.0 + coef) * field - total


def restrict(field):
    nx, ny, nz = field.shape
    return field.reshape(nx // 2, 2, ny // 2, 2, nz // 2, 2).sum(axis=(1, 3, 5)) * 0.5


def prolong(field):
    nx, ny, nz = field.shape
    spread = jnp.broadcast_to(field[:, None, :, None, :, None], (nx, 2, ny, 2, nz, 2))
    return spread.reshape(2 * nx, 2 * ny, 2 * nz)


def joined(mine, other, upper):
    first = jnp.where(upper, other, mine)
    second = jnp.where(upper, mine, other)
    return jnp.concatenate((first, second), axis=1)


def shards(right_side, coefficient):
    levels = lax.axis_size("agg").bit_length() - 1
    rows = right_side.shape[1]
    place = lax.axis_index("agg")
    fine_inverse = 1.0 / (6.0 + coefficient)
    fine = OMEGA * right_side * fine_inverse
    fine = fine + OMEGA * (right_side - fine_apply(fine, coefficient)) * fine_inverse
    resid = right_side - fine_apply(fine, coefficient)
    level_rhs = restrict(resid)
    level_coef = coefficient
    rhs_list = []
    coef_list = []
    err_list = []
    for level in range(1, levels + 1):
        upper = place >> level - 1 & 1 == 1
        if level > 1:
            level_rhs = restrict(resid)
        level_coef = restrict(coefficient) if level == 1 else restrict(coef_list[-1])
        other_rhs, other_coef = from_partner((level_rhs, level_coef), "agg", level - 1)
        level_rhs = joined(level_rhs, other_rhs, upper)
        level_coef = joined(level_coef, other_coef, upper)
        inverse = 1.0 / (6.0 + level_coef)
        err = OMEGA * level_rhs * inverse
        if level == levels:
            err = err + OMEGA * (level_rhs - coarse_apply(err, level_coef, rows)) * inverse
        else:
            resid = level_rhs - coarse_apply(err, level_coef, rows)
        rhs_list.append(level_rhs)
        coef_list.append(level_coef)
        err_list.append(err)
    for level in range(levels, 0, -1):
        coarse = err_list[level - 1]
        high = place >> level - 1 & 1
        half = coarse.shape[1] // 2
        coarse = lax.dynamic_slice_in_dim(coarse, high * half, half, 1)
        if level > 1:
            below_rhs = rhs_list[level - 2]
            below_coef = coef_list[level - 2]
            merged = err_list[level - 2] + prolong(coarse)
            merged = merged + OMEGA * (below_rhs - coarse_apply(merged, below_coef, rows)) / (
                6.0 + below_coef
            )
            err_list[level - 2] = merged
        else:
            fine = fine + prolong(coarse)
            fine = fine + OMEGA * (right_side - fine_apply(fine, coefficient)) * fine_inverse
    return fine


def solution(mesh):
    placed = (P("blk", "agg", None), P("blk", "agg", None))
    return jax.shard_map(
        shards, mesh=mesh, in_specs=placed, out_specs=P("blk", "agg", None), check_vma=False
    )
```

profile of v0, /device:TPU:14, one launch (start us, length us, event | category | flops | bytes accessed | tf_op | source)
XLA Modules:
  0.0 334.7 jit_solution(6450900750359924074)
XLA Ops:
  0.0 1.3 multiply_multiply_fusion
  1.3 6.2 %collective-permute-start = (f32[1,64,128]{2,1,0:T(8,128)S(1)}, f32[1,64,128]{2,1,0:T(8,128)S(1)}, u32[]{:S(2)}, u32[]{:S(2)}) collective-permute-start(f32[1,64,128]{2,1,0:T(8,128)S(1)} %get-tuple-element.30), channel_id=1, source_target_pairs={{1,0},{2,1},{3,2},{4,3},{5,4},{6,5},{7,6},{8,7},{9,8},{10,9},{11,1... | collective-permute-start | bytes 98312 | tf_op jit(solution)/shard_map/ppermute | solution.py:17
  7.5 1.9 collective-permute-start.1
  9.4 35.6 %reshape.299 = f32[8,2,32,2,64,2]{5,4,3,2,1,0:T(8,128)} reshape(f32[16,64,128]{2,1,0:T(8,128)} %param.3) | data formatting | bytes 1048576 | tf_op jit(solution)/shard_map/reshape | solution.py:60
  45.1 12.3 %reduce_sum.55 = f32[8,32,64]{2,1,0:T(8,128)S(1)} reduce(f32[8,2,32,2,64,2]{5,4,3,2,1,0:T(8,128)} %reshape.299, f32[]{:T(128)} %constant.20.clone.1), dimensions={1,3,5}, to_apply=%region_1.2 | reduce | flops 114688 | bytes 589828 | tf_op jit(solution)/shard_map/reduce_sum | solution.py:60
  58.3 1.2 fusion.85
  60.0 2.5 collective-permute-start.2
  62.5 1.9 collective-permute-start.3
  65.0 2.5 collective-permute-done.3
  67.5 1.7 fusion.21
  69.2 6.0 %collective-permute-start.4 = (f32[1,64,128]{2,1,0:T(8,128)S(1)}, f32[1,64,128]{2,1,0:T(8,128)S(1)}, u32[]{:S(2)}, u32[]{:S(2)}) collective-permute-start(f32[1,64,128]{2,1,0:T(8,128)S(1)} %get-tuple-element.24), channel_id=1, source_target_pairs={{1,0},{2,1},{3,2},{4,3},{5,4},{6,5},{7,6},{8,7},{9,8},{10,9},{11,1... | collective-permute-start | bytes 98312 | tf_op jit(solution)/shard_map/ppermute | solution.py:17
  75.3 1.9 collective-permute-start.5
  77.4 5.8 %collective-permute-done.5 = f32[1,64,128]{2,1,0:T(8,128)S(1)} collective-permute-done((f32[1,64,128]{2,1,0:T(8,128)S(1)}, f32[1,64,128]{2,1,0:T(8,128)S(1)}, u32[]{:S(2)}, u32[]{:S(2)}) %collective-permute-start.5) | collective-permute-done | bytes 32800 | tf_op jit(solution)/shard_map/ppermute | solution.py:16
  83.2 1.9 collective-permute-start.6
  85.1 2.4 collective-permute-start.7
  87.8 2.4 collective-permute-done.7
  90.6 34.8 %reshape.298 = f32[8,2,32,2,64,2]{5,4,3,2,1,0:T(8,128)} reshape(f32[16,64,128]{2,1,0:T(8,128)S(1)} %fusion.12) | data formatting | bytes 1048576 | tf_op jit(solution)/shard_map/reshape | solution.py:60
  125.4 12.2 %reduce_sum.54 = f32[8,32,64]{2,1,0:T(8,128)S(1)} reduce(f32[8,2,32,2,64,2]{5,4,3,2,1,0:T(8,128)} %reshape.298, f32[]{:T(128)} %constant.20.clone.1), dimensions={1,3,5}, to_apply=%region_0.1 | reduce | flops 114688 | bytes 589828 | tf_op jit(solution)/shard_map/reduce_sum | solution.py:60
  137.8 1.3 collective-permute-done.8
  139.5 10.1 %reshape.302 = f32[4,2,32,2,32,2]{5,4,3,2,1,0:T(8,128)} reshape(f32[8,64,64]{2,1,0:T(8,128)S(1)} %get-tuple-element.39) | data formatting | bytes 262144 | tf_op jit(solution)/shard_map/reshape | solution.py:60
  149.6 4.1 %reduce_sum.57 = f32[4,32,32]{2,1,0:T(8,128)S(1)} reduce(f32[4,2,32,2,32,2]{5,4,3,2,1,0:T(8,128)} %reshape.302, f32[]{:T(128)} %constant.20.clone.1), dimensions={1,3,5}, to_apply=%region_3.4 | reduce | flops 28672 | bytes 147460 | tf_op jit(solution)/shard_map/reduce_sum | solution.py:60
  153.8 1.9 collective-permute-start.10
  155.7 3.9 %collective-permute-start.11 = (f32[1,64,64]{2,1,0:T(8,128)S(1)}, f32[1,64,64]{2,1,0:T(8,128)S(1)}, u32[]{:S(2)}, u32[]{:S(2)}) collective-permute-start(f32[1,64,64]{2,1,0:T(8,128)S(1)} %get-tuple-element.46), channel_id=1, source_target_pairs={{0,1},{1,2},{2,3},{3,4},{4,5},{5,6},{6,7},{7,8},{8,9},{9,10},{10,1... | collective-permute-start | bytes 49160 | tf_op jit(solution)/shard_map/ppermute | solution.py:16
  159.7 3.9 %collective-permute-done.11 = f32[1,64,64]{2,1,0:T(8,128)S(1)} collective-permute-done((f32[1,64,64]{2,1,0:T(8,128)S(1)}, f32[1,64,64]{2,1,0:T(8,128)S(1)}, u32[]{:S(2)}, u32[]{:S(2)}) %collective-permute-start.11) | collective-permute-done | bytes 16416 | tf_op jit(solution)/shard_map/ppermute | solution.py:16
  163.6 1.0 broadcast_add_fusion
  164.6 10.1 %reshape.301 = f32[4,2,32,2,32,2]{5,4,3,2,1,0:T(8,128)} reshape(f32[8,64,64]{2,1,0:T(8,128)S(1)} %get-tuple-element.32) | data formatting | bytes 262144 | tf_op jit(solution)/shard_map/reshape | solution.py:60
  174.7 4.1 %reduce_sum.56 = f32[4,32,32]{2,1,0:T(8,128)S(1)} reduce(f32[4,2,32,2,32,2]{5,4,3,2,1,0:T(8,128)} %reshape.301, f32[]{:T(128)} %constant.20.clone.1), dimensions={1,3,5}, to_apply=%region_2.3 | reduce | flops 28672 | bytes 147460 | tf_op jit(solution)/shard_map/reduce_sum | solution.py:60
  178.8 2.3 collective-permute-start.12
  181.9 1.4 collective-permute-done.12
  186.2 3.0 reshape.305
  190.1 3.0 collective-permute-start.17
  193.1 1.9 collective-permute-start.14
  195.0 3.9 %collective-permute-start.15 = (f32[1,64,32]{2,1,0:T(8,128)}, f32[1,64,32]{2,1,0:T(8,128)S(1)}, u32[]{:S(2)}, u32[]{:S(2)}) collective-permute-start(f32[1,64,32]{2,1,0:T(8,128)} %get-tuple-element.66), channel_id=1, source_target_pairs={{0,1},{1,2},{2,3},{3,4},{4,5},{5,6},{6,7},{7,8},{8,9},{9,10},{10,1... | collective-permute-start | bytes 24584 | tf_op jit(solution)/shard_map/ppermute | solution.py:16
  198.9 1.0 fusion.60
  199.9 3.2 collective-permute-done.15
  203.1 1.9 broadcast_add_fusion.1
  205.8 3.0 reshape.304
  211.6 4.0 %collective-permute-done.16 = f32[2,32,16]{1,2,0:T(8,128)S(1)} collective-permute-done((f32[2,32,16]{1,2,0:T(8,128)S(1)}, f32[2,32,16]{1,2,0:T(8,128)S(1)}, u32[]{:S(2)}, u32[]{:S(2)}) %collective-permute-start.16) | collective-permute-done | bytes 4128 | tf_op jit(solution)/shard_map/ppermute | solution.py:29
  216.4 1.9 collective-permute-start.18
  218.3 3.9 %collective-permute-start.19 = (f32[1,64,16]{1,2,0:T(8,128)S(1)}, f32[1,64,16]{1,2,0:T(8,128)S(1)}, u32[]{:S(2)}, u32[]{:S(2)}) collective-permute-start(f32[1,64,16]{1,2,0:T(8,128)S(1)} %get-tuple-element.80), channel_id=1, source_target_pairs={{0,1},{1,2},{2,3},{3,4},{4,5},{5,6},{6,7},{7,8},{8,9},{9,10},{10,1... | collective-permute-start | bytes 12296 | tf_op jit(solution)/shard_map/ppermute | solution.py:16
  222.4 3.5 %collective-permute-done.19 = f32[1,64,16]{1,2,0:T(8,128)S(1)} collective-permute-done((f32[1,64,16]{1,2,0:T(8,128)S(1)}, f32[1,64,16]{1,2,0:T(8,128)S(1)}, u32[]{:S(2)}, u32[]{:S(2)}) %collective-permute-start.19) | collective-permute-done | bytes 4128 | tf_op jit(solution)/shard_map/ppermute | solution.py:16
  227.2 2.3 reshape.307
  229.4 1.6 copy.6
  234.0 2.3 reshape.308
  236.3 1.9 collective-permute-start.20
  238.2 4.1 %collective-permute-start.21 = (f32[1,64,32]{2,1,0:T(8,128)}, f32[1,64,32]{2,1,0:T(8,128)S(1)}, u32[]{:S(2)}, u32[]{:S(2)}) collective-permute-start(f32[1,64,32]{2,1,0:T(8,128)} %get-tuple-element.58), channel_id=1, source_target_pairs={{0,1},{1,2},{2,3},{3,4},{4,5},{5,6},{6,7},{7,8},{8,9},{9,10},{10,1... | collective-permute-start | bytes 24584 | tf_op jit(solution)/shard_map/ppermute | solution.py:16
  244.3 2.1 collective-permute-done.21
  246.3 1.3 fusion.56
  248.6 4.0 %broadcast_in_dim.51 = f32[4,2,32,2,32,2]{5,4,3,2,1,0:T(8,128)} broadcast(f32[4,32,32]{2,1,0:T(8,128)S(1)} %fusion.67), dimensions={0,2,4} | broadcast | bytes 147456 | tf_op jit(solution)/shard_map/broadcast_in_dim | solution.py:65
  252.5 8.2 %reshape.310 = f32[8,64,64]{2,1,0:T(8,128)S(1)} reshape(f32[4,2,32,2,32,2]{5,4,3,2,1,0:T(8,128)} %broadcast_in_dim.51) | data formatting | bytes 262144 | tf_op jit(solution)/shard_map/reshape | solution.py:66
  261.1 8.2 %reshape.311 = f32[8,1,64,64]{3,2,0,1:T(8,128)S(1)} reshape(f32[4,2,32,2,32,2]{5,4,3,2,1,0:T(8,128)} %broadcast_in_dim.51) | data formatting | bytes 262144 | tf_op jit(solution)/shard_map/reshape | solution.py:66
  269.3 2.0 collective-permute-start.22
  271.3 3.8 %collective-permute-start.23 = (f32[1,64,64]{2,1,0:T(8,128)S(1)}, f32[1,64,64]{2,1,0:T(8,128)S(1)}, u32[]{:S(2)}, u32[]{:S(2)}) collective-permute-start(f32[1,64,64]{2,1,0:T(8,128)S(1)} %get-tuple-element.38), channel_id=1, source_target_pairs={{0,1},{1,2},{2,3},{3,4},{4,5},{5,6},{6,7},{7,8},{8,9},{9,10},{10,1... | collective-permute-start | bytes 49160 | tf_op jit(solution)/shard_map/ppermute | solution.py:16
  275.3 3.9 %collective-permute-done.23 = f32[1,64,64]{2,1,0:T(8,128)S(1)} collective-permute-done((f32[1,64,64]{2,1,0:T(8,128)S(1)}, f32[1,64,64]{2,1,0:T(8,128)S(1)}, u32[]{:S(2)}, u32[]{:S(2)}) %collective-permute-start.23) | collective-permute-done | bytes 16416 | tf_op jit(solution)/shard_map/ppermute | solution.py:16
  279.4 1.0 fusion.53
  280.4 11.4 %broadcast_in_dim.52 = f32[8,2,32,2,64,2]{5,4,3,2,1,0:T(8,128)} broadcast(f32[8,32,64]{2,1,0:T(8,128)S(1)} %fusion.53), dimensions={0,2,4} | broadcast | bytes 589824 | tf_op jit(solution)/shard_map/broadcast_in_dim | solution.py:65
  291.9 24.1 %reshape.313 = f32[16,64,128]{2,1,0:T(8,128)S(1)} reshape(f32[8,2,32,2,64,2]{5,4,3,2,1,0:T(8,128)} %broadcast_in_dim.52) | data formatting | bytes 1048576 | tf_op jit(solution)/shard_map/reshape | solution.py:66
  316.0 1.9 collective-permute-start.24
  317.9 3.9 %collective-permute-start.25 = (f32[1,64,128]{2,1,0:T(8,128)S(1)}, f32[1,64,128]{2,1,0:T(8,128)S(1)}, u32[]{:S(2)}, u32[]{:S(2)}) collective-permute-start(f32[1,64,128]{2,1,0:T(8,128)S(1)} %get-tuple-element.17), channel_id=1, source_target_pairs={{0,1},{1,2},{2,3},{3,4},{4,5},{5,6},{6,7},{7,8},{8,9},{9,10},{10,1... | collective-permute-start | bytes 98312 | tf_op jit(solution)/shard_map/ppermute | solution.py:16
  322.1 3.8 %collective-permute-done.25 = f32[1,64,128]{2,1,0:T(8,128)S(1)} collective-permute-done((f32[1,64,128]{2,1,0:T(8,128)S(1)}, f32[1,64,128]{2,1,0:T(8,128)S(1)}, u32[]{:S(2)}, u32[]{:S(2)}) %collective-permute-start.25) | collective-permute-done | bytes 32800 | tf_op jit(solution)/shard_map/ppermute | solution.py:16
  325.9 1.9 collective-permute-start.26
  327.8 2.4 collective-permute-start.27
  330.4 2.9 collective-permute-done.27
  333.4 1.3 fusion.6
  (136 shorter events, 20.9 us)
Async XLA Ops:
  1.3 58.7 %collective-permute-start = (f32[1,64,128]{2,1,0:T(8,128)S(1)}, f32[1,64,128]{2,1,0:T(8,128)S(1)}, u32[]{:S(2)}, u32[]{:S(2)}) collective-permute-start(f32[1,64,128]{2,1,0:T(8,128)S(1)} %get-tuple-element.30), channel_id=1, source_target_pairs={{1,0},{2,1},{3,2},{4,3},{5,4},{6,5},{7,6},{8,7},{9,8},{10,9},{11,1... | collective-permute-start | bytes 98312 | tf_op jit(solution)/shard_map/ppermute | solution.py:17
  7.5 52.5 %collective-permute-start.1 = (f32[1,64,128]{2,1,0:T(8,128)S(1)}, f32[1,64,128]{2,1,0:T(8,128)S(1)}, u32[]{:S(2)}, u32[]{:S(2)}) collective-permute-start(f32[1,64,128]{2,1,0:T(8,128)S(1)} %get-tuple-element.29), channel_id=1, source_target_pairs={{0,1},{1,2},{2,3},{3,4},{4,5},{5,6},{6,7},{7,8},{8,9},{9,10},{10,1... | collective-permute-start | bytes 98312 | tf_op jit(solution)/shard_map/ppermute | solution.py:16
  45.1 22.4 %copy-start = (f32[16,64,128]{2,1,0:T(8,128)S(1)}, f32[16,64,128]{2,1,0:T(8,128)}, u32[]{:S(2)}) copy-start(f32[16,64,128]{2,1,0:T(8,128)} %param.3) | copy-start | bytes 1572868
  45.1 22.4 %copy-start.1 = (f32[16,64,128]{2,1,0:T(8,128)S(1)}, f32[16,64,128]{2,1,0:T(8,128)}, u32[]{:S(2)}) copy-start(f32[16,64,128]{2,1,0:T(8,128)} %param.2) | copy-start | bytes 1572868
  58.0 79.7 %collective-permute-start.9 = (f32[8,32,64]{2,1,0:T(8,128)}, f32[8,32,64]{2,1,0:T(8,128)S(1)}, u32[]{:S(2)}, u32[]{:S(2)}) collective-permute-start(f32[8,32,64]{2,1,0:T(8,128)} %broadcast_multiply_fusion), channel_id=1, source_target_pairs={{0,16},{16,0},{32,48},{48,32},{64,80},{80,64},{96,112},{112,96},{1... | collective-permute-start | bytes 196616 | tf_op jit(solution)/shard_map/ppermute | solution.py:29
  59.4 66.0 %copy-start.15 = (pred[128]{0:T(512)(128)(4,1)}, pred[128]{0:T(512)(128)(4,1)S(1)}, u32[]{:S(2)}) copy-start(pred[128]{0:T(512)(128)(4,1)S(1)} %get-tuple-element.81) | copy-start | bytes 388
  59.4 66.0 %copy-start.17 = (pred[128]{0:T(512)(128)(4,1)}, pred[128]{0:T(512)(128)(4,1)S(1)}, u32[]{:S(2)}) copy-start(pred[128]{0:T(512)(128)(4,1)S(1)} %get-tuple-element.82) | copy-start | bytes 388
  59.4 104.2 %copy-start.19 = (pred[64]{0:T(512)(128)(4,1)}, pred[64]{0:T(512)(128)(4,1)S(1)}, u32[]{:S(2)}) copy-start(pred[64]{0:T(512)(128)(4,1)S(1)} %get-tuple-element.83) | copy-start | bytes 196
  59.4 104.2 %copy-start.21 = (pred[64]{0:T(512)(128)(4,1)}, pred[64]{0:T(512)(128)(4,1)S(1)}, u32[]{:S(2)}) copy-start(pred[64]{0:T(512)(128)(4,1)S(1)} %get-tuple-element.84) | copy-start | bytes 196
  60.0 5.0 %collective-permute-start.2 = (f32[18,1,128]{2,1,0:T(1,128)S(1)}, f32[18,1,128]{2,1,0:T(1,128)S(1)}, u32[]{:S(2)}, u32[]{:S(2)}) collective-permute-start(f32[18,1,128]{2,1,0:T(1,128)S(1)} %get-tuple-element.11), channel_id=1, source_target_pairs={{16,0},{32,16},{48,32},{64,48},{80,64},{96,80},{112,96},{17,1},{33... | collective-permute-start | bytes 27656 | tf_op jit(solution)/shard_map/ppermute | solution.py:17
  62.5 5.0 %collective-permute-start.3 = (f32[18,1,128]{2,1,0:T(1,128)S(1)}, f32[18,1,128]{2,1,0:T(1,128)S(1)}, u32[]{:S(2)}, u32[]{:S(2)}) collective-permute-start(f32[18,1,128]{2,1,0:T(1,128)S(1)} %get-tuple-element.12), channel_id=1, source_target_pairs={{0,16},{16,32},{32,48},{48,64},{64,80},{80,96},{96,112},{1,17},{17... | collective-permute-start | bytes 27656 | tf_op jit(solution)/shard_map/ppermute | solution.py:16
  69.2 8.2 %collective-permute-start.4 = (f32[1,64,128]{2,1,0:T(8,128)S(1)}, f32[1,64,128]{2,1,0:T(8,128)S(1)}, u32[]{:S(2)}, u32[]{:S(2)}) collective-permute-start(f32[1,64,128]{2,1,0:T(8,128)S(1)} %get-tuple-element.24), channel_id=1, source_target_pairs={{1,0},{2,1},{3,2},{4,3},{5,4},{6,5},{7,6},{8,7},{9,8},{10,9},{11,1... | collective-permute-start | bytes 98312 | tf_op jit(solution)/shard_map/ppermute | solution.py:17
  75.3 7.9 %collective-permute-start.5 = (f32[1,64,128]{2,1,0:T(8,128)S(1)}, f32[1,64,128]{2,1,0:T(8,128)S(1)}, u32[]{:S(2)}, u32[]{:S(2)}) collective-permute-start(f32[1,64,128]{2,1,0:T(8,128)S(1)} %get-tuple-element.23), channel_id=1, source_target_pairs={{0,1},{1,2},{2,3},{3,4},{4,5},{5,6},{6,7},{7,8},{8,9},{9,10},{10,1... | collective-permute-start | bytes 98312 | tf_op jit(solution)/shard_map/ppermute | solution.py:16
  83.2 4.6 %collective-permute-start.6 = (f32[18,1,128]{2,1,0:T(1,128)S(1)}, f32[18,1,128]{2,1,0:T(1,128)S(1)}, u32[]{:S(2)}, u32[]{:S(2)}) collective-permute-start(f32[18,1,128]{2,1,0:T(1,128)S(1)} %get-tuple-element.9), channel_id=1, source_target_pairs={{16,0},{32,16},{48,32},{64,48},{80,64},{96,80},{112,96},{17,1},{33... | collective-permute-start | bytes 27656 | tf_op jit(solution)/shard_map/ppermute | solution.py:17
  85.1 5.0 %collective-permute-start.7 = (f32[18,1,128]{2,1,0:T(1,128)S(1)}, f32[18,1,128]{2,1,0:T(1,128)S(1)}, u32[]{:S(2)}, u32[]{:S(2)}) collective-permute-start(f32[18,1,128]{2,1,0:T(1,128)S(1)} %get-tuple-element.10), channel_id=1, source_target_pairs={{0,16},{16,32},{32,48},{48,64},{64,80},{80,96},{96,112},{1,17},{17... | collective-permute-start | bytes 27656 | tf_op jit(solution)/shard_map/ppermute | solution.py:16
  137.7 1.4 collective-permute-start.8
  139.1 24.5 %copy-start.4 = (f32[8,32,64]{2,1,0:T(8,128)}, f32[8,32,64]{2,1,0:T(8,128)S(1)}, u32[]{:S(2)}) copy-start(f32[8,32,64]{2,1,0:T(8,128)S(1)} %get-tuple-element.49) | copy-start | bytes 196612
  139.1 24.5 %copy-start.6 = (f32[8,32,64]{2,1,0:T(8,128)}, f32[8,32,64]{2,1,0:T(8,128)S(1)}, u32[]{:S(2)}) copy-start(f32[8,32,64]{2,1,0:T(8,128)S(1)} %get-tuple-element.50) | copy-start | bytes 196612
  153.7 27.4 %collective-permute-start.13 = (f32[4,32,32]{2,1,0:T(8,128)S(1)}, f32[4,32,32]{2,1,0:T(8,128)}, u32[]{:S(2)}, u32[]{:S(2)}) collective-permute-start(f32[4,32,32]{2,1,0:T(8,128)S(1)} %broadcast_multiply_fusion.2), channel_id=1, source_target_pairs={{0,32},{32,0},{16,48},{48,16},{64,96},{96,64},{80,112},{112,80},{1... | collective-permute-start | bytes 49160 | tf_op jit(solution)/shard_map/ppermute | solution.py:29
  153.8 5.9 %collective-permute-start.10 = (f32[1,64,64]{2,1,0:T(8,128)S(1)}, f32[1,64,64]{2,1,0:T(8,128)S(1)}, u32[]{:S(2)}, u32[]{:S(2)}) collective-permute-start(f32[1,64,64]{2,1,0:T(8,128)S(1)} %get-tuple-element.45), channel_id=1, source_target_pairs={{1,0},{2,1},{3,2},{4,3},{5,4},{6,5},{7,6},{8,7},{9,8},{10,9},{11,1... | collective-permute-start | bytes 49160 | tf_op jit(solution)/shard_map/ppermute | solution.py:17
  155.7 7.9 %collective-permute-start.11 = (f32[1,64,64]{2,1,0:T(8,128)S(1)}, f32[1,64,64]{2,1,0:T(8,128)S(1)}, u32[]{:S(2)}, u32[]{:S(2)}) collective-permute-start(f32[1,64,64]{2,1,0:T(8,128)S(1)} %get-tuple-element.46), channel_id=1, source_target_pairs={{0,1},{1,2},{2,3},{3,4},{4,5},{5,6},{6,7},{7,8},{8,9},{9,10},{10,1... | collective-permute-start | bytes 49160 | tf_op jit(solution)/shard_map/ppermute | solution.py:16
  159.7 19.1 %copy-start.8 = (f32[8,1,64,64]{3,2,0,1:T(8,128)}, f32[8,1,64,64]{3,2,0,1:T(8,128)S(1)}, u32[]{:S(2)}) copy-start(f32[8,1,64,64]{3,2,0,1:T(8,128)S(1)} %fusion.39) | copy-start | bytes 393220
  178.8 4.5 %collective-permute-start.12 = (f32[4,32,32]{2,1,0:T(8,128)S(1)}, f32[4,32,32]{2,1,0:T(8,128)S(1)}, u32[]{:S(2)}, u32[]{:S(2)}) collective-permute-start(f32[4,32,32]{2,1,0:T(8,128)S(1)} %broadcast_multiply_fusion.3), channel_id=1, source_target_pairs={{0,32},{32,0},{16,48},{48,16},{64,96},{96,64},{80,112},{112,80},{1... | collective-permute-start | bytes 49160 | tf_op jit(solution)/shard_map/ppermute | solution.py:29
  181.9 3.6 %copy-start.13 = (f32[4,32,32]{2,1,0:T(8,128)}, f32[4,32,32]{2,1,0:T(8,128)S(1)}, u32[]{:S(2)}) copy-start(f32[4,32,32]{2,1,0:T(8,128)S(1)} %get-tuple-element.67) | copy-start | bytes 49156
  181.9 3.6 %copy-start.14 = (f32[4,32,32]{2,1,0:T(8,128)}, f32[4,32,32]{2,1,0:T(8,128)S(1)}, u32[]{:S(2)}) copy-start(f32[4,32,32]{2,1,0:T(8,128)S(1)} %get-tuple-element.68) | copy-start | bytes 49156
  183.3 2.2 copy-start.10
  183.3 2.2 copy-start.11
  190.1 20.8 %collective-permute-start.17 = (f32[2,32,16]{1,2,0:T(8,128)}, f32[2,32,16]{1,2,0:T(8,128)}, u32[]{:S(2)}, u32[]{:S(2)}) collective-permute-start(f32[2,32,16]{1,2,0:T(8,128)} %broadcast_multiply_fusion.4), channel_id=1, source_target_pairs={{0,64},{64,0},{16,80},{80,16},{32,96},{96,32},{48,112},{112,48},{1... | collective-permute-start | bytes 12296 | tf_op jit(solution)/shard_map/ppermute | solution.py:29
  193.1 6.8 %collective-permute-start.14 = (f32[1,64,32]{2,1,0:T(8,128)}, f32[1,64,32]{2,1,0:T(8,128)S(1)}, u32[]{:S(2)}, u32[]{:S(2)}) collective-permute-start(f32[1,64,32]{2,1,0:T(8,128)} %get-tuple-element.65), channel_id=1, source_target_pairs={{1,0},{2,1},{3,2},{4,3},{5,4},{6,5},{7,6},{8,7},{9,8},{10,9},{11,1... | collective-permute-start | bytes 24584 | tf_op jit(solution)/shard_map/ppermute | solution.py:17
  195.0 8.1 %collective-permute-start.15 = (f32[1,64,32]{2,1,0:T(8,128)}, f32[1,64,32]{2,1,0:T(8,128)S(1)}, u32[]{:S(2)}, u32[]{:S(2)}) collective-permute-start(f32[1,64,32]{2,1,0:T(8,128)} %get-tuple-element.66), channel_id=1, source_target_pairs={{0,1},{1,2},{2,3},{3,4},{4,5},{5,6},{6,7},{7,8},{8,9},{9,10},{10,1... | collective-permute-start | bytes 24584 | tf_op jit(solution)/shard_map/ppermute | solution.py:16
  199.9 5.1 %copy-start.12 = (f32[4,1,64,32]{3,2,0,1:T(8,128)}, f32[4,1,64,32]{3,2,0,1:T(8,128)S(1)}, u32[]{:S(2)}) copy-start(f32[4,1,64,32]{3,2,0,1:T(8,128)S(1)} %fusion.60) | copy-start | bytes 98308
  210.3 5.2 %collective-permute-start.16 = (f32[2,32,16]{1,2,0:T(8,128)S(1)}, f32[2,32,16]{1,2,0:T(8,128)S(1)}, u32[]{:S(2)}, u32[]{:S(2)}) collective-permute-start(f32[2,32,16]{1,2,0:T(8,128)S(1)} %broadcast_multiply_fusion.5), channel_id=1, source_target_pairs={{0,64},{64,0},{16,80},{80,16},{32,96},{96,32},{48,112},{112,48},{1... | collective-permute-start | bytes 12296 | tf_op jit(solution)/shard_map/ppermute | solution.py:29
  211.6 34.8 %copy-start.23 = (pred[32]{0:T(512)(128)(4,1)S(1)}, pred[32]{0:T(512)(128)(4,1)}, u32[]{:S(2)}) copy-start(pred[32]{0:T(512)(128)(4,1)} %get-tuple-element.85) | copy-start | bytes 100
  211.6 34.8 %copy-start.24 = (pred[32]{0:T(512)(128)(4,1)S(1)}, pred[32]{0:T(512)(128)(4,1)}, u32[]{:S(2)}) copy-start(pred[32]{0:T(512)(128)(4,1)} %get-tuple-element.86) | copy-start | bytes 100
  216.4 6.0 %collective-permute-start.18 = (f32[1,64,16]{1,2,0:T(8,128)S(1)}, f32[1,64,16]{1,2,0:T(8,128)S(1)}, u32[]{:S(2)}, u32[]{:S(2)}) collective-permute-start(f32[1,64,16]{1,2,0:T(8,128)S(1)} %get-tuple-element.79), channel_id=1, source_target_pairs={{1,0},{2,1},{3,2},{4,3},{5,4},{6,5},{7,6},{8,7},{9,8},{10,9},{11,1... | collective-permute-start | bytes 12296 | tf_op jit(solution)/shard_map/ppermute | solution.py:17
  218.3 7.7 %collective-permute-start.19 = (f32[1,64,16]{1,2,0:T(8,128)S(1)}, f32[1,64,16]{1,2,0:T(8,128)S(1)}, u32[]{:S(2)}, u32[]{:S(2)}) collective-permute-start(f32[1,64,16]{1,2,0:T(8,128)S(1)} %get-tuple-element.80), channel_id=1, source_target_pairs={{0,1},{1,2},{2,3},{3,4},{4,5},{5,6},{6,7},{7,8},{8,9},{9,10},{10,1... | collective-permute-start | bytes 12296 | tf_op jit(solution)/shard_map/ppermute | solution.py:16
  231.9 1.5 copy-start.3
  236.3 8.0 %collective-permute-start.20 = (f32[1,64,32]{2,1,0:T(8,128)}, f32[1,64,32]{2,1,0:T(8,128)S(1)}, u32[]{:S(2)}, u32[]{:S(2)}) collective-permute-start(f32[1,64,32]{2,1,0:T(8,128)} %get-tuple-element.57), channel_id=1, source_target_pairs={{1,0},{2,1},{3,2},{4,3},{5,4},{6,5},{7,6},{8,7},{9,8},{10,9},{11,1... | collective-permute-start | bytes 24584 | tf_op jit(solution)/shard_map/ppermute | solution.py:17
  238.2 8.1 %collective-permute-start.21 = (f32[1,64,32]{2,1,0:T(8,128)}, f32[1,64,32]{2,1,0:T(8,128)S(1)}, u32[]{:S(2)}, u32[]{:S(2)}) collective-permute-start(f32[1,64,32]{2,1,0:T(8,128)} %get-tuple-element.58), channel_id=1, source_target_pairs={{0,1},{1,2},{2,3},{3,4},{4,5},{5,6},{6,7},{7,8},{8,9},{9,10},{10,1... | collective-permute-start | bytes 24584 | tf_op jit(solution)/shard_map/ppermute | solution.py:16
  252.5 22.6 %copy-start.9 = (f32[8,1,64,64]{3,2,0,1:T(8,128)S(1)}, f32[8,1,64,64]{3,2,0,1:T(8,128)}, u32[]{:S(2)}) copy-start(f32[8,1,64,64]{3,2,0,1:T(8,128)} %copy-done.8) | copy-start | bytes 393220
  260.7 18.5 %copy-start.20 = (pred[64]{0:T(512)(128)(4,1)S(1)}, pred[64]{0:T(512)(128)(4,1)}, u32[]{:S(2)}) copy-start(pred[64]{0:T(512)(128)(4,1)} %copy-done.19) | copy-start | bytes 196
  260.7 18.4 %copy-start.22 = (pred[64]{0:T(512)(128)(4,1)S(1)}, pred[64]{0:T(512)(128)(4,1)}, u32[]{:S(2)}) copy-start(pred[64]{0:T(512)(128)(4,1)} %copy-done.21) | copy-start | bytes 196
  260.8 18.7 %copy-start.5 = (f32[8,32,64]{2,1,0:T(8,128)S(1)}, f32[8,32,64]{2,1,0:T(8,128)}, u32[]{:S(2)}) copy-start(f32[8,32,64]{2,1,0:T(8,128)} %copy-done.4) | copy-start | bytes 196612
  260.8 18.7 %copy-start.7 = (f32[8,32,64]{2,1,0:T(8,128)S(1)}, f32[8,32,64]{2,1,0:T(8,128)}, u32[]{:S(2)}) copy-start(f32[8,32,64]{2,1,0:T(8,128)} %copy-done.6) | copy-start | bytes 196612
  269.3 6.0 %collective-permute-start.22 = (f32[1,64,64]{2,1,0:T(8,128)S(1)}, f32[1,64,64]{2,1,0:T(8,128)S(1)}, u32[]{:S(2)}, u32[]{:S(2)}) collective-permute-start(f32[1,64,64]{2,1,0:T(8,128)S(1)} %get-tuple-element.37), channel_id=1, source_target_pairs={{1,0},{2,1},{3,2},{4,3},{5,4},{6,5},{7,6},{8,7},{9,8},{10,9},{11,1... | collective-permute-start | bytes 49160 | tf_op jit(solution)/shard_map/ppermute | solution.py:17
  271.3 7.9 %collective-permute-start.23 = (f32[1,64,64]{2,1,0:T(8,128)S(1)}, f32[1,64,64]{2,1,0:T(8,128)S(1)}, u32[]{:S(2)}, u32[]{:S(2)}) collective-permute-start(f32[1,64,64]{2,1,0:T(8,128)S(1)} %get-tuple-element.38), channel_id=1, source_target_pairs={{0,1},{1,2},{2,3},{3,4},{4,5},{5,6},{6,7},{7,8},{8,9},{9,10},{10,1... | collective-permute-start | bytes 49160 | tf_op jit(solution)/shard_map/ppermute | solution.py:16
  291.8 41.5 %copy-start.2 = (f32[16,64,128]{2,1,0:T(8,128)S(1)}, f32[16,64,128]{2,1,0:T(8,128)}, u32[]{:S(2)}) copy-start(f32[16,64,128]{2,1,0:T(8,128)} %param.2) | copy-start | bytes 1572868
  291.8 41.5 %copy-start.16 = (pred[128]{0:T(512)(128)(4,1)S(1)}, pred[128]{0:T(512)(128)(4,1)}, u32[]{:S(2)}) copy-start(pred[128]{0:T(512)(128)(4,1)} %copy-done.15) | copy-start | bytes 388
  291.9 41.5 %copy-start.18 = (pred[128]{0:T(512)(128)(4,1)S(1)}, pred[128]{0:T(512)(128)(4,1)}, u32[]{:S(2)}) copy-start(pred[128]{0:T(512)(128)(4,1)} %copy-done.17) | copy-start | bytes 388
  316.0 6.1 %collective-permute-start.24 = (f32[1,64,128]{2,1,0:T(8,128)S(1)}, f32[1,64,128]{2,1,0:T(8,128)S(1)}, u32[]{:S(2)}, u32[]{:S(2)}) collective-permute-start(f32[1,64,128]{2,1,0:T(8,128)S(1)} %get-tuple-element.18), channel_id=1, source_target_pairs={{1,0},{2,1},{3,2},{4,3},{5,4},{6,5},{7,6},{8,7},{9,8},{10,9},{11,1... | collective-permute-start | bytes 98312 | tf_op jit(solution)/shard_map/ppermute | solution.py:17
  317.9 7.9 %collective-permute-start.25 = (f32[1,64,128]{2,1,0:T(8,128)S(1)}, f32[1,64,128]{2,1,0:T(8,128)S(1)}, u32[]{:S(2)}, u32[]{:S(2)}) collective-permute-start(f32[1,64,128]{2,1,0:T(8,128)S(1)} %get-tuple-element.17), channel_id=1, source_target_pairs={{0,1},{1,2},{2,3},{3,4},{4,5},{5,6},{6,7},{7,8},{8,9},{9,10},{10,1... | collective-permute-start | bytes 98312 | tf_op jit(solution)/shard_map/ppermute | solution.py:16
  325.9 4.6 %collective-permute-start.26 = (f32[18,1,128]{2,1,0:T(1,128)S(1)}, f32[18,1,128]{2,1,0:T(1,128)S(1)}, u32[]{:S(2)}, u32[]{:S(2)}) collective-permute-start(f32[18,1,128]{2,1,0:T(1,128)S(1)} %get-tuple-element.7), channel_id=1, source_target_pairs={{16,0},{32,16},{48,32},{64,48},{80,64},{96,80},{112,96},{17,1},{33... | collective-permute-start | bytes 27656 | tf_op jit(solution)/shard_map/ppermute | solution.py:17
  327.8 5.5 %collective-permute-start.27 = (f32[18,1,128]{2,1,0:T(1,128)S(1)}, f32[18,1,128]{2,1,0:T(1,128)S(1)}, u32[]{:S(2)}, u32[]{:S(2)}) collective-permute-start(f32[18,1,128]{2,1,0:T(1,128)S(1)} %get-tuple-element.8), channel_id=1, source_target_pairs={{0,16},{16,32},{32,48},{48,64},{64,80},{80,96},{96,112},{1,17},{17... | collective-permute-start | bytes 27656 | tf_op jit(solution)/shard_map/ppermute | solution.py:16
where the time goes:
time: 337 us; the launch traced here: 335 us
  local copies, waits for them, and re-layouts  168 us (50%)
  starting transfers between devices  70.3 us (21%)
  other arithmetic  54.7 us (16%)
  waiting for transfers between devices  40.6 us (12%)
    reshape x6, local copies, waits for them, and re-layouts, restrict(): field.reshape(nx // 2, 2, ny // 2, 2, nz // 2, 2).sum(axis=(1, 3, 5)) * 0.5  96.6 us
    reshape x7, local copies, waits for them, and re-layouts, prolong(): return spread.reshape(2 * nx, 2 * ny, 2 * nz)  47.5 us
    ppermute x11, starting transfers between devices, padded_2(): before = lax.ppermute(last, axis, up)  34.3 us
    ppermute x11, waiting for transfers between devices, padded_2(): before = lax.ppermute(last, axis, up)  33.9 us
    reduce_sum x6, other arithmetic, restrict(): field.reshape(nx // 2, 2, ny // 2, 2, nz // 2, 2).sum(axis=(1, 3, 5)) * 0.5  33.7 us
    ppermute x11, starting transfers between devices, padded_2(): after = lax.ppermute(first, axis, down)  30.1 us
    broadcast_in_dim x3, local copies, waits for them, and re-layouts, prolong(): jnp.broadcast_to(field[:, None, :, None, :, None], (nx, 2, ny, 2, nz, 2))  15.7 us
  transfers between devices with their start and end apart: 28, of which 13 were waited for; matrix products, arithmetic and copies ran while one was open for 38% of the time, Pallas kernels for 0%

commit v1 on v0

v1 whole, which is shorter than its diff:
```python
import jax
import jax.numpy as jnp
from jax import lax
from jax.experimental import pallas as pl
from jax.experimental.pallas import tpu as pltpu
from jax.sharding import PartitionSpec as P

OMEGA = 0.8
F32 = jnp.float32
WINDOW = 64
VM = pl.BlockSpec(memory_space=pltpu.VMEM)
SM = pl.BlockSpec(memory_space=pltpu.SMEM)


def shape(*dims):
    return jax.ShapeDtypeStruct(dims, F32)


def call(body, outs, scratch, *args):
    return pl.pallas_call(
        body,
        out_shape=outs,
        in_specs=[SM] + [VM] * (len(args) - 1),
        out_specs=tuple(VM for _ in outs),
        scratch_shapes=[pltpu.VMEM(s, F32) for s in scratch],
        compiler_params=pltpu.CompilerParams(vmem_limit_bytes=56 << 20),
    )(*args)


def iota(rows, axis):
    return lax.broadcasted_iota(jnp.int32, (rows, 128), axis)


def pair_matrix(down):
    i, j = iota(128, 0), iota(128, 1)
    return jnp.where((i >> 1) == j if down else i == (j >> 1), 1.0, 0.0).astype(F32)


def dot(a, m):
    return jnp.dot(a, m, preferred_element_type=F32, precision=lax.Precision.HIGHEST)


def turn(v, by, axis):
    return pltpu.roll(v, by % v.shape[axis], axis)


def z_sum(v):
    lane = iota(v.shape[0], 1)
    below = jnp.where(lane == 0, 0.0, turn(v, 1, 1))
    return below + jnp.where(lane == 127, 0.0, turn(v, -1, 1))


def plane_sum(v):
    return turn(v, 1, 0) + turn(v, -1, 0) + z_sum(v)


def windowed_sum(v, row):
    at = row & (WINDOW - 1)
    below = jnp.where(at == 0, 0.0, turn(v, 1, 0))
    above = jnp.where(at == WINDOW - 1, 0.0, turn(v, -1, 0))
    return below + above + turn(v, 1, 1) + turn(v, -1, 1)


def inside(at, size):
    return (at >= 0) & (at < size)


def row_pairs(ref, k, rows):
    return ref[k, pl.ds(0, rows, stride=2), :] + ref[k, pl.ds(1, rows, stride=2), :]


def spread_rows(ref, k, v):
    rows = v.shape[0]
    ref[k, pl.ds(0, rows, stride=2), :] = v
    ref[k, pl.ds(1, rows, stride=2), :] = v


def down_kernel(
    blocks, aggs,
    at, b, c, xe, xo, ye, yo,
    p0, vown, wown, e1, w1, bc2, se, so,
    v, w, q, bx, cx, rs, b1, c1, r1,
):
    bi, ai = at[0], at[1]
    x_even, y_even = (bi & 1) == 0, (ai & 1) == 0
    y_lo = jnp.where(ai > 0, 1.0, 0.0)
    y_hi = jnp.where(ai < aggs - 1, 1.0, 0.0)

    def put(p, rows, bb, cc, scale):
        ww = scale / (6.0 + cc)
        vv = ww * bb
        w[p, rows], v[p, rows], bx[p, rows], cx[p, rows] = ww, vv, bb, cc
        return vv, ww

    def plane(p, bb, cc, scale):
        out = put(p, pl.ds(8, 64), bb, cc, scale)
        lo = [jnp.where(y_even, yo[k, p], ye[k, p]) for k in (0, 1)]
        hi = [jnp.where(y_even, ye[k, p], yo[k, p]) for k in (0, 1)]
        put(p, pl.ds(4, 4), *lo, scale * y_lo)
        put(p, pl.ds(72, 4), *hi, scale * y_hi)
        return out

    def own(i, carry):
        vown[i], wown[i] = plane(i + 4, b[i], c[i], OMEGA)
        return carry

    def edge(i, carry):
        lo = [jnp.where(x_even, xo[k, i], xe[k, i]) for k in (0, 1)]
        hi = [jnp.where(x_even, xe[k, i], xo[k, i]) for k in (0, 1)]
        plane(i, *lo, jnp.where(bi > 0, OMEGA, 0.0))
        plane(i + 20, *hi, jnp.where(bi < blocks - 1, OMEGA, 0.0))
        return carry

    lax.fori_loop(0, 16, own, 0)
    lax.fori_loop(0, 4, edge, 0)

    def smooth(p, carry):
        vv = v[p]
        qq = 0.4 * vv + w[p] * (v[p - 1] + v[p + 1] + plane_sum(vv))
        q[p] = qq
        return carry

    lax.fori_loop(1, 23, smooth, 0)

    def first(k, carry):
        p0[k] = q[k + 3] + OMEGA * v[k + 3]
        return carry

    lax.fori_loop(0, 18, first, 0)

    half = 0.5 * pair_matrix(True)

    def resid(p):
        return 0.04 * bx[p] + (q[p - 1] + q[p + 1] + plane_sum(q[p]))

    row1 = ai * 32 - 4 + iota(40, 0)
    keep1 = inside(row1, 32 * aggs) & (iota(40, 1) < 64)

    def coarse(k, carry):
        p = 2 + 2 * k
        rs[0] = resid(p) + resid(p + 1)
        rs[1] = cx[p] + cx[p + 1]
        both = jnp.concatenate([row_pairs(rs, 0, 40), row_pairs(rs, 1, 40)], axis=0)
        both = dot(both, half)
        bb, cc = both[:40], both[40:]
        ok = keep1 & inside(bi * 8 + k - 1, 8 * blocks)
        ww = jnp.where(ok, OMEGA / (6.0 + cc), 0.0)
        b1[k], c1[k] = bb, cc
        w1[k + 1] = ww
        e1[k + 1] = jnp.where(ok, ww * bb, 0.0)
        return carry

    lax.fori_loop(0, 10, coarse, 0)

    def resid1(k):
        near = e1[k] + e1[k + 2] + windowed_sum(e1[k + 1], row1)
        return 0.2 * b1[k] + near

    lane16 = iota(16, 1)

    def coarse2(k, carry):
        p = 1 + 2 * k
        r1[0] = resid1(p) + resid1(p + 1)
        r1[1] = c1[p] + c1[p + 1]
        pairs = [r1[i, pl.ds(4, 16, stride=2), :] + r1[i, pl.ds(5, 16, stride=2), :] for i in (0, 1)]
        both = dot(jnp.concatenate(pairs, axis=0), half)
        bb = jnp.where(lane16 < 32, both[:16], 0.0)
        cc = jnp.where(lane16 < 32, both[16:], 0.0)
        mix = bb + turn(cc, 32, 1)
        bc2[k] = mix
        for ref, lo_side in ((se, jnp.logical_not(y_even)), (so, y_even)):
            ref[k, 0:5] = jnp.where(lo_side, mix[0:5], mix[11:16])
            for j in (0, 1):
                n = 2 + 2 * k + j
                ref[k, 5 + j : 6 + j] = jnp.where(lo_side, e1[n, 5:6], e1[n, 34:35])
            ref[k, 7:8] = jnp.zeros((1, 128), F32)
        return carry

    lax.fori_loop(0, 4, coarse2, 0)


def join_kernel(at, bc2, ye, yo, e1, wide, se, so, sf, sg):
    bi, ai = at[0], at[1]
    x_even, y_even = (bi & 1) == 0, (ai & 1) == 0
    low_pair = (bi & 2) == 0
    for k in range(4):
        wide[k] = jnp.zeros((32, 128), F32)
        wide[k, 3:8] = jnp.where(y_even, yo[k, 0:5], ye[k, 0:5])
        wide[k, 8:24] = bc2[k]
        wide[k, 24:29] = jnp.where(y_even, ye[k, 0:5], yo[k, 0:5])
        se[k] = wide[k]
        so[k] = wide[k]
    up, down = e1[8, 4:36], e1[3, 4:36]
    se[4] = jnp.where(x_even, up, down)
    so[4] = jnp.where(x_even, down, up)
    sf[0] = jnp.where(low_pair, wide[3], wide[0])
    sg[0] = jnp.where(low_pair, wide[0], wide[3])


def up_kernel(
    blocks, aggs,
    at, p0, vown, wown, e1in, w1, wide, ye, yo, xe, xo, xf, xg,
    out,
    bc, e2, w2, b2, c2, rs, b3, e3, w3, pe2, m2, t2, e1, pe1, m1, mf,
):
    bi, ai = at[0], at[1]
    x_even, y_even = (bi & 1) == 0, (ai & 1) == 0
    low_pair = (bi & 2) == 0
    half, twice = 0.5 * pair_matrix(True), pair_matrix(False)

    bc[0] = jnp.where(low_pair, xg[0], xf[0])
    bc[13] = jnp.where(low_pair, xf[0], xg[0])
    for k in range(4):
        bc[1 + k] = jnp.where(x_even, xo[k], xe[k])
        bc[5 + k] = wide[k]
        bc[9 + k] = jnp.where(x_even, xe[k], xo[k])

    row2 = ai * 16 - 8 + iota(32, 0)
    lane2 = iota(32, 1) < 32
    keep2 = inside(row2, 16 * aggs) & lane2
    for k in range(14):
        mix = bc[k]
        bb = jnp.where(lane2, mix, 0.0)
        cc = jnp.where(lane2, turn(mix, -32, 1), 0.0)
        ww = jnp.where(keep2 & inside(bi * 4 + k - 5, 4 * blocks), OMEGA / (6.0 + cc), 0.0)
        b2[k], c2[k], w2[k], e2[k] = bb, cc, ww, ww * bb

    def resid2(k):
        return 0.2 * b2[k] + (e2[k - 1] + e2[k + 1] + windowed_sum(e2[k], row2))

    for j in range(6):
        k = 1 + 2 * j
        rs[j] = resid2(k) + resid2(k + 1)
        rs[6 + j] = c2[k] + c2[k + 1]
    both = dot(jnp.concatenate([row_pairs(rs, j, 16) for j in range(12)], axis=0), half)
    row3 = ai * 8 - 4 + iota(16, 0)
    keep3 = inside(row3, 8 * aggs) & (iota(16, 1) < 16)
    for j in range(6):
        bb, cc = both[16 * j : 16 * j + 16], both[96 + 16 * j : 112 + 16 * j]
        ww = jnp.where(keep3 & inside(bi * 2 + j - 2, 2 * blocks), OMEGA / (6.0 + cc), 0.0)
        w3[j], e3[j] = ww, ww * bb
    solved = []
    for j in range(1, 5):
        near = e3[j - 1] + e3[j + 1] + windowed_sum(e3[j], row3)
        solved.append(1.2 * e3[j] + w3[j] * near)
    wider = dot(jnp.concatenate(solved, axis=0), twice)
    for j in range(4):
        spread_rows(pe2, j, wider[16 * j : 16 * j + 16])
    for k in range(3, 11):
        m2[k] = e2[k] + pe2[(k - 3) // 2]
    solved = []
    for k in range(4, 10):
        near = m2[k - 1] + m2[k + 1] + windowed_sum(m2[k], row2)
        solved.append(0.2 * m2[k] + e2[k] + w2[k] * near)
    wider = dot(jnp.concatenate(solved, axis=0), twice)
    for k in range(6):
        t2[k] = wider[32 * k : 32 * k + 32]
        spread_rows(pe1, k, t2[k, 6:26])

    for k in range(1, 11):
        e1[k] = e1in[k]
    for k in (0, 11):
        e1[k] = jnp.zeros((40, 128), F32)
    e1[0, 4:36] = jnp.where(x_even, xo[4], xe[4])
    e1[11, 4:36] = jnp.where(x_even, xe[4], xo[4])
    for n in range(8):
        k, j = n // 2, n % 2
        mine, other = ye[k, 5 + j : 6 + j], yo[k, 5 + j : 6 + j]
        e1[n + 2, 2:3] = jnp.where(y_even, other, mine)
        e1[n + 2, 37:38] = jnp.where(y_even, mine, other)
    for k in range(12):
        m1[k] = e1[k] + pe1[k // 2]
    row1 = ai * 32 - 4 + iota(40, 0)

    def fine(k, carry):
        near = m1[k] + m1[k + 2] + windowed_sum(m1[k + 1], row1)
        v = 0.2 * m1[k + 1] + e1[k + 1] + w1[k + 1] * near
        spread_rows(rs80, k, dot(v, twice))
        return carry

    rs80 = mf.at[pl.ds(18, 10)]
    lax.fori_loop(0, 10, fine, 0)

    def merge(k, carry):
        mf[k] = p0[k] + mf[18 + (k + 1) // 2]
        return carry

    lax.fori_loop(0, 18, merge, 0)

    def last(k, carry):
        m = mf[k + 1]
        near = (plane_sum(m) + mf[k] + mf[k + 2])[8:72]
        out[k] = 0.2 * m[8:72] + vown[k] + wown[k] * near
        return carry

    lax.fori_loop(0, 16, last, 0)


def swaps(size, apart):
    inner = [(i, i ^ apart) for i in range(size)]
    outer = []
    for i in range(apart, size - apart):
        if i & apart:
            outer += [(i, i + apart), (i + apart, i)]
    return inner, outer


def shards(b, c):
    blocks, aggs = lax.axis_size("blk"), lax.axis_size("agg")
    bi, ai = lax.axis_index("blk"), lax.axis_index("agg")
    at = jnp.stack([bi, ai]).astype(jnp.int32)
    x_even, y_even = (bi & 1) == 0, (ai & 1) == 0
    near_in, near_out = swaps(blocks, 1)
    far_in, far_out = swaps(blocks, 2)
    side_in, side_out = swaps(aggs, 1)

    first = jnp.stack([b[:4], c[:4]])
    last = jnp.stack([b[12:], c[12:]])
    xe = lax.ppermute(jnp.where(x_even, last, first), "blk", near_in)
    xo = lax.ppermute(jnp.where(x_even, first, last), "blk", near_out)
    lo, hi = jnp.where(x_even, xo, xe), jnp.where(x_even, xe, xo)

    def rows(cut):
        own = jnp.stack([b[:, cut], c[:, cut]])
        return jnp.concatenate([lo[:, :, cut], own, hi[:, :, cut]], axis=1)

    first, last = rows(slice(0, 4)), rows(slice(60, 64))
    ye = lax.ppermute(jnp.where(y_even, last, first), "agg", side_in)
    yo = lax.ppermute(jnp.where(y_even, first, last), "agg", side_out)

    big, mid = (24, 80, 128), (12, 40, 128)
    p0, vown, wown, e1, w1, bc2, se, so = call(
        lambda *refs: down_kernel(blocks, aggs, *refs),
        (shape(18, 80, 128), shape(16, 64, 128), shape(16, 64, 128), shape(*mid), shape(*mid),
         shape(4, 16, 128), shape(4, 8, 128), shape(4, 8, 128)),
        [big] * 5 + [(2, 80, 128), mid, mid, (2, 40, 128)],
        at, b, c, xe, xo, ye, yo,
    )
    ye = lax.ppermute(se, "agg", side_in)
    yo = lax.ppermute(so, "agg", side_out)
    wide, se, so, sf, sg = call(
        join_kernel,
        (shape(4, 32, 128), shape(5, 32, 128), shape(5, 32, 128), shape(1, 32, 128), shape(1, 32, 128)),
        [],
        at, bc2, ye, yo, e1,
    )
    xe = lax.ppermute(se, "blk", near_in)
    xo = lax.ppermute(so, "blk", near_out)
    xf = lax.ppermute(sf, "blk", far_in)
    xg = lax.ppermute(sg, "blk", far_out)
    small = (14, 32, 128)
    (out,) = call(
        lambda *refs: up_kernel(blocks, aggs, *refs),
        (shape(16, 64, 128),),
        [small] * 5 + [(12, 32, 128), (6, 16, 128), (6, 16, 128), (6, 16, 128), (4, 32, 128),
                       small, (6, 32, 128), mid, (6, 40, 128), mid, (28, 80, 128)],
        at, p0, vown, wown, e1, w1, wide, ye, yo, xe, xo, xf, xg,
    )
    return out


def solution(mesh):
    placed = (P("blk", "agg", None), P("blk", "agg", None))
    return jax.shard_map(
        shards, mesh=mesh, in_specs=placed, out_specs=P("blk", "agg", None), check_vma=False
    )
```

time: 337 us -> 63.7 us (0.19)
  local copies, waits for them, and re-layouts: 168 us -> 5.26 us
  other arithmetic: 54.7 us -> 0.73 us
  starting transfers between devices: 70.3 us -> 21.8 us
  waiting for transfers between devices: 40.6 us -> 16.3 us
  Pallas kernels: 0 us -> 19.2 us
    reshape x13 -> x0, local copies, waits for them, and re-layouts: 144 us -> none  [the longest x6 96.6 us: restrict(): field.reshape(nx // 2, 2, ny // 2, 2, nz // 2, 2).sum(axis=(1, 3, 5)) * 0.5]
    ppermute x28 -> x10, starting transfers between devices: 70.3 us -> 21.8 us  [the longest x1 6.21 us: shards(): xo = lax.ppermute(jnp.where(x_even, first, last), 'blk', near_out)]
    reduce_sum x6 -> x0, other arithmetic: 33.7 us -> none  [restrict(): field.reshape(nx // 2, 2, ny // 2, 2, nz // 2, 2).sum(axis=(1, 3, 5)) * 0.5]
    ppermute x28 -> x10, waiting for transfers between devices: 40.6 us -> 16.3 us  [the longest x1 5.22 us: shards(): xo = lax.ppermute(jnp.where(x_even, first, last), 'blk', near_out)]
    pallas_call x0 -> x3, Pallas kernels: none -> 19.2 us  [call(): pl.pallas_call(body, out_shape=outs, in_specs=[SM] + [VM] * (len(args) -...]
    broadcast_in_dim x3 -> x0, local copies, waits for them, and re-layouts: 15.7 us -> none  [prolong(): jnp.broadcast_to(field[:, None, :, None, :, None], (nx, 2, ny, 2, nz, 2))]
    add x15 -> x0, other arithmetic: 12.2 us -> none  [the longest x2 3.05 us: shards(): fine + OMEGA * (right_side - fine_apply(fine, coefficient)) * fine_inverse]
    slice x24 -> x2, local copies, waits for them, and re-layouts: 6.97 us -> 0.01 us  [rows(): return jnp.concatenate([lo[:, :, cut], own, hi[:, :, cut]], axis=1)]
  transfers between devices with their start and end apart: 28 -> 10, of which waited for: 13 -> 5; matrix products, arithmetic and copies ran while one was open for 38% -> 2% of each run, Pallas kernels for 0% -> 0%
where the time goes in v1:
time: 63.7 us; the launch traced here: 63.4 us
  starting transfers between devices  21.8 us (34%)
  Pallas kernels  19.2 us (30%)
  waiting for transfers between devices  16.3 us (26%)
  local copies, waits for them, and re-layouts  5.26 us (8%)
  other arithmetic  0.73 us (1%)
    pallas_call x3, Pallas kernels, call(): pl.pallas_call(body, out_shape=outs, in_specs=[SM] + [VM] * (len(args) -...  19.2 us
    ppermute x1, starting transfers between devices, shards(): xo = lax.ppermute(jnp.where(x_even, first, last), 'blk', near_out)  6.21 us
    ppermute x1, waiting for transfers between devices, shards(): xo = lax.ppermute(jnp.where(x_even, first, last), 'blk', near_out)  5.22 us
    ppermute x1, waiting for transfers between devices, shards(): xg = lax.ppermute(sg, 'blk', far_out)  4.5 us
    ppermute x1, starting transfers between devices, shards(): xo = lax.ppermute(so, 'blk', near_out)  3.99 us
    ppermute x1, starting transfers between devices, shards(): xg = lax.ppermute(sg, 'blk', far_out)  3.68 us
    ppermute x1, waiting for transfers between devices, shards(): yo = lax.ppermute(so, 'agg', side_out)  3.32 us
    unnamed x20, local copies, waits for them, and re-layouts  3.15 us
  transfers between devices with their start and end apart: 10, of which 5 were waited for; matrix products, arithmetic and copies ran while one was open for 2% of the time, Pallas kernels for 0%

profile of v1, /device:TPU:14, one launch (start us, length us, event | category | flops | bytes accessed | tf_op | source)
XLA Modules:
  0.0 63.4 jit_solution(11042870688595965060)
XLA Ops:
  0.0 1.1 %slice_bitcast_fusion.2 = (f32[1,4,64,128]{3,2,1,0:T(8,128)S(1)}, f32[1,4,64,128]{3,2,1,0:T(8,128)S(1)}, f32[1,4,64,128]{3,2,1,0:T(8,128)S(1)}, f32[1,4,64,128]{3,2,1,0:T(8,128)S(1)}) fusion(f32[16,64,128]{2,1,0:T(8,128)} %refs_2_.1, f32[16,64,128]{2,1,0:T(8,128)} %refs_1_.1), kind=kLoop, calls=%fused_computation.6 | loop fusion | bytes 1048576 | tf_op jit(solution)/shard_map/stack | solution.py:318
  1.2 6.2 %collective-permute-start.1 = (f32[2,4,64,128]{3,2,1,0:T(8,128)S(1)}, f32[2,4,64,128]{3,2,1,0:T(8,128)S(1)}, u32[]{:S(2)}, u32[]{:S(2)}) collective-permute-start(f32[2,4,64,128]{3,2,1,0:T(8,128)S(1)} %get-tuple-element.37), channel_id=1, source_target_pairs={{1,2},{2,1},{3,4},{4,3},{5,6},{6,5},{7,8},{8,7},{9,10},{10,9},{11,... | collective-permute-start | bytes 786440 | tf_op jit(solution)/shard_map/ppermute | solution.py:320
  7.4 0.1 collective-permute-start
  7.5 1.0 %slice_bitcast_fusion.6 = (f32[1,16,4,128]{3,2,1,0:T(4,128)S(1)}, f32[1,16,4,128]{3,2,1,0:T(4,128)S(1)}, f32[1,16,4,128]{3,2,1,0:T(4,128)S(1)}, f32[1,16,4,128]{3,2,1,0:T(4,128)S(1)}) fusion(f32[16,64,128]{2,1,0:T(8,128)} %refs_2_.1, f32[16,64,128]{2,1,0:T(8,128)} %refs_1_.1), kind=kLoop, calls=%fused_computation.16 | loop fusion | bytes 262144 | tf_op jit(solution)/shard_map/stack | solution.py:324
  8.5 5.2 %collective-permute-done.1.refs_4_ = f32[2,4,64,128]{3,2,1,0:T(8,128)S(1)} collective-permute-done((f32[2,4,64,128]{3,2,1,0:T(8,128)S(1)}, f32[2,4,64,128]{3,2,1,0:T(8,128)S(1)}, u32[]{:S(2)}, u32[]{:S(2)}) %collective-permute-start.1) | collective-permute-done | bytes 262176 | tf_op jit(solution)/shard_map/ppermute | solution.py:320
  13.7 0.0 copy-start
  13.7 1.6 %collective-permute-done.refs_3_ = f32[2,4,64,128]{3,2,1,0:T(8,128)S(1)} collective-permute-done((f32[2,4,64,128]{3,2,1,0:T(8,128)S(1)}, f32[2,4,64,128]{3,2,1,0:T(8,128)S(1)}, u32[]{:S(2)}, u32[]{:S(2)}) %collective-permute-start) | collective-permute-done | bytes 262176 | tf_op jit(solution)/shard_map/ppermute | solution.py:319
  15.2 0.0 copy-start.1
  15.3 0.0 copy-done
  15.3 0.6 %copy-done.1 = f32[2,4,64,128]{3,2,1,0:T(8,128)} copy-done((f32[2,4,64,128]{3,2,1,0:T(8,128)}, f32[2,4,64,128]{3,2,1,0:T(8,128)S(1)}, u32[]{:S(2)}) %copy-start.1) | copy-done | bytes 262168
  16.0 0.1 broadcast_select_fusion.2
  16.0 1.9 %collective-permute-start.3 = (f32[2,24,4,128]{3,2,1,0:T(4,128)S(1)}, f32[2,24,4,128]{3,2,1,0:T(4,128)S(1)}, u32[]{:S(2)}, u32[]{:S(2)}) collective-permute-start(f32[2,24,4,128]{3,2,1,0:T(4,128)S(1)} %get-tuple-element.47), channel_id=1, source_target_pairs={{16,32},{32,16},{48,64},{64,48},{80,96},{96,80},{17,33},{33,17},{4... | collective-permute-start | bytes 294920 | tf_op jit(solution)/shard_map/ppermute | solution.py:329
  18.0 1.8 %collective-permute-start.2 = (f32[2,24,4,128]{3,2,1,0:T(4,128)S(1)}, f32[2,24,4,128]{3,2,1,0:T(4,128)S(1)}, u32[]{:S(2)}, u32[]{:S(2)}) collective-permute-start(f32[2,24,4,128]{3,2,1,0:T(4,128)S(1)} %get-tuple-element.48), channel_id=1, source_target_pairs={{0,16},{16,0},{32,48},{48,32},{64,80},{80,64},{96,112},{112,96},{1... | collective-permute-start | bytes 294920 | tf_op jit(solution)/shard_map/ppermute | solution.py:328
  19.7 0.6 pad_add_fusion.refs_0_.at
  20.3 1.7 %collective-permute-done.3.refs_6_ = f32[2,24,4,128]{3,2,1,0:T(4,128)S(1)} collective-permute-done((f32[2,24,4,128]{3,2,1,0:T(4,128)S(1)}, f32[2,24,4,128]{3,2,1,0:T(4,128)S(1)}, u32[]{:S(2)}, u32[]{:S(2)}) %collective-permute-start.3) | collective-permute-done | bytes 98336 | tf_op jit(solution)/shard_map/ppermute | solution.py:329
  22.0 0.0 copy-start.2
  22.0 0.0 collective-permute-done.2.refs_5_
  22.0 0.6 copy-done.2
  22.6 0.0 copy-start.3
  22.6 0.6 %copy-done.3 = f32[2,24,4,128]{3,2,1,0:T(4,128)} copy-done((f32[2,24,4,128]{3,2,1,0:T(4,128)}, f32[2,24,4,128]{3,2,1,0:T(4,128)S(1)}, u32[]{:S(2)}) %copy-start.3) | copy-done | bytes 98328
  23.2 9.6 %shard_map.28 = (f32[18,80,128]{2,1,0:T(8,128)}, f32[16,64,128]{2,1,0:T(8,128)}, f32[16,64,128]{2,1,0:T(8,128)}, f32[12,40,128]{2,1,0:T(8,128)}, f32[12,40,128]{...) custom-call(s32[2]{0:T(128)} %pad_add_fusion.refs_0_.at, ...), custom_call_target="tpu_custom_call" | custom-call | tf_op jit(solution)/shard_map/pallas_call | solution.py:20
  32.8 0.1 collective-permute-start.4
  32.9 1.9 %collective-permute-start.5 = (f32[4,8,128]{2,1,0:T(8,128)}, f32[4,8,128]{2,1,0:T(8,128)S(1)}, u32[]{:S(2)}, u32[]{:S(2)}) collective-permute-start(f32[4,8,128]{2,1,0:T(8,128)} %get-tuple-element.25), channel_id=1, source_target_pairs={{16,32},{32,16},{48,64},{64,48},{80,96},{96,80},{17,33},{33,17},{4... | collective-permute-start | bytes 49160 | tf_op jit(solution)/shard_map/ppermute | solution.py:340
  34.8 0.0 collective-permute-done.4.ye.refs_7_
  34.9 0.0 copy-start.6
  34.9 3.3 %collective-permute-done.5.yo.refs_8_ = f32[4,8,128]{2,1,0:T(8,128)S(1)} collective-permute-done((f32[4,8,128]{2,1,0:T(8,128)}, f32[4,8,128]{2,1,0:T(8,128)S(1)}, u32[]{:S(2)}, u32[]{:S(2)}) %collective-permute-start.5) | collective-permute-done | bytes 16416 | tf_op jit(solution)/shard_map/ppermute | solution.py:340
  38.2 0.0 copy-start.7
  38.2 0.0 copy-done.6
  38.2 0.6 copy-done.7
  38.8 1.7 %shard_map.29 = (f32[4,32,128]{2,1,0:T(8,128)}, f32[5,32,128]{2,1,0:T(8,128)}, f32[5,32,128]{2,1,0:T(8,128)}, f32[1,32,128]{2,1,0:T(8,128)}, f32[1,32,128]{2,1,0:T(8,128)}) custom-call(s32[2]{0:T(128)} %pad_add_fusion.refs_0_.at, f32[4,16,128]{2,1,0:T(8,128)} %get-tuple-element.23.bc2, f32[4,8,128]{2,1,0:T(8,128)} %copy-done.6, f32[4,8,128]{2,1,0:T(8,128)} %copy-done.7, ...), custom_call_target="tpu_custom_call" | custom-call | tf_op jit(solution)/shard_map/pallas_call | solution.py:20
  40.5 0.3 collective-permute-start.6
  40.8 4.0 %collective-permute-start.7 = (f32[5,32,128]{2,1,0:T(8,128)}, f32[5,32,128]{2,1,0:T(8,128)S(1)}, u32[]{:S(2)}, u32[]{:S(2)}) collective-permute-start(f32[5,32,128]{2,1,0:T(8,128)} %get-tuple-element.28), channel_id=1, source_target_pairs={{1,2},{2,1},{3,4},{4,3},{5,6},{6,5},{7,8},{8,7},{9,10},{10,9},{11,... | collective-permute-start | bytes 245768 | tf_op jit(solution)/shard_map/ppermute | solution.py:348
  44.8 1.8 %collective-permute-start.8 = (f32[1,32,128]{2,1,0:T(8,128)}, f32[1,32,128]{2,1,0:T(8,128)S(1)}, u32[]{:S(2)}, u32[]{:S(2)}) collective-permute-start(f32[1,32,128]{2,1,0:T(8,128)} %get-tuple-element.29), channel_id=1, source_target_pairs={{0,2},{1,3},{2,0},{3,1},{4,6},{5,7},{6,4},{7,5},{8,10},{9,11},{10,... | collective-permute-start | bytes 49160 | tf_op jit(solution)/shard_map/ppermute | solution.py:349
  46.6 3.7 %collective-permute-start.9 = (f32[1,32,128]{2,1,0:T(8,128)}, f32[1,32,128]{2,1,0:T(8,128)S(1)}, u32[]{:S(2)}, u32[]{:S(2)}) collective-permute-start(f32[1,32,128]{2,1,0:T(8,128)} %get-tuple-element.30), channel_id=1, source_target_pairs={{2,4},{4,2},{3,5},{5,3},{6,8},{8,6},{7,9},{9,7},{10,12},{12,10},{1... | collective-permute-start | bytes 49160 | tf_op jit(solution)/shard_map/ppermute | solution.py:350
  50.3 0.0 collective-permute-done.8.refs_11_
  50.3 0.0 copy-start.8
  50.3 4.5 %collective-permute-done.9.refs_12_ = f32[1,32,128]{2,1,0:T(8,128)S(1)} collective-permute-done((f32[1,32,128]{2,1,0:T(8,128)}, f32[1,32,128]{2,1,0:T(8,128)S(1)}, u32[]{:S(2)}, u32[]{:S(2)}) %collective-permute-start.9) | collective-permute-done | bytes 16416 | tf_op jit(solution)/shard_map/ppermute | solution.py:350
  54.8 0.0 copy-start.9
  54.8 0.0 collective-permute-done.6.refs_9_
  54.8 0.0 copy-start.4
  54.8 0.0 collective-permute-done.7.refs_10_
  54.8 0.0 copy-start.5
  54.8 0.0 copy-done.8
  54.8 0.6 copy-done.9
  55.4 0.0 copy-done.4
  55.4 0.0 copy-done.5
  55.5 7.9 %shard_map.30 = f32[16,64,128]{2,1,0:T(8,128)} custom-call(s32[2]{0:T(128)} %pad_add_fusion.refs_0_.at, f32[18,80,128]{2,1,0:T(8,128)} %get-tuple-element.18.refs_1_, f32[16,64,128]{2,1,0:T(8,128)} %get-tuple-element.19.refs_2_, f32[16,64,128]{2,1,0:T(8,128)} %get-tuple-element.20.refs_3_, f32[12,40,128]{2,1,0:T(8,128)} %get-tuple-element.21.e1.refs_4_, ...), custom_call_target="tpu_custom_call" | custom-call | tf_op jit(solution)/shard_map/pallas_call | solution.py:20
  (4 shorter events, 0.1 us)
Async XLA Ops:
  1.2 12.5 %collective-permute-start.1 = (f32[2,4,64,128]{3,2,1,0:T(8,128)S(1)}, f32[2,4,64,128]{3,2,1,0:T(8,128)S(1)}, u32[]{:S(2)}, u32[]{:S(2)}) collective-permute-start(f32[2,4,64,128]{3,2,1,0:T(8,128)S(1)} %get-tuple-element.37), channel_id=1, source_target_pairs={{1,2},{2,1},{3,4},{4,3},{5,6},{6,5},{7,8},{8,7},{9,10},{10,9},{11,... | collective-permute-start | bytes 786440 | tf_op jit(solution)/shard_map/ppermute | solution.py:320
  7.4 7.8 %collective-permute-start = (f32[2,4,64,128]{3,2,1,0:T(8,128)S(1)}, f32[2,4,64,128]{3,2,1,0:T(8,128)S(1)}, u32[]{:S(2)}, u32[]{:S(2)}) collective-permute-start(f32[2,4,64,128]{3,2,1,0:T(8,128)S(1)} %get-tuple-element.38), channel_id=1, source_target_pairs={{0,1},{1,0},{2,3},{3,2},{4,5},{5,4},{6,7},{7,6},{8,9},{9,8},{10,11... | collective-permute-start | bytes 786440 | tf_op jit(solution)/shard_map/ppermute | solution.py:319
  13.7 1.6 %copy-start = (f32[2,4,64,128]{3,2,1,0:T(8,128)}, f32[2,4,64,128]{3,2,1,0:T(8,128)S(1)}, u32[]{:S(2)}) copy-start(f32[2,4,64,128]{3,2,1,0:T(8,128)S(1)} %collective-permute-done.1.refs_4_) | copy-start | bytes 786436
  15.2 0.7 %copy-start.1 = (f32[2,4,64,128]{3,2,1,0:T(8,128)}, f32[2,4,64,128]{3,2,1,0:T(8,128)S(1)}, u32[]{:S(2)}) copy-start(f32[2,4,64,128]{3,2,1,0:T(8,128)S(1)} %collective-permute-done.refs_3_) | copy-start | bytes 786436
  16.0 5.9 %collective-permute-start.3 = (f32[2,24,4,128]{3,2,1,0:T(4,128)S(1)}, f32[2,24,4,128]{3,2,1,0:T(4,128)S(1)}, u32[]{:S(2)}, u32[]{:S(2)}) collective-permute-start(f32[2,24,4,128]{3,2,1,0:T(4,128)S(1)} %get-tuple-element.47), channel_id=1, source_target_pairs={{16,32},{32,16},{48,64},{64,48},{80,96},{96,80},{17,33},{33,17},{4... | collective-permute-start | bytes 294920 | tf_op jit(solution)/shard_map/ppermute | solution.py:329
  18.0 4.0 %collective-permute-start.2 = (f32[2,24,4,128]{3,2,1,0:T(4,128)S(1)}, f32[2,24,4,128]{3,2,1,0:T(4,128)S(1)}, u32[]{:S(2)}, u32[]{:S(2)}) collective-permute-start(f32[2,24,4,128]{3,2,1,0:T(4,128)S(1)} %get-tuple-element.48), channel_id=1, source_target_pairs={{0,16},{16,0},{32,48},{48,32},{64,80},{80,64},{96,112},{112,96},{1... | collective-permute-start | bytes 294920 | tf_op jit(solution)/shard_map/ppermute | solution.py:328
  22.0 0.6 %copy-start.2 = (f32[2,24,4,128]{3,2,1,0:T(4,128)}, f32[2,24,4,128]{3,2,1,0:T(4,128)S(1)}, u32[]{:S(2)}) copy-start(f32[2,24,4,128]{3,2,1,0:T(4,128)S(1)} %collective-permute-done.3.refs_6_) | copy-start | bytes 294916
  22.6 0.6 %copy-start.3 = (f32[2,24,4,128]{3,2,1,0:T(4,128)}, f32[2,24,4,128]{3,2,1,0:T(4,128)S(1)}, u32[]{:S(2)}) copy-start(f32[2,24,4,128]{3,2,1,0:T(4,128)S(1)} %collective-permute-done.2.refs_5_) | copy-start | bytes 294916
  32.8 2.0 %collective-permute-start.4 = (f32[4,8,128]{2,1,0:T(8,128)}, f32[4,8,128]{2,1,0:T(8,128)S(1)}, u32[]{:S(2)}, u32[]{:S(2)}) collective-permute-start(f32[4,8,128]{2,1,0:T(8,128)} %get-tuple-element.24), channel_id=1, source_target_pairs={{0,16},{16,0},{32,48},{48,32},{64,80},{80,64},{96,112},{112,96},{1... | collective-permute-start | bytes 49160 | tf_op jit(solution)/shard_map/ppermute | solution.py:339
  32.9 5.3 %collective-permute-start.5 = (f32[4,8,128]{2,1,0:T(8,128)}, f32[4,8,128]{2,1,0:T(8,128)S(1)}, u32[]{:S(2)}, u32[]{:S(2)}) collective-permute-start(f32[4,8,128]{2,1,0:T(8,128)} %get-tuple-element.25), channel_id=1, source_target_pairs={{16,32},{32,16},{48,64},{64,48},{80,96},{96,80},{17,33},{33,17},{4... | collective-permute-start | bytes 49160 | tf_op jit(solution)/shard_map/ppermute | solution.py:340
  34.9 3.3 %copy-start.6 = (f32[4,8,128]{2,1,0:T(8,128)}, f32[4,8,128]{2,1,0:T(8,128)S(1)}, u32[]{:S(2)}) copy-start(f32[4,8,128]{2,1,0:T(8,128)S(1)} %collective-permute-done.4.ye.refs_7_) | copy-start | bytes 49156
  38.2 0.6 copy-start.7
  40.5 14.3 %collective-permute-start.6 = (f32[5,32,128]{2,1,0:T(8,128)}, f32[5,32,128]{2,1,0:T(8,128)S(1)}, u32[]{:S(2)}, u32[]{:S(2)}) collective-permute-start(f32[5,32,128]{2,1,0:T(8,128)} %get-tuple-element.27), channel_id=1, source_target_pairs={{0,1},{1,0},{2,3},{3,2},{4,5},{5,4},{6,7},{7,6},{8,9},{9,8},{10,11... | collective-permute-start | bytes 245768 | tf_op jit(solution)/shard_map/ppermute | solution.py:347
  40.8 14.0 %collective-permute-start.7 = (f32[5,32,128]{2,1,0:T(8,128)}, f32[5,32,128]{2,1,0:T(8,128)S(1)}, u32[]{:S(2)}, u32[]{:S(2)}) collective-permute-start(f32[5,32,128]{2,1,0:T(8,128)} %get-tuple-element.28), channel_id=1, source_target_pairs={{1,2},{2,1},{3,4},{4,3},{5,6},{6,5},{7,8},{8,7},{9,10},{10,9},{11,... | collective-permute-start | bytes 245768 | tf_op jit(solution)/shard_map/ppermute | solution.py:348
  44.8 5.5 %collective-permute-start.8 = (f32[1,32,128]{2,1,0:T(8,128)}, f32[1,32,128]{2,1,0:T(8,128)S(1)}, u32[]{:S(2)}, u32[]{:S(2)}) collective-permute-start(f32[1,32,128]{2,1,0:T(8,128)} %get-tuple-element.29), channel_id=1, source_target_pairs={{0,2},{1,3},{2,0},{3,1},{4,6},{5,7},{6,4},{7,5},{8,10},{9,11},{10,... | collective-permute-start | bytes 49160 | tf_op jit(solution)/shard_map/ppermute | solution.py:349
  46.6 8.2 %collective-permute-start.9 = (f32[1,32,128]{2,1,0:T(8,128)}, f32[1,32,128]{2,1,0:T(8,128)S(1)}, u32[]{:S(2)}, u32[]{:S(2)}) collective-permute-start(f32[1,32,128]{2,1,0:T(8,128)} %get-tuple-element.30), channel_id=1, source_target_pairs={{2,4},{4,2},{3,5},{5,3},{6,8},{8,6},{7,9},{9,7},{10,12},{12,10},{1... | collective-permute-start | bytes 49160 | tf_op jit(solution)/shard_map/ppermute | solution.py:350
  50.3 4.5 %copy-start.8 = (f32[1,32,128]{2,1,0:T(8,128)}, f32[1,32,128]{2,1,0:T(8,128)S(1)}, u32[]{:S(2)}) copy-start(f32[1,32,128]{2,1,0:T(8,128)S(1)} %collective-permute-done.8.refs_11_) | copy-start | bytes 49156
  54.8 0.6 copy-start.9
  54.8 0.6 %copy-start.4 = (f32[5,32,128]{2,1,0:T(8,128)}, f32[5,32,128]{2,1,0:T(8,128)S(1)}, u32[]{:S(2)}) copy-start(f32[5,32,128]{2,1,0:T(8,128)S(1)} %collective-permute-done.6.refs_9_) | copy-start | bytes 245764
  54.8 0.7 %copy-start.5 = (f32[5,32,128]{2,1,0:T(8,128)}, f32[5,32,128]{2,1,0:T(8,128)S(1)}, u32[]{:S(2)}) copy-start(f32[5,32,128]{2,1,0:T(8,128)S(1)} %collective-permute-done.7.refs_10_) | copy-start | bytes 245764

commit v2 on v1

--- a/solution.py
+++ b/solution.py
@@ -297,11 +297,10 @@
 
 
 def swaps(size, apart):
-    inner = [(i, i ^ apart) for i in range(size)]
-    outer = []
-    for i in range(apart, size - apart):
-        if i & apart:
-            outer += [(i, i + apart), (i + apart, i)]
+    inner, outer = [], []
+    for i in range(size):
+        inner.append((i, i ^ apart))
+        outer.append((i, (i + apart) % size if i & apart else (i - apart) % size))
     return inner, outer
 
 

time: 63.7 us -> 59.8 us (0.939)
  the two profiles are of different devices: /device:TPU:14 before, /device:TPU:0 now
where the time goes in v2:
time: 59.8 us; the launch traced here: 59.5 us
  Pallas kernels  19.2 us (32%)
  waiting for transfers between devices  17.9 us (30%)
  starting transfers between devices  16.4 us (27%)
  local copies, waits for them, and re-layouts  5.26 us (9%)
  other arithmetic  0.73 us (1%)
    pallas_call x3, Pallas kernels, call(): pl.pallas_call(body, out_shape=outs, in_specs=[SM] + [VM] * (len(args) -...  19.2 us
    ppermute x1, starting transfers between devices, shards(): xo = lax.ppermute(jnp.where(x_even, first, last), 'blk', near_out)  6.42 us
    ppermute x1, waiting for transfers between devices, shards(): xo = lax.ppermute(jnp.where(x_even, first, last), 'blk', near_out)  5.34 us
    ppermute x1, starting transfers between devices, shards(): xo = lax.ppermute(so, 'blk', near_out)  3.46 us
    unnamed x20, local copies, waits for them, and re-layouts  3.15 us
    ppermute x1, waiting for transfers between devices, shards(): xf = lax.ppermute(sf, 'blk', far_in)  3.04 us
    ppermute x1, waiting for transfers between devices, shards(): yo = lax.ppermute(jnp.where(y_even, first, last), 'agg', side_out)  2.97 us
    ppermute x1, waiting for transfers between devices, shards(): yo = lax.ppermute(so, 'agg', side_out)  2.75 us
  transfers between devices with their start and end apart: 10, of which 6 were waited for; matrix products, arithmetic and copies ran while one was open for 3% of the time, Pallas kernels for 0%

profile of v2, /device:TPU:0, one launch (start us, length us, event | category | flops | bytes accessed | tf_op | source)
XLA Modules:
  0.0 59.5 jit_solution(587968504692445676)
XLA Ops:
  0.0 1.1 %slice_bitcast_fusion.2 = (f32[1,4,64,128]{3,2,1,0:T(8,128)S(1)}, f32[1,4,64,128]{3,2,1,0:T(8,128)S(1)}, f32[1,4,64,128]{3,2,1,0:T(8,128)S(1)}, f32[1,4,64,128]{3,2,1,0:T(8,128)S(1)}) fusion(f32[16,64,128]{2,1,0:T(8,128)} %refs_2_.1, f32[16,64,128]{2,1,0:T(8,128)} %refs_1_.1), kind=kLoop, calls=%fused_computation.6 | loop fusion | bytes 1048576 | tf_op jit(solution)/shard_map/stack | solution.py:317
  1.2 6.4 %collective-permute-start.1 = (f32[2,4,64,128]{3,2,1,0:T(8,128)S(1)}, f32[2,4,64,128]{3,2,1,0:T(8,128)S(1)}, u32[]{:S(2)}, u32[]{:S(2)}) collective-permute-start(f32[2,4,64,128]{3,2,1,0:T(8,128)S(1)} %get-tuple-element.37), channel_id=1, source_target_pairs={{0,15},{1,2},{2,1},{3,4},{4,3},{5,6},{6,5},{7,8},{8,7},{9,10},{10,... | collective-permute-start | bytes 786440 | tf_op jit(solution)/shard_map/ppermute | solution.py:319
  7.6 0.0 collective-permute-start
  7.6 1.0 %slice_bitcast_fusion.6 = (f32[1,16,4,128]{3,2,1,0:T(4,128)S(1)}, f32[1,16,4,128]{3,2,1,0:T(4,128)S(1)}, f32[1,16,4,128]{3,2,1,0:T(4,128)S(1)}, f32[1,16,4,128]{3,2,1,0:T(4,128)S(1)}) fusion(f32[16,64,128]{2,1,0:T(8,128)} %refs_2_.1, f32[16,64,128]{2,1,0:T(8,128)} %refs_1_.1), kind=kLoop, calls=%fused_computation.16 | loop fusion | bytes 262144 | tf_op jit(solution)/shard_map/stack | solution.py:323
  8.6 5.3 %collective-permute-done.1.refs_4_ = f32[2,4,64,128]{3,2,1,0:T(8,128)S(1)} collective-permute-done((f32[2,4,64,128]{3,2,1,0:T(8,128)S(1)}, f32[2,4,64,128]{3,2,1,0:T(8,128)S(1)}, u32[]{:S(2)}, u32[]{:S(2)}) %collective-permute-start.1) | collective-permute-done | bytes 262176 | tf_op jit(solution)/shard_map/ppermute | solution.py:319
  13.9 0.0 copy-start
  13.9 1.5 %collective-permute-done.refs_3_ = f32[2,4,64,128]{3,2,1,0:T(8,128)S(1)} collective-permute-done((f32[2,4,64,128]{3,2,1,0:T(8,128)S(1)}, f32[2,4,64,128]{3,2,1,0:T(8,128)S(1)}, u32[]{:S(2)}, u32[]{:S(2)}) %collective-permute-start) | collective-permute-done | bytes 262176 | tf_op jit(solution)/shard_map/ppermute | solution.py:318
  15.4 0.0 copy-start.1
  15.4 0.0 copy-done
  15.4 0.6 %copy-done.1 = f32[2,4,64,128]{3,2,1,0:T(8,128)} copy-done((f32[2,4,64,128]{3,2,1,0:T(8,128)}, f32[2,4,64,128]{3,2,1,0:T(8,128)S(1)}, u32[]{:S(2)}) %copy-start.1) | copy-done | bytes 262168
  16.1 0.1 broadcast_select_fusion.2
  16.2 1.4 %collective-permute-start.3 = (f32[2,24,4,128]{3,2,1,0:T(4,128)S(1)}, f32[2,24,4,128]{3,2,1,0:T(4,128)S(1)}, u32[]{:S(2)}, u32[]{:S(2)}) collective-permute-start(f32[2,24,4,128]{3,2,1,0:T(4,128)S(1)} %get-tuple-element.47), channel_id=1, source_target_pairs={{0,112},{16,32},{32,16},{48,64},{64,48},{80,96},{96,80},{112,0},{1... | collective-permute-start | bytes 294920 | tf_op jit(solution)/shard_map/ppermute | solution.py:328
  17.6 0.4 collective-permute-start.2
  17.9 0.6 pad_add_fusion.refs_0_.at
  18.5 3.0 %collective-permute-done.3.refs_6_ = f32[2,24,4,128]{3,2,1,0:T(4,128)S(1)} collective-permute-done((f32[2,24,4,128]{3,2,1,0:T(4,128)S(1)}, f32[2,24,4,128]{3,2,1,0:T(4,128)S(1)}, u32[]{:S(2)}, u32[]{:S(2)}) %collective-permute-start.3) | collective-permute-done | bytes 98336 | tf_op jit(solution)/shard_map/ppermute | solution.py:328
  21.5 0.0 copy-start.2
  21.5 0.0 collective-permute-done.2.refs_5_
  21.5 0.6 %copy-done.2 = f32[2,24,4,128]{3,2,1,0:T(4,128)} copy-done((f32[2,24,4,128]{3,2,1,0:T(4,128)}, f32[2,24,4,128]{3,2,1,0:T(4,128)S(1)}, u32[]{:S(2)}) %copy-start.2) | copy-done | bytes 98328
  22.1 0.0 copy-start.3
  22.1 0.6 %copy-done.3 = f32[2,24,4,128]{3,2,1,0:T(4,128)} copy-done((f32[2,24,4,128]{3,2,1,0:T(4,128)}, f32[2,24,4,128]{3,2,1,0:T(4,128)S(1)}, u32[]{:S(2)}) %copy-start.3) | copy-done | bytes 98328
  22.8 9.6 %shard_map.28 = (f32[18,80,128]{2,1,0:T(8,128)}, f32[16,64,128]{2,1,0:T(8,128)}, f32[16,64,128]{2,1,0:T(8,128)}, f32[12,40,128]{2,1,0:T(8,128)}, f32[12,40,128]{...) custom-call(s32[2]{0:T(128)} %pad_add_fusion.refs_0_.at, ...), custom_call_target="tpu_custom_call" | custom-call | tf_op jit(solution)/shard_map/pallas_call | solution.py:20
  32.3 0.0 collective-permute-start.4
  32.3 1.9 %collective-permute-start.5 = (f32[4,8,128]{2,1,0:T(8,128)}, f32[4,8,128]{2,1,0:T(8,128)S(1)}, u32[]{:S(2)}, u32[]{:S(2)}) collective-permute-start(f32[4,8,128]{2,1,0:T(8,128)} %get-tuple-element.25), channel_id=1, source_target_pairs={{0,112},{16,32},{32,16},{48,64},{64,48},{80,96},{96,80},{112,0},{1... | collective-permute-start | bytes 49160 | tf_op jit(solution)/shard_map/ppermute | solution.py:339
  34.2 0.0 collective-permute-done.4.ye.refs_7_
  34.3 0.0 copy-start.6
  34.3 2.8 %collective-permute-done.5.yo.refs_8_ = f32[4,8,128]{2,1,0:T(8,128)S(1)} collective-permute-done((f32[4,8,128]{2,1,0:T(8,128)}, f32[4,8,128]{2,1,0:T(8,128)S(1)}, u32[]{:S(2)}, u32[]{:S(2)}) %collective-permute-start.5) | collective-permute-done | bytes 16416 | tf_op jit(solution)/shard_map/ppermute | solution.py:339
  37.0 0.0 copy-start.7
  37.0 0.0 copy-done.6
  37.0 0.6 copy-done.7
  37.6 1.7 %shard_map.29 = (f32[4,32,128]{2,1,0:T(8,128)}, f32[5,32,128]{2,1,0:T(8,128)}, f32[5,32,128]{2,1,0:T(8,128)}, f32[1,32,128]{2,1,0:T(8,128)}, f32[1,32,128]{2,1,0:T(8,128)}) custom-call(s32[2]{0:T(128)} %pad_add_fusion.refs_0_.at, f32[4,16,128]{2,1,0:T(8,128)} %get-tuple-element.23.bc2, f32[4,8,128]{2,1,0:T(8,128)} %copy-done.6, f32[4,8,128]{2,1,0:T(8,128)} %copy-done.7, ...), custom_call_target="tpu_custom_call" | custom-call | tf_op jit(solution)/shard_map/pallas_call | solution.py:20
  39.3 0.3 collective-permute-start.6
  39.6 3.5 %collective-permute-start.7 = (f32[5,32,128]{2,1,0:T(8,128)}, f32[5,32,128]{2,1,0:T(8,128)S(1)}, u32[]{:S(2)}, u32[]{:S(2)}) collective-permute-start(f32[5,32,128]{2,1,0:T(8,128)} %get-tuple-element.28), channel_id=1, source_target_pairs={{0,15},{1,2},{2,1},{3,4},{4,3},{5,6},{6,5},{7,8},{8,7},{9,10},{10,... | collective-permute-start | bytes 245768 | tf_op jit(solution)/shard_map/ppermute | solution.py:347
  43.1 0.3 collective-permute-start.8
  43.4 2.2 %collective-permute-start.9 = (f32[1,32,128]{2,1,0:T(8,128)}, f32[1,32,128]{2,1,0:T(8,128)S(1)}, u32[]{:S(2)}, u32[]{:S(2)}) collective-permute-start(f32[1,32,128]{2,1,0:T(8,128)} %get-tuple-element.30), channel_id=1, source_target_pairs={{0,14},{1,15},{2,4},{3,5},{4,2},{5,3},{6,8},{7,9},{8,6},{9,7},{10,... | collective-permute-start | bytes 49160 | tf_op jit(solution)/shard_map/ppermute | solution.py:349
  45.6 3.0 %collective-permute-done.8.refs_11_ = f32[1,32,128]{2,1,0:T(8,128)S(1)} collective-permute-done((f32[1,32,128]{2,1,0:T(8,128)}, f32[1,32,128]{2,1,0:T(8,128)S(1)}, u32[]{:S(2)}, u32[]{:S(2)}) %collective-permute-start.8) | collective-permute-done | bytes 16416 | tf_op jit(solution)/shard_map/ppermute | solution.py:348
  48.7 0.0 copy-start.8
  48.7 2.3 %collective-permute-done.9.refs_12_ = f32[1,32,128]{2,1,0:T(8,128)S(1)} collective-permute-done((f32[1,32,128]{2,1,0:T(8,128)}, f32[1,32,128]{2,1,0:T(8,128)S(1)}, u32[]{:S(2)}, u32[]{:S(2)}) %collective-permute-start.9) | collective-permute-done | bytes 16416 | tf_op jit(solution)/shard_map/ppermute | solution.py:349
  51.0 0.0 copy-start.9
  51.0 0.0 collective-permute-done.6.refs_9_
  51.0 0.0 copy-start.4
  51.0 0.0 collective-permute-done.7.refs_10_
  51.0 0.0 copy-start.5
  51.0 0.0 copy-done.8
  51.0 0.6 copy-done.9
  51.6 0.0 copy-done.4
  51.6 0.0 copy-done.5
  51.6 7.9 %shard_map.30 = f32[16,64,128]{2,1,0:T(8,128)} custom-call(s32[2]{0:T(128)} %pad_add_fusion.refs_0_.at, f32[18,80,128]{2,1,0:T(8,128)} %get-tuple-element.18.refs_1_, f32[16,64,128]{2,1,0:T(8,128)} %get-tuple-element.19.refs_2_, f32[16,64,128]{2,1,0:T(8,128)} %get-tuple-element.20.refs_3_, f32[12,40,128]{2,1,0:T(8,128)} %get-tuple-element.21.e1.refs_4_, ...), custom_call_target="tpu_custom_call" | custom-call | tf_op jit(solution)/shard_map/pallas_call | solution.py:20
  (4 shorter events, 0.1 us)
Async XLA Ops:
  1.2 12.7 %collective-permute-start.1 = (f32[2,4,64,128]{3,2,1,0:T(8,128)S(1)}, f32[2,4,64,128]{3,2,1,0:T(8,128)S(1)}, u32[]{:S(2)}, u32[]{:S(2)}) collective-permute-start(f32[2,4,64,128]{3,2,1,0:T(8,128)S(1)} %get-tuple-element.37), channel_id=1, source_target_pairs={{0,15},{1,2},{2,1},{3,4},{4,3},{5,6},{6,5},{7,8},{8,7},{9,10},{10,... | collective-permute-start | bytes 786440 | tf_op jit(solution)/shard_map/ppermute | solution.py:319
  7.6 7.8 %collective-permute-start = (f32[2,4,64,128]{3,2,1,0:T(8,128)S(1)}, f32[2,4,64,128]{3,2,1,0:T(8,128)S(1)}, u32[]{:S(2)}, u32[]{:S(2)}) collective-permute-start(f32[2,4,64,128]{3,2,1,0:T(8,128)S(1)} %get-tuple-element.38), channel_id=1, source_target_pairs={{0,1},{1,0},{2,3},{3,2},{4,5},{5,4},{6,7},{7,6},{8,9},{9,8},{10,11... | collective-permute-start | bytes 786440 | tf_op jit(solution)/shard_map/ppermute | solution.py:318
  13.9 1.5 %copy-start = (f32[2,4,64,128]{3,2,1,0:T(8,128)}, f32[2,4,64,128]{3,2,1,0:T(8,128)S(1)}, u32[]{:S(2)}) copy-start(f32[2,4,64,128]{3,2,1,0:T(8,128)S(1)} %collective-permute-done.1.refs_4_) | copy-start | bytes 786436
  15.4 0.7 %copy-start.1 = (f32[2,4,64,128]{3,2,1,0:T(8,128)}, f32[2,4,64,128]{3,2,1,0:T(8,128)S(1)}, u32[]{:S(2)}) copy-start(f32[2,4,64,128]{3,2,1,0:T(8,128)S(1)} %collective-permute-done.refs_3_) | copy-start | bytes 786436
  16.2 5.3 %collective-permute-start.3 = (f32[2,24,4,128]{3,2,1,0:T(4,128)S(1)}, f32[2,24,4,128]{3,2,1,0:T(4,128)S(1)}, u32[]{:S(2)}, u32[]{:S(2)}) collective-permute-start(f32[2,24,4,128]{3,2,1,0:T(4,128)S(1)} %get-tuple-element.47), channel_id=1, source_target_pairs={{0,112},{16,32},{32,16},{48,64},{64,48},{80,96},{96,80},{112,0},{1... | collective-permute-start | bytes 294920 | tf_op jit(solution)/shard_map/ppermute | solution.py:328
  17.6 3.9 %collective-permute-start.2 = (f32[2,24,4,128]{3,2,1,0:T(4,128)S(1)}, f32[2,24,4,128]{3,2,1,0:T(4,128)S(1)}, u32[]{:S(2)}, u32[]{:S(2)}) collective-permute-start(f32[2,24,4,128]{3,2,1,0:T(4,128)S(1)} %get-tuple-element.48), channel_id=1, source_target_pairs={{0,16},{16,0},{32,48},{48,32},{64,80},{80,64},{96,112},{112,96},{1... | collective-permute-start | bytes 294920 | tf_op jit(solution)/shard_map/ppermute | solution.py:327
  21.5 0.6 %copy-start.2 = (f32[2,24,4,128]{3,2,1,0:T(4,128)}, f32[2,24,4,128]{3,2,1,0:T(4,128)S(1)}, u32[]{:S(2)}) copy-start(f32[2,24,4,128]{3,2,1,0:T(4,128)S(1)} %collective-permute-done.3.refs_6_) | copy-start | bytes 294916
  22.1 0.6 %copy-start.3 = (f32[2,24,4,128]{3,2,1,0:T(4,128)}, f32[2,24,4,128]{3,2,1,0:T(4,128)S(1)}, u32[]{:S(2)}) copy-start(f32[2,24,4,128]{3,2,1,0:T(4,128)S(1)} %collective-permute-done.2.refs_5_) | copy-start | bytes 294916
  32.3 1.9 %collective-permute-start.4 = (f32[4,8,128]{2,1,0:T(8,128)}, f32[4,8,128]{2,1,0:T(8,128)S(1)}, u32[]{:S(2)}, u32[]{:S(2)}) collective-permute-start(f32[4,8,128]{2,1,0:T(8,128)} %get-tuple-element.24), channel_id=1, source_target_pairs={{0,16},{16,0},{32,48},{48,32},{64,80},{80,64},{96,112},{112,96},{1... | collective-permute-start | bytes 49160 | tf_op jit(solution)/shard_map/ppermute | solution.py:338
  32.3 4.7 %collective-permute-start.5 = (f32[4,8,128]{2,1,0:T(8,128)}, f32[4,8,128]{2,1,0:T(8,128)S(1)}, u32[]{:S(2)}, u32[]{:S(2)}) collective-permute-start(f32[4,8,128]{2,1,0:T(8,128)} %get-tuple-element.25), channel_id=1, source_target_pairs={{0,112},{16,32},{32,16},{48,64},{64,48},{80,96},{96,80},{112,0},{1... | collective-permute-start | bytes 49160 | tf_op jit(solution)/shard_map/ppermute | solution.py:339
  34.3 2.8 %copy-start.6 = (f32[4,8,128]{2,1,0:T(8,128)}, f32[4,8,128]{2,1,0:T(8,128)S(1)}, u32[]{:S(2)}) copy-start(f32[4,8,128]{2,1,0:T(8,128)S(1)} %collective-permute-done.4.ye.refs_7_) | copy-start | bytes 49156
  37.0 0.6 copy-start.7
  39.3 11.7 %collective-permute-start.6 = (f32[5,32,128]{2,1,0:T(8,128)}, f32[5,32,128]{2,1,0:T(8,128)S(1)}, u32[]{:S(2)}, u32[]{:S(2)}) collective-permute-start(f32[5,32,128]{2,1,0:T(8,128)} %get-tuple-element.27), channel_id=1, source_target_pairs={{0,1},{1,0},{2,3},{3,2},{4,5},{5,4},{6,7},{7,6},{8,9},{9,8},{10,11... | collective-permute-start | bytes 245768 | tf_op jit(solution)/shard_map/ppermute | solution.py:346
  39.6 11.4 %collective-permute-start.7 = (f32[5,32,128]{2,1,0:T(8,128)}, f32[5,32,128]{2,1,0:T(8,128)S(1)}, u32[]{:S(2)}, u32[]{:S(2)}) collective-permute-start(f32[5,32,128]{2,1,0:T(8,128)} %get-tuple-element.28), channel_id=1, source_target_pairs={{0,15},{1,2},{2,1},{3,4},{4,3},{5,6},{6,5},{7,8},{8,7},{9,10},{10,... | collective-permute-start | bytes 245768 | tf_op jit(solution)/shard_map/ppermute | solution.py:347
  43.1 5.6 %collective-permute-start.8 = (f32[1,32,128]{2,1,0:T(8,128)}, f32[1,32,128]{2,1,0:T(8,128)S(1)}, u32[]{:S(2)}, u32[]{:S(2)}) collective-permute-start(f32[1,32,128]{2,1,0:T(8,128)} %get-tuple-element.29), channel_id=1, source_target_pairs={{0,2},{1,3},{2,0},{3,1},{4,6},{5,7},{6,4},{7,5},{8,10},{9,11},{10,... | collective-permute-start | bytes 49160 | tf_op jit(solution)/shard_map/ppermute | solution.py:348
  43.4 7.6 %collective-permute-start.9 = (f32[1,32,128]{2,1,0:T(8,128)}, f32[1,32,128]{2,1,0:T(8,128)S(1)}, u32[]{:S(2)}, u32[]{:S(2)}) collective-permute-start(f32[1,32,128]{2,1,0:T(8,128)} %get-tuple-element.30), channel_id=1, source_target_pairs={{0,14},{1,15},{2,4},{3,5},{4,2},{5,3},{6,8},{7,9},{8,6},{9,7},{10,... | collective-permute-start | bytes 49160 | tf_op jit(solution)/shard_map/ppermute | solution.py:349
  48.7 2.3 %copy-start.8 = (f32[1,32,128]{2,1,0:T(8,128)}, f32[1,32,128]{2,1,0:T(8,128)S(1)}, u32[]{:S(2)}) copy-start(f32[1,32,128]{2,1,0:T(8,128)S(1)} %collective-permute-done.8.refs_11_) | copy-start | bytes 49156
  51.0 0.6 %copy-start.9 = (f32[1,32,128]{2,1,0:T(8,128)}, f32[1,32,128]{2,1,0:T(8,128)S(1)}, u32[]{:S(2)}) copy-start(f32[1,32,128]{2,1,0:T(8,128)S(1)} %collective-permute-done.9.refs_12_) | copy-start | bytes 49156
  51.0 0.6 %copy-start.4 = (f32[5,32,128]{2,1,0:T(8,128)}, f32[5,32,128]{2,1,0:T(8,128)S(1)}, u32[]{:S(2)}) copy-start(f32[5,32,128]{2,1,0:T(8,128)S(1)} %collective-permute-done.6.refs_9_) | copy-start | bytes 245764
  51.0 0.7 %copy-start.5 = (f32[5,32,128]{2,1,0:T(8,128)}, f32[5,32,128]{2,1,0:T(8,128)S(1)}, u32[]{:S(2)}) copy-start(f32[5,32,128]{2,1,0:T(8,128)S(1)} %collective-permute-done.7.refs_10_) | copy-start | bytes 245764

commit v3 on v2

--- a/solution.py
+++ b/solution.py
@@ -23,7 +23,7 @@
         in_specs=[SM] + [VM] * (len(args) - 1),
         out_specs=tuple(VM for _ in outs),
         scratch_shapes=[pltpu.VMEM(s, F32) for s in scratch],
-        compiler_params=pltpu.CompilerParams(vmem_limit_bytes=56 << 20),
+        compiler_params=pltpu.CompilerParams(vmem_limit_bytes=16 << 20),
     )(*args)
 
 

time: 59.8 us -> 52 us (0.87)
  Pallas kernels: 19.2 us -> 14.9 us
  local copies, waits for them, and re-layouts: 5.26 us -> 1.18 us
  waiting for transfers between devices: 17.9 us -> 18.9 us
    pallas_call x3, Pallas kernels: 19.2 us -> 14.9 us  [call(): pl.pallas_call(body, out_shape=outs, in_specs=[SM] + [VM] * (len(args) -...]
    unnamed x20 -> x4, local copies, waits for them, and re-layouts: 3.15 us -> 0.01 us
    another operation x1, local copies, waits for them, and re-layouts: 0.96 us -> 0.03 us  [rows(): own = jnp.stack([b[:, cut], c[:, cut]])]
    ppermute x1, waiting for transfers between devices: 5.34 us -> 6.26 us  [shards(): xo = lax.ppermute(jnp.where(x_even, first, last), 'blk', near_out)]
  transfers between devices with their start and end apart: 10 -> 10, of which waited for: 6 -> 6; matrix products, arithmetic and copies ran while one was open for 3% -> 0% of each run, Pallas kernels for 0% -> 0%
where the time goes in v3:
time: 52 us; the launch traced here: 51.9 us
  waiting for transfers between devices  18.9 us (36%)
  starting transfers between devices  16.5 us (32%)
  Pallas kernels  14.9 us (29%)
  local copies, waits for them, and re-layouts  1.18 us (2%)
    pallas_call x3, Pallas kernels, call(): pl.pallas_call(body, out_shape=outs, in_specs=[SM] + [VM] * (len(args) -...  14.9 us
    ppermute x1, starting transfers between devices, shards(): xo = lax.ppermute(jnp.where(x_even, first, last), 'blk', near_out)  6.42 us
    ppermute x1, waiting for transfers between devices, shards(): xo = lax.ppermute(jnp.where(x_even, first, last), 'blk', near_out)  6.26 us
    ppermute x1, waiting for transfers between devices, shards(): yo = lax.ppermute(jnp.where(y_even, first, last), 'agg', side_out)  3.48 us
    ppermute x1, starting transfers between devices, shards(): xo = lax.ppermute(so, 'blk', near_out)  3.41 us
    ppermute x1, waiting for transfers between devices, shards(): xf = lax.ppermute(sf, 'blk', far_in)  2.83 us
    ppermute x1, waiting for transfers between devices, shards(): yo = lax.ppermute(so, 'agg', side_out)  2.55 us
    ppermute x1, waiting for transfers between devices, shards(): xg = lax.ppermute(sg, 'blk', far_out)  2.33 us
  transfers between devices with their start and end apart: 10, of which 6 were waited for; matrix products, arithmetic and copies ran while one was open for 0% of the time, Pallas kernels for 0%

profile of v3, /device:TPU:0, one launch (start us, length us, event | category | flops | bytes accessed | tf_op | source)
XLA Modules:
  0.0 51.9 jit_solution(5679734501976627071)
XLA Ops:
  0.0 1.1 %slice_bitcast_fusion.2 = (f32[1,4,64,128]{3,2,1,0:T(8,128)S(1)}, f32[1,4,64,128]{3,2,1,0:T(8,128)S(1)}, f32[1,4,64,128]{3,2,1,0:T(8,128)S(1)}, f32[1,4,64,128]{3,2,1,0:T(8,128)S(1)}) fusion(f32[16,64,128]{2,1,0:T(8,128)} %refs_2_.1, f32[16,64,128]{2,1,0:T(8,128)} %refs_1_.1), kind=kLoop, calls=%fused_computation.6 | loop fusion | bytes 1048576 | tf_op jit(solution)/shard_map/stack | solution.py:317
  1.1 0.0 copy-start
  1.1 0.0 copy-start.1
  1.2 6.4 %collective-permute-start.1 = (f32[2,4,64,128]{3,2,1,0:T(8,128)S(1)}, f32[2,4,64,128]{3,2,1,0:T(8,128)S(1)}, u32[]{:S(2)}, u32[]{:S(2)}) collective-permute-start(f32[2,4,64,128]{3,2,1,0:T(8,128)S(1)} %get-tuple-element.37), channel_id=1, source_target_pairs={{0,15},{1,2},{2,1},{3,4},{4,3},{5,6},{6,5},{7,8},{8,7},{9,10},{10,... | collective-permute-start | bytes 786440 | tf_op jit(solution)/shard_map/ppermute | solution.py:319
  7.6 0.0 collective-permute-start
  7.6 0.0 copy-done
  7.6 0.0 copy-done.1
  7.7 6.3 %collective-permute-done.1.refs_4_ = f32[2,4,64,128]{3,2,1,0:T(8,128)S(1)} collective-permute-done((f32[2,4,64,128]{3,2,1,0:T(8,128)S(1)}, f32[2,4,64,128]{3,2,1,0:T(8,128)S(1)}, u32[]{:S(2)}, u32[]{:S(2)}) %collective-permute-start.1) | collective-permute-done | bytes 262176 | tf_op jit(solution)/shard_map/ppermute | solution.py:319
  13.9 1.5 %collective-permute-done.refs_3_ = f32[2,4,64,128]{3,2,1,0:T(8,128)S(1)} collective-permute-done((f32[2,4,64,128]{3,2,1,0:T(8,128)S(1)}, f32[2,4,64,128]{3,2,1,0:T(8,128)S(1)}, u32[]{:S(2)}, u32[]{:S(2)}) %collective-permute-start) | collective-permute-done | bytes 262176 | tf_op jit(solution)/shard_map/ppermute | solution.py:318
  15.5 0.1 broadcast_select_fusion.2
  15.5 1.4 %collective-permute-start.3 = (f32[2,24,4,128]{3,2,1,0:T(4,128)S(1)}, f32[2,24,4,128]{3,2,1,0:T(4,128)S(1)}, u32[]{:S(2)}, u32[]{:S(2)}) collective-permute-start(f32[2,24,4,128]{3,2,1,0:T(4,128)S(1)} %get-tuple-element.47), channel_id=1, source_target_pairs={{0,112},{16,32},{32,16},{48,64},{64,48},{80,96},{96,80},{112,0},{1... | collective-permute-start | bytes 294920 | tf_op jit(solution)/shard_map/ppermute | solution.py:328
  16.9 0.4 collective-permute-start.2
  17.3 0.1 pad_add_fusion.refs_0_.at
  17.4 3.5 %collective-permute-done.3.refs_6_ = f32[2,24,4,128]{3,2,1,0:T(4,128)S(1)} collective-permute-done((f32[2,24,4,128]{3,2,1,0:T(4,128)S(1)}, f32[2,24,4,128]{3,2,1,0:T(4,128)S(1)}, u32[]{:S(2)}, u32[]{:S(2)}) %collective-permute-start.3) | collective-permute-done | bytes 98336 | tf_op jit(solution)/shard_map/ppermute | solution.py:328
  20.9 0.0 collective-permute-done.2.refs_5_
  20.9 7.6 %shard_map.28 = (f32[18,80,128]{2,1,0:T(8,128)S(1)}, f32[16,64,128]{2,1,0:T(8,128)S(1)}, f32[16,64,128]{2,1,0:T(8,128)S(1)}, f32[12,40,128]{2,1,0:T(8,128)S(1)},...) custom-call(s32[2]{0:T(128)S(1)} %pad_add_fusion.refs_0_.at, ...), custom_call_target="tpu_custom_call" | custom-call | tf_op jit(solution)/shard_map/pallas_call | solution.py:20
  28.5 0.0 collective-permute-start.4
  28.5 1.9 %collective-permute-start.5 = (f32[4,8,128]{2,1,0:T(8,128)S(1)}, f32[4,8,128]{2,1,0:T(8,128)S(1)}, u32[]{:S(2)}, u32[]{:S(2)}) collective-permute-start(f32[4,8,128]{2,1,0:T(8,128)S(1)} %get-tuple-element.25), channel_id=1, source_target_pairs={{0,112},{16,32},{32,16},{48,64},{64,48},{80,96},{96,80},{112,0},{1... | collective-permute-start | bytes 49160 | tf_op jit(solution)/shard_map/ppermute | solution.py:339
  30.4 0.0 collective-permute-done.4.ye.refs_7_
  30.4 2.5 %collective-permute-done.5.yo.refs_8_ = f32[4,8,128]{2,1,0:T(8,128)S(1)} collective-permute-done((f32[4,8,128]{2,1,0:T(8,128)S(1)}, f32[4,8,128]{2,1,0:T(8,128)S(1)}, u32[]{:S(2)}, u32[]{:S(2)}) %collective-permute-start.5) | collective-permute-done | bytes 16416 | tf_op jit(solution)/shard_map/ppermute | solution.py:339
  33.0 0.6 %shard_map.29 = (f32[4,32,128]{2,1,0:T(8,128)S(1)}, f32[5,32,128]{2,1,0:T(8,128)S(1)}, f32[5,32,128]{2,1,0:T(8,128)S(1)}, f32[1,32,128]{2,1,0:T(8,128)S(1)}, f32[1,32,128]{2,1,0:T(8,128)S(1)}) custom-call(s32[2]{0:T(128)S(1)} %pad_add_fusion.refs_0_.at, f32[4,16,128]{2,1,0:T(8,128)S(1)} %get-tuple-element.23.bc2, ...), custom_call_target="tpu_custom_call" | custom-call | tf_op jit(solution)/shard_map/pallas_call | solution.py:20
  33.6 0.4 collective-permute-start.6
  33.9 3.4 %collective-permute-start.7 = (f32[5,32,128]{2,1,0:T(8,128)S(1)}, f32[5,32,128]{2,1,0:T(8,128)S(1)}, u32[]{:S(2)}, u32[]{:S(2)}) collective-permute-start(f32[5,32,128]{2,1,0:T(8,128)S(1)} %get-tuple-element.28), channel_id=1, source_target_pairs={{0,15},{1,2},{2,1},{3,4},{4,3},{5,6},{6,5},{7,8},{8,7},{9,10},{10,... | collective-permute-start | bytes 245768 | tf_op jit(solution)/shard_map/ppermute | solution.py:347
  37.3 0.4 collective-permute-start.8
  37.7 2.2 %collective-permute-start.9 = (f32[1,32,128]{2,1,0:T(8,128)S(1)}, f32[1,32,128]{2,1,0:T(8,128)S(1)}, u32[]{:S(2)}, u32[]{:S(2)}) collective-permute-start(f32[1,32,128]{2,1,0:T(8,128)S(1)} %get-tuple-element.30), channel_id=1, source_target_pairs={{0,14},{1,15},{2,4},{3,5},{4,2},{5,3},{6,8},{7,9},{8,6},{9,7},{10,... | collective-permute-start | bytes 49160 | tf_op jit(solution)/shard_map/ppermute | solution.py:349
  39.9 2.8 %collective-permute-done.8.refs_11_ = f32[1,32,128]{2,1,0:T(8,128)S(1)} collective-permute-done((f32[1,32,128]{2,1,0:T(8,128)S(1)}, f32[1,32,128]{2,1,0:T(8,128)S(1)}, u32[]{:S(2)}, u32[]{:S(2)}) %collective-permute-start.8) | collective-permute-done | bytes 16416 | tf_op jit(solution)/shard_map/ppermute | solution.py:348
  42.8 2.3 %collective-permute-done.9.refs_12_ = f32[1,32,128]{2,1,0:T(8,128)S(1)} collective-permute-done((f32[1,32,128]{2,1,0:T(8,128)S(1)}, f32[1,32,128]{2,1,0:T(8,128)S(1)}, u32[]{:S(2)}, u32[]{:S(2)}) %collective-permute-start.9) | collective-permute-done | bytes 16416 | tf_op jit(solution)/shard_map/ppermute | solution.py:349
  45.1 0.0 collective-permute-done.6.refs_9_
  45.1 0.0 collective-permute-done.7.refs_10_
  45.1 6.8 %shard_map.30 = f32[16,64,128]{2,1,0:T(8,128)} custom-call(s32[2]{0:T(128)S(1)} %pad_add_fusion.refs_0_.at, f32[18,80,128]{2,1,0:T(8,128)S(1)} %get-tuple-element.18.refs_1_, f32[16,64,128]{2,1,0:T(8,128)S(1)} %get-tuple-element.19.refs_2_, f32[16,64,128]{2,1,0:T(8,128)S(1)} %get-tuple-element.20.refs_3_, f32[12,40,128]{2,1,0:T(8,128)S(1)} %get-tuple-element.21.e1.refs_4_, ...), custom_call_target="tpu_custom_call" | custom-call | tf_op jit(solution)/shard_map/pallas_call | solution.py:20
  (5 shorter events, 0.1 us)
Async XLA Ops:
  1.1 6.5 %copy-start = (f32[16,64,128]{2,1,0:T(8,128)S(1)}, f32[16,64,128]{2,1,0:T(8,128)}, u32[]{:S(2)}) copy-start(f32[16,64,128]{2,1,0:T(8,128)} %refs_1_.1) | copy-start | bytes 1572868
  1.1 6.5 %copy-start.1 = (f32[16,64,128]{2,1,0:T(8,128)S(1)}, f32[16,64,128]{2,1,0:T(8,128)}, u32[]{:S(2)}) copy-start(f32[16,64,128]{2,1,0:T(8,128)} %refs_2_.1) | copy-start | bytes 1572868
  1.2 12.7 %collective-permute-start.1 = (f32[2,4,64,128]{3,2,1,0:T(8,128)S(1)}, f32[2,4,64,128]{3,2,1,0:T(8,128)S(1)}, u32[]{:S(2)}, u32[]{:S(2)}) collective-permute-start(f32[2,4,64,128]{3,2,1,0:T(8,128)S(1)} %get-tuple-element.37), channel_id=1, source_target_pairs={{0,15},{1,2},{2,1},{3,4},{4,3},{5,6},{6,5},{7,8},{8,7},{9,10},{10,... | collective-permute-start | bytes 786440 | tf_op jit(solution)/shard_map/ppermute | solution.py:319
  7.6 7.8 %collective-permute-start = (f32[2,4,64,128]{3,2,1,0:T(8,128)S(1)}, f32[2,4,64,128]{3,2,1,0:T(8,128)S(1)}, u32[]{:S(2)}, u32[]{:S(2)}) collective-permute-start(f32[2,4,64,128]{3,2,1,0:T(8,128)S(1)} %get-tuple-element.38), channel_id=1, source_target_pairs={{0,1},{1,0},{2,3},{3,2},{4,5},{5,4},{6,7},{7,6},{8,9},{9,8},{10,11... | collective-permute-start | bytes 786440 | tf_op jit(solution)/shard_map/ppermute | solution.py:318
  15.5 5.3 %collective-permute-start.3 = (f32[2,24,4,128]{3,2,1,0:T(4,128)S(1)}, f32[2,24,4,128]{3,2,1,0:T(4,128)S(1)}, u32[]{:S(2)}, u32[]{:S(2)}) collective-permute-start(f32[2,24,4,128]{3,2,1,0:T(4,128)S(1)} %get-tuple-element.47), channel_id=1, source_target_pairs={{0,112},{16,32},{32,16},{48,64},{64,48},{80,96},{96,80},{112,0},{1... | collective-permute-start | bytes 294920 | tf_op jit(solution)/shard_map/ppermute | solution.py:328
  16.9 3.9 %collective-permute-start.2 = (f32[2,24,4,128]{3,2,1,0:T(4,128)S(1)}, f32[2,24,4,128]{3,2,1,0:T(4,128)S(1)}, u32[]{:S(2)}, u32[]{:S(2)}) collective-permute-start(f32[2,24,4,128]{3,2,1,0:T(4,128)S(1)} %get-tuple-element.48), channel_id=1, source_target_pairs={{0,16},{16,0},{32,48},{48,32},{64,80},{80,64},{96,112},{112,96},{1... | collective-permute-start | bytes 294920 | tf_op jit(solution)/shard_map/ppermute | solution.py:327
  28.5 1.9 %collective-permute-start.4 = (f32[4,8,128]{2,1,0:T(8,128)S(1)}, f32[4,8,128]{2,1,0:T(8,128)S(1)}, u32[]{:S(2)}, u32[]{:S(2)}) collective-permute-start(f32[4,8,128]{2,1,0:T(8,128)S(1)} %get-tuple-element.24), channel_id=1, source_target_pairs={{0,16},{16,0},{32,48},{48,32},{64,80},{80,64},{96,112},{112,96},{1... | collective-permute-start | bytes 49160 | tf_op jit(solution)/shard_map/ppermute | solution.py:338
  28.5 4.5 %collective-permute-start.5 = (f32[4,8,128]{2,1,0:T(8,128)S(1)}, f32[4,8,128]{2,1,0:T(8,128)S(1)}, u32[]{:S(2)}, u32[]{:S(2)}) collective-permute-start(f32[4,8,128]{2,1,0:T(8,128)S(1)} %get-tuple-element.25), channel_id=1, source_target_pairs={{0,112},{16,32},{32,16},{48,64},{64,48},{80,96},{96,80},{112,0},{1... | collective-permute-start | bytes 49160 | tf_op jit(solution)/shard_map/ppermute | solution.py:339
  33.6 11.5 %collective-permute-start.6 = (f32[5,32,128]{2,1,0:T(8,128)S(1)}, f32[5,32,128]{2,1,0:T(8,128)S(1)}, u32[]{:S(2)}, u32[]{:S(2)}) collective-permute-start(f32[5,32,128]{2,1,0:T(8,128)S(1)} %get-tuple-element.27), channel_id=1, source_target_pairs={{0,1},{1,0},{2,3},{3,2},{4,5},{5,4},{6,7},{7,6},{8,9},{9,8},{10,11... | collective-permute-start | bytes 245768 | tf_op jit(solution)/shard_map/ppermute | solution.py:346
  33.9 11.2 %collective-permute-start.7 = (f32[5,32,128]{2,1,0:T(8,128)S(1)}, f32[5,32,128]{2,1,0:T(8,128)S(1)}, u32[]{:S(2)}, u32[]{:S(2)}) collective-permute-start(f32[5,32,128]{2,1,0:T(8,128)S(1)} %get-tuple-element.28), channel_id=1, source_target_pairs={{0,15},{1,2},{2,1},{3,4},{4,3},{5,6},{6,5},{7,8},{8,7},{9,10},{10,... | collective-permute-start | bytes 245768 | tf_op jit(solution)/shard_map/ppermute | solution.py:347
  37.3 5.4 %collective-permute-start.8 = (f32[1,32,128]{2,1,0:T(8,128)S(1)}, f32[1,32,128]{2,1,0:T(8,128)S(1)}, u32[]{:S(2)}, u32[]{:S(2)}) collective-permute-start(f32[1,32,128]{2,1,0:T(8,128)S(1)} %get-tuple-element.29), channel_id=1, source_target_pairs={{0,2},{1,3},{2,0},{3,1},{4,6},{5,7},{6,4},{7,5},{8,10},{9,11},{10,... | collective-permute-start | bytes 49160 | tf_op jit(solution)/shard_map/ppermute | solution.py:348
  37.7 7.4 %collective-permute-start.9 = (f32[1,32,128]{2,1,0:T(8,128)S(1)}, f32[1,32,128]{2,1,0:T(8,128)S(1)}, u32[]{:S(2)}, u32[]{:S(2)}) collective-permute-start(f32[1,32,128]{2,1,0:T(8,128)S(1)} %get-tuple-element.30), channel_id=1, source_target_pairs={{0,14},{1,15},{2,4},{3,5},{4,2},{5,3},{6,8},{7,9},{8,6},{9,7},{10,... | collective-permute-start | bytes 49160 | tf_op jit(solution)/shard_map/ppermute | solution.py:349

commit v4 on v3

v4 whole, which is shorter than its diff:
```python
import jax
import jax.numpy as jnp
from jax import lax
from jax.experimental import pallas as pl
from jax.experimental.pallas import tpu as pltpu
from jax.sharding import PartitionSpec as P

OMEGA = 0.8
F32 = jnp.float32
WINDOW = 64
VM = pl.BlockSpec(memory_space=pltpu.VMEM)
SM = pl.BlockSpec(memory_space=pltpu.SMEM)


def shape(*dims):
    return jax.ShapeDtypeStruct(dims, F32)


def call(body, outs, scratch, *args):
    return pl.pallas_call(
        body,
        out_shape=outs,
        in_specs=[SM] + [VM] * (len(args) - 1),
        out_specs=tuple(VM for _ in outs),
        scratch_shapes=[pltpu.VMEM(s, F32) for s in scratch],
        compiler_params=pltpu.CompilerParams(vmem_limit_bytes=16 << 20),
    )(*args)


def iota(rows, axis):
    return lax.broadcasted_iota(jnp.int32, (rows, 128), axis)


def pick(kind):
    i, j = iota(128, 0), iota(128, 1)
    if kind == "pairs":
        at = (i >> 1) == j
    elif kind == "beside":
        at = (i >= 2 * j - 1) & (i <= 2 * j + 2)
    else:
        at = i == (j >> 1)
    return jnp.where(at, 1.0, 0.0).astype(jnp.bfloat16)


def halves(a):
    high = a.astype(jnp.bfloat16)
    return [high, (a - high.astype(F32)).astype(jnp.bfloat16)]


def dot(*terms):
    left = jnp.concatenate([h for a, _ in terms for h in halves(a)], axis=1)
    right = jnp.concatenate([m for _, m in terms for _ in (0, 1)], axis=0)
    return jnp.dot(left, right, preferred_element_type=F32)


def turn(v, by, axis):
    return pltpu.roll(v, by % v.shape[axis], axis)


def z_sum(v):
    lane = iota(v.shape[0], 1)
    below = jnp.where(lane == 0, 0.0, turn(v, 1, 1))
    return below + jnp.where(lane == 127, 0.0, turn(v, -1, 1))


def beside(ref, k, v, start, rows):
    return ref[k, pl.ds(start - 1, rows)] + ref[k, pl.ds(start + 1, rows)] + z_sum(v)


def windowed(ref, k, v, rows, at):
    below = jnp.where(at == 0, 0.0, ref[k, pl.ds(7, rows)])
    above = jnp.where(at == WINDOW - 1, 0.0, ref[k, pl.ds(9, rows)])
    return below + above + turn(v, 1, 1) + turn(v, -1, 1)


def inside(at, size):
    return (at >= 0) & (at < size)


def every_other(ref, k, start, rows):
    return ref[k, pl.ds(start, rows, stride=2), :]


def row_pairs(ref, k, start, rows):
    return every_other(ref, k, start, rows) + every_other(ref, k, start + 1, rows)


def gather(both, rest, k, at_both, at_rest, rows, at=None):
    below, above = every_other(both, k, at_both - 1, rows), every_other(both, k, at_both + 2, rows)
    if at is not None:
        below = jnp.where(at == 0, 0.0, below)
        above = jnp.where(at == WINDOW // 2 - 1, 0.0, above)
    own = row_pairs(both, k, at_both, rows)
    return row_pairs(rest, k, at_rest, rows) + own + below + above, own


def down_kernel(
    blocks, aggs,
    at, b, c, xe, xo, ye, yo,
    p0, vown, wown, e1, w1, bc2, se, so,
    v, w, q, bx, cx, own1, rest1, b1, c1, own2, rest2,
):
    bi, ai = at[0], at[1]
    x_even, y_even = (bi & 1) == 0, (ai & 1) == 0
    y_lo = jnp.where(ai > 0, 1.0, 0.0)
    y_hi = jnp.where(ai < aggs - 1, 1.0, 0.0)

    def put(p, rows, bb, cc, scale):
        ww = scale / (6.0 + cc)
        vv = ww * bb
        w[p, rows], v[p, rows], bx[p, rows], cx[p, rows] = ww, vv, bb, cc
        return vv, ww

    def plane(p, bb, cc, scale):
        out = put(p, pl.ds(16, 64), bb, cc, scale)
        lo = [jnp.where(y_even, yo[k, p], ye[k, p]) for k in (0, 1)]
        hi = [jnp.where(y_even, ye[k, p], yo[k, p]) for k in (0, 1)]
        put(p, pl.ds(12, 4), *lo, scale * y_lo)
        put(p, pl.ds(80, 4), *hi, scale * y_hi)
        return out

    def own(k, carry):
        for i in (2 * k, 2 * k + 1):
            vown[i], wown[i] = plane(i + 4, b[i], c[i], OMEGA)
        return carry

    def edge(i, carry):
        lo = [jnp.where(x_even, xo[k, i], xe[k, i]) for k in (0, 1)]
        hi = [jnp.where(x_even, xe[k, i], xo[k, i]) for k in (0, 1)]
        plane(i, *lo, jnp.where(bi > 0, OMEGA, 0.0))
        plane(i + 20, *hi, jnp.where(bi < blocks - 1, OMEGA, 0.0))
        return carry

    lax.fori_loop(0, 8, own, 0)
    lax.fori_loop(0, 4, edge, 0)
    rows = pl.ds(8, 80)

    def smooth(k, carry):
        for p in (1 + 2 * k, 2 + 2 * k):
            vv = v[p, rows]
            near = v[p - 1, rows] + v[p + 1, rows] + beside(v, p, vv, 8, 80)
            qq = 0.4 * vv + w[p, rows] * near
            q[p, rows] = qq
            p0[p] = qq + OMEGA * vv
        return carry

    lax.fori_loop(0, 11, smooth, 0)

    pairs, sides = pick("pairs"), pick("beside")
    row1 = ai * 32 - 4 + iota(40, 0)
    keep1 = inside(row1, 32 * aggs) & (iota(40, 1) < 64)

    def coarse(k, carry):
        p = 2 + 2 * k
        both = q[p, rows] + q[p + 1, rows]
        own1[k, pl.ds(8, 80)] = both
        rest1[k] = 0.04 * (bx[p, rows] + bx[p + 1, rows]) + (both + (q[p - 1, rows] + q[p + 2, rows]))
        cx[k, rows] = cx[p, rows] + cx[p + 1, rows]
        return carry

    lax.fori_loop(0, 10, coarse, 0)

    def coarse_dots(k, carry):
        n = 2 * k
        ends, mids, sums = [], [], []
        for i in (n, n + 1):
            end, mid = gather(own1, rest1, i, 8, 0, 40)
            ends.append(end)
            mids.append(mid)
            sums.append(row_pairs(cx, i, 8, 40))
        bb2 = dot((jnp.concatenate(ends, axis=0), pairs), (jnp.concatenate(mids, axis=0), sides))
        cc2 = dot((jnp.concatenate(sums, axis=0), pairs))
        for i in (0, 1):
            bb, cc = 0.5 * bb2[40 * i : 40 * i + 40], 0.5 * cc2[40 * i : 40 * i + 40]
            ok = keep1 & inside(bi * 8 + n + i - 1, 8 * blocks)
            ww = jnp.where(ok, OMEGA / (6.0 + cc), 0.0)
            b1[n + i], c1[n + i] = bb, cc
            w1[n + i + 1] = ww
            e1[n + i + 1] = jnp.where(ok, ww * bb, 0.0)
        return carry

    lax.fori_loop(0, 5, coarse_dots, 0)

    at2 = (ai * 16 + iota(16, 0)) & (WINDOW // 2 - 1)
    lane16 = iota(16, 1)
    ends, mids, sums = [], [], []
    for k in range(4):
        p = 1 + 2 * k
        both = e1[p + 1] + e1[p + 2]
        own2[k] = both
        rest2[k] = 0.2 * (b1[p] + b1[p + 1]) + (both + (e1[p] + e1[p + 3]))
        end, mid = gather(own2, rest2, k, 4, 4, 16, at2)
        ends.append(end)
        mids.append(mid)
        sums.append(row_pairs(c1, p, 4, 16) + row_pairs(c1, p + 1, 4, 16))
    bb2 = dot((jnp.concatenate(ends, axis=0), pairs), (jnp.concatenate(mids, axis=0), sides))
    cc2 = dot((jnp.concatenate(sums, axis=0), pairs))
    for k in range(4):
        bb = jnp.where(lane16 < 32, 0.5 * bb2[16 * k : 16 * k + 16], 0.0)
        cc = jnp.where(lane16 < 32, 0.5 * cc2[16 * k : 16 * k + 16], 0.0)
        mix = bb + turn(cc, 32, 1)
        bc2[k] = mix
        for ref, lo_side in ((se, jnp.logical_not(y_even)), (so, y_even)):
            ref[k, 0:5] = jnp.where(lo_side, mix[0:5], mix[11:16])
            for j in (0, 1):
                n = 2 + 2 * k + j
                ref[k, 5 + j : 6 + j] = jnp.where(lo_side, e1[n, 5:6], e1[n, 34:35])
            ref[k, 7:8] = jnp.zeros((1, 128), F32)


def join_kernel(at, bc2, ye, yo, e1, wide, se, so, sf, sg):
    bi, ai = at[0], at[1]
    x_even, y_even = (bi & 1) == 0, (ai & 1) == 0
    low_pair = (bi & 2) == 0
    for k in range(4):
        wide[k] = jnp.zeros((32, 128), F32)
        wide[k, 3:8] = jnp.where(y_even, yo[k, 0:5], ye[k, 0:5])
        wide[k, 8:24] = bc2[k]
        wide[k, 24:29] = jnp.where(y_even, ye[k, 0:5], yo[k, 0:5])
        se[k] = wide[k]
        so[k] = wide[k]
    up, down = e1[8, 4:36], e1[3, 4:36]
    se[4] = jnp.where(x_even, up, down)
    so[4] = jnp.where(x_even, down, up)
    sf[0] = jnp.where(low_pair, wide[3], wide[0])
    sg[0] = jnp.where(low_pair, wide[0], wide[3])


def up_kernel(
    blocks, aggs,
    at, p0, vown, wown, e1in, w1, wide, ye, yo, xe, xo, xf, xg,
    out,
    bc, e2, w2, b2, c2, own2, rest2, m2, t2, e1, m1, mf,
):
    bi, ai = at[0], at[1]
    x_even, y_even = (bi & 1) == 0, (ai & 1) == 0
    low_pair = (bi & 2) == 0
    pairs, sides, copies = pick("pairs"), pick("beside"), pick("copies")

    bc[0] = jnp.where(low_pair, xg[0], xf[0])
    bc[13] = jnp.where(low_pair, xf[0], xg[0])
    for k in range(4):
        bc[1 + k] = jnp.where(x_even, xo[k], xe[k])
        bc[5 + k] = wide[k]
        bc[9 + k] = jnp.where(x_even, xe[k], xo[k])

    row2 = ai * 16 - 8 + iota(32, 0)
    lane2 = iota(32, 1) < 32
    keep2 = inside(row2, 16 * aggs) & lane2
    for k in range(14):
        mix = bc[k]
        bb = jnp.where(lane2, mix, 0.0)
        cc = jnp.where(lane2, turn(mix, -32, 1), 0.0)
        ww = jnp.where(keep2 & inside(bi * 4 + k - 5, 4 * blocks), OMEGA / (6.0 + cc), 0.0)
        b2[k], c2[k], w2[k], e2[k] = bb, cc, ww, ww * bb

    row3 = ai * 8 - 4 + iota(16, 0)
    at3 = row3 & (WINDOW // 2 - 1)
    ends, mids, sums = [], [], []
    for j in range(6):
        k = 1 + 2 * j
        both = e2[k] + e2[k + 1]
        own2[j, 8:40] = both
        rest2[j] = 0.2 * (b2[k] + b2[k + 1]) + (both + (e2[k - 1] + e2[k + 2]))
        end, mid = gather(own2, rest2, j, 8, 0, 16, at3)
        ends.append(end)
        mids.append(mid)
        sums.append(row_pairs(c2, k, 0, 16) + row_pairs(c2, k + 1, 0, 16))
    bb3 = dot((jnp.concatenate(ends, axis=0), pairs), (jnp.concatenate(mids, axis=0), sides))
    cc3 = dot((jnp.concatenate(sums, axis=0), pairs))
    keep3 = inside(row3, 8 * aggs) & (iota(16, 1) < 16)
    e3, w3 = [], []
    for j in range(6):
        bb, cc = 0.5 * bb3[16 * j : 16 * j + 16], 0.5 * cc3[16 * j : 16 * j + 16]
        ok = keep3 & inside(bi * 2 + j - 2, 2 * blocks)
        ww = jnp.where(ok, OMEGA / (6.0 + cc), 0.0)
        w3.append(ww)
        e3.append(jnp.where(ok, ww * bb, 0.0))
    solved = []
    for j in range(1, 5):
        v = e3[j]
        near = e3[j - 1] + e3[j + 1] + turn(v, 1, 0) + turn(v, -1, 0) + turn(v, 1, 1) + turn(v, -1, 1)
        solved.append(1.2 * v + w3[j] * near)
    wider = dot((jnp.concatenate(solved, axis=0), copies))
    for k in range(3, 11):
        j = (k - 3) // 2
        for r in (0, 1):
            m2[k, pl.ds(8 + r, 16, stride=2), :] = every_other(e2, k, r, 16) + wider[16 * j : 16 * j + 16]
    at2 = row2 & (WINDOW - 1)
    rows = pl.ds(8, 32)
    solved = []
    for k in range(4, 10):
        v = m2[k, rows]
        near = m2[k - 1, rows] + m2[k + 1, rows] + windowed(m2, k, v, 32, at2)
        solved.append(0.2 * v + e2[k] + w2[k] * near)
    wider = dot((jnp.concatenate(solved, axis=0), copies))
    for k in range(6):
        t2[k] = wider[32 * k : 32 * k + 32]

    for k in range(1, 11):
        e1[k] = e1in[k]
    for k in (0, 11):
        e1[k] = jnp.zeros((40, 128), F32)
    e1[0, 4:36] = jnp.where(x_even, xo[4], xe[4])
    e1[11, 4:36] = jnp.where(x_even, xe[4], xo[4])
    for n in range(8):
        k, j = n // 2, n % 2
        mine, other = ye[k, 5 + j : 6 + j], yo[k, 5 + j : 6 + j]
        e1[n + 2, 2:3] = jnp.where(y_even, other, mine)
        e1[n + 2, 37:38] = jnp.where(y_even, mine, other)
    for k in range(12):
        for r in (0, 1):
            m1[k, pl.ds(8 + r, 20, stride=2), :] = every_other(e1, k, r, 20) + t2[k // 2, 6:26]
    at1 = (ai * 32 - 4 + iota(40, 0)) & (WINDOW - 1)

    def fine(n, carry):
        rows = pl.ds(8, 40)
        solved = []
        for k in (2 * n, 2 * n + 1):
            v = m1[k + 1, rows]
            near = m1[k, rows] + m1[k + 2, rows] + windowed(m1, k + 1, v, 40, at1)
            solved.append(0.2 * v + e1[k + 1] + w1[k + 1] * near)
        wider = dot((jnp.concatenate(solved, axis=0), copies))
        for i in (0, 1):
            for j in (0, 1):
                k = 4 * n + 2 * i + j
                for r in (0, 1):
                    old = p0[k + 2, pl.ds(r, 40, stride=2), :]
                    mf[k, pl.ds(8 + r, 40, stride=2), :] = old + wider[40 * i : 40 * i + 40]
        return carry

    lax.fori_loop(0, 5, fine, 0)

    def last(n, carry):
        rows = pl.ds(16, 64)
        for k in (2 * n, 2 * n + 1):
            m = mf[k + 2, rows]
            near = mf[k + 1, rows] + mf[k + 3, rows] + beside(mf, k + 2, m, 16, 64)
            out[k] = 0.2 * m + vown[k] + wown[k] * near
        return carry

    lax.fori_loop(0, 8, last, 0)


def swaps(size, apart):
    inner, outer = [], []
    for i in range(size):
        inner.append((i, i ^ apart))
        outer.append((i, (i + apart) % size if i & apart else (i - apart) % size))
    return inner, outer


def shards(b, c):
    blocks, aggs = lax.axis_size("blk"), lax.axis_size("agg")
    bi, ai = lax.axis_index("blk"), lax.axis_index("agg")
    at = jnp.stack([bi, ai]).astype(jnp.int32)
    x_even, y_even = (bi & 1) == 0, (ai & 1) == 0
    near_in, near_out = swaps(blocks, 1)
    far_in, far_out = swaps(blocks, 2)
    side_in, side_out = swaps(aggs, 1)

    first = jnp.stack([b[:4], c[:4]])
    last = jnp.stack([b[12:], c[12:]])
    xe = lax.ppermute(jnp.where(x_even, last, first), "blk", near_in)
    xo = lax.ppermute(jnp.where(x_even, first, last), "blk", near_out)
    lo, hi = jnp.where(x_even, xo, xe), jnp.where(x_even, xe, xo)

    def rows(cut):
        own = jnp.stack([b[:, cut], c[:, cut]])
        return jnp.concatenate([lo[:, :, cut], own, hi[:, :, cut]], axis=1)

    first, last = rows(slice(0, 4)), rows(slice(60, 64))
    ye = lax.ppermute(jnp.where(y_even, last, first), "agg", side_in)
    yo = lax.ppermute(jnp.where(y_even, first, last), "agg", side_out)

    big, mid = (24, 96, 128), (12, 40, 128)
    p0, vown, wown, e1, w1, bc2, se, so = call(
        lambda *refs: down_kernel(blocks, aggs, *refs),
        (shape(24, 80, 128), shape(16, 64, 128), shape(16, 64, 128), shape(*mid), shape(*mid),
         shape(4, 16, 128), shape(4, 8, 128), shape(4, 8, 128)),
        [big] * 5 + [(10, 96, 128), (10, 80, 128), mid, mid, (4, 40, 128), (4, 40, 128)],
        at, b, c, xe, xo, ye, yo,
    )
    ye = lax.ppermute(se, "agg", side_in)
    yo = lax.ppermute(so, "agg", side_out)
    wide, se, so, sf, sg = call(
        join_kernel,
        (shape(4, 32, 128), shape(5, 32, 128), shape(5, 32, 128), shape(1, 32, 128), shape(1, 32, 128)),
        [],
        at, bc2, ye, yo, e1,
    )
    xe = lax.ppermute(se, "blk", near_in)
    xo = lax.ppermute(so, "blk", near_out)
    xf = lax.ppermute(sf, "blk", far_in)
    xg = lax.ppermute(sg, "blk", far_out)
    small = (14, 32, 128)
    (out,) = call(
        lambda *refs: up_kernel(blocks, aggs, *refs),
        (shape(16, 64, 128),),
        [small] * 5 + [(6, 48, 128), (6, 32, 128), (14, 48, 128), (6, 32, 128), mid, (12, 56, 128), (20, 96, 128)],
        at, p0, vown, wown, e1, w1, wide, ye, yo, xe, xo, xf, xg,
    )
    return out


def solution(mesh):
    placed = (P("blk", "agg", None), P("blk", "agg", None))
    return jax.shard_map(
        shards, mesh=mesh, in_specs=placed, out_specs=P("blk", "agg", None), check_vma=False
    )
```

time: 52 us -> 45.5 us (0.88)
  Pallas kernels: 14.9 us -> 8.36 us
    pallas_call x3, Pallas kernels: 14.9 us -> 8.36 us  [call(): pl.pallas_call(body, out_shape=outs, in_specs=[SM] + [VM] * (len(args) -...]
where the time goes in v4:
time: 45.5 us; the launch traced here: 45.3 us
  waiting for transfers between devices  18.9 us (42%)
  starting transfers between devices  16.5 us (36%)
  Pallas kernels  8.36 us (18%)
  local copies, waits for them, and re-layouts  1.18 us (3%)
    pallas_call x3, Pallas kernels, call(): pl.pallas_call(body, out_shape=outs, in_specs=[SM] + [VM] * (len(args) -...  8.36 us
    ppermute x1, starting transfers between devices, shards(): xo = lax.ppermute(jnp.where(x_even, first, last), 'blk', near_out)  6.42 us
    ppermute x1, waiting for transfers between devices, shards(): xo = lax.ppermute(jnp.where(x_even, first, last), 'blk', near_out)  6.26 us
    ppermute x1, waiting for transfers between devices, shards(): yo = lax.ppermute(jnp.where(y_even, first, last), 'agg', side_out)  3.48 us
    ppermute x1, starting transfers between devices, shards(): xo = lax.ppermute(so, 'blk', near_out)  3.41 us
    ppermute x1, waiting for transfers between devices, shards(): xf = lax.ppermute(sf, 'blk', far_in)  2.83 us
    ppermute x1, waiting for transfers between devices, shards(): yo = lax.ppermute(so, 'agg', side_out)  2.55 us
    ppermute x1, waiting for transfers between devices, shards(): xg = lax.ppermute(sg, 'blk', far_out)  2.33 us
  transfers between devices with their start and end apart: 10, of which 6 were waited for; matrix products, arithmetic and copies ran while one was open for 0% of the time, Pallas kernels for 0%

profile of v4, /device:TPU:0, one launch (start us, length us, event | category | flops | bytes accessed | tf_op | source)
XLA Modules:
  0.0 45.3 jit_solution(8212844941239643909)
XLA Ops:
  0.0 1.1 %slice_bitcast_fusion.2 = (f32[1,4,64,128]{3,2,1,0:T(8,128)S(1)}, f32[1,4,64,128]{3,2,1,0:T(8,128)S(1)}, f32[1,4,64,128]{3,2,1,0:T(8,128)S(1)}, f32[1,4,64,128]{3,2,1,0:T(8,128)S(1)}) fusion(f32[16,64,128]{2,1,0:T(8,128)} %refs_2_.1, f32[16,64,128]{2,1,0:T(8,128)} %refs_1_.1), kind=kLoop, calls=%fused_computation.6 | loop fusion | bytes 1048576 | tf_op jit(solution)/shard_map/stack | solution.py:363
  1.1 0.0 copy-start
  1.1 0.0 copy-start.1
  1.2 6.4 %collective-permute-start.1 = (f32[2,4,64,128]{3,2,1,0:T(8,128)S(1)}, f32[2,4,64,128]{3,2,1,0:T(8,128)S(1)}, u32[]{:S(2)}, u32[]{:S(2)}) collective-permute-start(f32[2,4,64,128]{3,2,1,0:T(8,128)S(1)} %get-tuple-element.37), channel_id=1, source_target_pairs={{0,15},{1,2},{2,1},{3,4},{4,3},{5,6},{6,5},{7,8},{8,7},{9,10},{10,... | collective-permute-start | bytes 786440 | tf_op jit(solution)/shard_map/ppermute | solution.py:365
  7.6 0.0 collective-permute-start
  7.6 0.0 copy-done
  7.6 0.0 copy-done.1
  7.7 6.3 %collective-permute-done.1.refs_4_ = f32[2,4,64,128]{3,2,1,0:T(8,128)S(1)} collective-permute-done((f32[2,4,64,128]{3,2,1,0:T(8,128)S(1)}, f32[2,4,64,128]{3,2,1,0:T(8,128)S(1)}, u32[]{:S(2)}, u32[]{:S(2)}) %collective-permute-start.1) | collective-permute-done | bytes 262176 | tf_op jit(solution)/shard_map/ppermute | solution.py:365
  13.9 1.5 %collective-permute-done.refs_3_ = f32[2,4,64,128]{3,2,1,0:T(8,128)S(1)} collective-permute-done((f32[2,4,64,128]{3,2,1,0:T(8,128)S(1)}, f32[2,4,64,128]{3,2,1,0:T(8,128)S(1)}, u32[]{:S(2)}, u32[]{:S(2)}) %collective-permute-start) | collective-permute-done | bytes 262176 | tf_op jit(solution)/shard_map/ppermute | solution.py:364
  15.5 0.1 broadcast_select_fusion.2
  15.5 1.4 %collective-permute-start.3 = (f32[2,24,4,128]{3,2,1,0:T(4,128)S(1)}, f32[2,24,4,128]{3,2,1,0:T(4,128)S(1)}, u32[]{:S(2)}, u32[]{:S(2)}) collective-permute-start(f32[2,24,4,128]{3,2,1,0:T(4,128)S(1)} %get-tuple-element.47), channel_id=1, source_target_pairs={{0,112},{16,32},{32,16},{48,64},{64,48},{80,96},{96,80},{112,0},{1... | collective-permute-start | bytes 294920 | tf_op jit(solution)/shard_map/ppermute | solution.py:374
  16.9 0.4 collective-permute-start.2
  17.3 0.1 pad_add_fusion.refs_0_.at
  17.4 3.5 %collective-permute-done.3.refs_6_ = f32[2,24,4,128]{3,2,1,0:T(4,128)S(1)} collective-permute-done((f32[2,24,4,128]{3,2,1,0:T(4,128)S(1)}, f32[2,24,4,128]{3,2,1,0:T(4,128)S(1)}, u32[]{:S(2)}, u32[]{:S(2)}) %collective-permute-start.3) | collective-permute-done | bytes 98336 | tf_op jit(solution)/shard_map/ppermute | solution.py:374
  20.9 0.0 collective-permute-done.2.refs_5_
  20.9 3.7 %shard_map.28 = (f32[24,80,128]{2,1,0:T(8,128)S(1)}, f32[16,64,128]{2,1,0:T(8,128)S(1)}, f32[16,64,128]{2,1,0:T(8,128)S(1)}, f32[12,40,128]{2,1,0:T(8,128)S(1)},...) custom-call(s32[2]{0:T(128)S(1)} %pad_add_fusion.refs_0_.at, ...), custom_call_target="tpu_custom_call" | custom-call | tf_op jit(solution)/shard_map/pallas_call | solution.py:20
  24.6 0.1 collective-permute-start.4
  24.7 1.9 %collective-permute-start.5 = (f32[4,8,128]{2,1,0:T(8,128)S(1)}, f32[4,8,128]{2,1,0:T(8,128)S(1)}, u32[]{:S(2)}, u32[]{:S(2)}) collective-permute-start(f32[4,8,128]{2,1,0:T(8,128)S(1)} %get-tuple-element.25), channel_id=1, source_target_pairs={{0,112},{16,32},{32,16},{48,64},{64,48},{80,96},{96,80},{112,0},{1... | collective-permute-start | bytes 49160 | tf_op jit(solution)/shard_map/ppermute | solution.py:385
  26.6 0.0 collective-permute-done.4.ye.refs_7_
  26.6 2.5 %collective-permute-done.5.yo.refs_8_ = f32[4,8,128]{2,1,0:T(8,128)S(1)} collective-permute-done((f32[4,8,128]{2,1,0:T(8,128)S(1)}, f32[4,8,128]{2,1,0:T(8,128)S(1)}, u32[]{:S(2)}, u32[]{:S(2)}) %collective-permute-start.5) | collective-permute-done | bytes 16416 | tf_op jit(solution)/shard_map/ppermute | solution.py:385
  29.1 0.6 %shard_map.29 = (f32[4,32,128]{2,1,0:T(8,128)S(1)}, f32[5,32,128]{2,1,0:T(8,128)S(1)}, f32[5,32,128]{2,1,0:T(8,128)S(1)}, f32[1,32,128]{2,1,0:T(8,128)S(1)}, f32[1,32,128]{2,1,0:T(8,128)S(1)}) custom-call(s32[2]{0:T(128)S(1)} %pad_add_fusion.refs_0_.at, f32[4,16,128]{2,1,0:T(8,128)S(1)} %get-tuple-element.23.bc2, ...), custom_call_target="tpu_custom_call" | custom-call | tf_op jit(solution)/shard_map/pallas_call | solution.py:20
  29.7 0.4 collective-permute-start.6
  30.0 3.4 %collective-permute-start.7 = (f32[5,32,128]{2,1,0:T(8,128)S(1)}, f32[5,32,128]{2,1,0:T(8,128)S(1)}, u32[]{:S(2)}, u32[]{:S(2)}) collective-permute-start(f32[5,32,128]{2,1,0:T(8,128)S(1)} %get-tuple-element.28), channel_id=1, source_target_pairs={{0,15},{1,2},{2,1},{3,4},{4,3},{5,6},{6,5},{7,8},{8,7},{9,10},{10,... | collective-permute-start | bytes 245768 | tf_op jit(solution)/shard_map/ppermute | solution.py:393
  33.5 0.4 collective-permute-start.8
  33.9 2.2 %collective-permute-start.9 = (f32[1,32,128]{2,1,0:T(8,128)S(1)}, f32[1,32,128]{2,1,0:T(8,128)S(1)}, u32[]{:S(2)}, u32[]{:S(2)}) collective-permute-start(f32[1,32,128]{2,1,0:T(8,128)S(1)} %get-tuple-element.30), channel_id=1, source_target_pairs={{0,14},{1,15},{2,4},{3,5},{4,2},{5,3},{6,8},{7,9},{8,6},{9,7},{10,... | collective-permute-start | bytes 49160 | tf_op jit(solution)/shard_map/ppermute | solution.py:395
  36.0 2.8 %collective-permute-done.8.refs_11_ = f32[1,32,128]{2,1,0:T(8,128)S(1)} collective-permute-done((f32[1,32,128]{2,1,0:T(8,128)S(1)}, f32[1,32,128]{2,1,0:T(8,128)S(1)}, u32[]{:S(2)}, u32[]{:S(2)}) %collective-permute-start.8) | collective-permute-done | bytes 16416 | tf_op jit(solution)/shard_map/ppermute | solution.py:394
  38.9 2.3 %collective-permute-done.9.refs_12_ = f32[1,32,128]{2,1,0:T(8,128)S(1)} collective-permute-done((f32[1,32,128]{2,1,0:T(8,128)S(1)}, f32[1,32,128]{2,1,0:T(8,128)S(1)}, u32[]{:S(2)}, u32[]{:S(2)}) %collective-permute-start.9) | collective-permute-done | bytes 16416 | tf_op jit(solution)/shard_map/ppermute | solution.py:395
  41.2 0.0 collective-permute-done.6.refs_9_
  41.2 0.0 collective-permute-done.7.refs_10_
  41.2 4.1 %shard_map.30 = f32[16,64,128]{2,1,0:T(8,128)} custom-call(s32[2]{0:T(128)S(1)} %pad_add_fusion.refs_0_.at, f32[24,80,128]{2,1,0:T(8,128)S(1)} %get-tuple-element.18.refs_1_, f32[16,64,128]{2,1,0:T(8,128)S(1)} %get-tuple-element.19.refs_2_, f32[16,64,128]{2,1,0:T(8,128)S(1)} %get-tuple-element.20.refs_3_, f32[12,40,128]{2,1,0:T(8,128)S(1)} %get-tuple-element.21.e1.refs_4_, ...), custom_call_target="tpu_custom_call" | custom-call | tf_op jit(solution)/shard_map/pallas_call | solution.py:20
  (5 shorter events, 0.1 us)
Async XLA Ops:
  1.1 6.5 %copy-start = (f32[16,64,128]{2,1,0:T(8,128)S(1)}, f32[16,64,128]{2,1,0:T(8,128)}, u32[]{:S(2)}) copy-start(f32[16,64,128]{2,1,0:T(8,128)} %refs_1_.1) | copy-start | bytes 1572868
  1.1 6.5 %copy-start.1 = (f32[16,64,128]{2,1,0:T(8,128)S(1)}, f32[16,64,128]{2,1,0:T(8,128)}, u32[]{:S(2)}) copy-start(f32[16,64,128]{2,1,0:T(8,128)} %refs_2_.1) | copy-start | bytes 1572868
  1.2 12.7 %collective-permute-start.1 = (f32[2,4,64,128]{3,2,1,0:T(8,128)S(1)}, f32[2,4,64,128]{3,2,1,0:T(8,128)S(1)}, u32[]{:S(2)}, u32[]{:S(2)}) collective-permute-start(f32[2,4,64,128]{3,2,1,0:T(8,128)S(1)} %get-tuple-element.37), channel_id=1, source_target_pairs={{0,15},{1,2},{2,1},{3,4},{4,3},{5,6},{6,5},{7,8},{8,7},{9,10},{10,... | collective-permute-start | bytes 786440 | tf_op jit(solution)/shard_map/ppermute | solution.py:365
  7.6 7.8 %collective-permute-start = (f32[2,4,64,128]{3,2,1,0:T(8,128)S(1)}, f32[2,4,64,128]{3,2,1,0:T(8,128)S(1)}, u32[]{:S(2)}, u32[]{:S(2)}) collective-permute-start(f32[2,4,64,128]{3,2,1,0:T(8,128)S(1)} %get-tuple-element.38), channel_id=1, source_target_pairs={{0,1},{1,0},{2,3},{3,2},{4,5},{5,4},{6,7},{7,6},{8,9},{9,8},{10,11... | collective-permute-start | bytes 786440 | tf_op jit(solution)/shard_map/ppermute | solution.py:364
  15.5 5.3 %collective-permute-start.3 = (f32[2,24,4,128]{3,2,1,0:T(4,128)S(1)}, f32[2,24,4,128]{3,2,1,0:T(4,128)S(1)}, u32[]{:S(2)}, u32[]{:S(2)}) collective-permute-start(f32[2,24,4,128]{3,2,1,0:T(4,128)S(1)} %get-tuple-element.47), channel_id=1, source_target_pairs={{0,112},{16,32},{32,16},{48,64},{64,48},{80,96},{96,80},{112,0},{1... | collective-permute-start | bytes 294920 | tf_op jit(solution)/shard_map/ppermute | solution.py:374
  16.9 3.9 %collective-permute-start.2 = (f32[2,24,4,128]{3,2,1,0:T(4,128)S(1)}, f32[2,24,4,128]{3,2,1,0:T(4,128)S(1)}, u32[]{:S(2)}, u32[]{:S(2)}) collective-permute-start(f32[2,24,4,128]{3,2,1,0:T(4,128)S(1)} %get-tuple-element.48), channel_id=1, source_target_pairs={{0,16},{16,0},{32,48},{48,32},{64,80},{80,64},{96,112},{112,96},{1... | collective-permute-start | bytes 294920 | tf_op jit(solution)/shard_map/ppermute | solution.py:373
  24.6 2.0 %collective-permute-start.4 = (f32[4,8,128]{2,1,0:T(8,128)S(1)}, f32[4,8,128]{2,1,0:T(8,128)S(1)}, u32[]{:S(2)}, u32[]{:S(2)}) collective-permute-start(f32[4,8,128]{2,1,0:T(8,128)S(1)} %get-tuple-element.24), channel_id=1, source_target_pairs={{0,16},{16,0},{32,48},{48,32},{64,80},{80,64},{96,112},{112,96},{1... | collective-permute-start | bytes 49160 | tf_op jit(solution)/shard_map/ppermute | solution.py:384
  24.7 4.5 %collective-permute-start.5 = (f32[4,8,128]{2,1,0:T(8,128)S(1)}, f32[4,8,128]{2,1,0:T(8,128)S(1)}, u32[]{:S(2)}, u32[]{:S(2)}) collective-permute-start(f32[4,8,128]{2,1,0:T(8,128)S(1)} %get-tuple-element.25), channel_id=1, source_target_pairs={{0,112},{16,32},{32,16},{48,64},{64,48},{80,96},{96,80},{112,0},{1... | collective-permute-start | bytes 49160 | tf_op jit(solution)/shard_map/ppermute | solution.py:385
  29.7 11.5 %collective-permute-start.6 = (f32[5,32,128]{2,1,0:T(8,128)S(1)}, f32[5,32,128]{2,1,0:T(8,128)S(1)}, u32[]{:S(2)}, u32[]{:S(2)}) collective-permute-start(f32[5,32,128]{2,1,0:T(8,128)S(1)} %get-tuple-element.27), channel_id=1, source_target_pairs={{0,1},{1,0},{2,3},{3,2},{4,5},{5,4},{6,7},{7,6},{8,9},{9,8},{10,11... | collective-permute-start | bytes 245768 | tf_op jit(solution)/shard_map/ppermute | solution.py:392
  30.0 11.2 %collective-permute-start.7 = (f32[5,32,128]{2,1,0:T(8,128)S(1)}, f32[5,32,128]{2,1,0:T(8,128)S(1)}, u32[]{:S(2)}, u32[]{:S(2)}) collective-permute-start(f32[5,32,128]{2,1,0:T(8,128)S(1)} %get-tuple-element.28), channel_id=1, source_target_pairs={{0,15},{1,2},{2,1},{3,4},{4,3},{5,6},{6,5},{7,8},{8,7},{9,10},{10,... | collective-permute-start | bytes 245768 | tf_op jit(solution)/shard_map/ppermute | solution.py:393
  33.5 5.4 %collective-permute-start.8 = (f32[1,32,128]{2,1,0:T(8,128)S(1)}, f32[1,32,128]{2,1,0:T(8,128)S(1)}, u32[]{:S(2)}, u32[]{:S(2)}) collective-permute-start(f32[1,32,128]{2,1,0:T(8,128)S(1)} %get-tuple-element.29), channel_id=1, source_target_pairs={{0,2},{1,3},{2,0},{3,1},{4,6},{5,7},{6,4},{7,5},{8,10},{9,11},{10,... | collective-permute-start | bytes 49160 | tf_op jit(solution)/shard_map/ppermute | solution.py:394
  33.9 7.4 %collective-permute-start.9 = (f32[1,32,128]{2,1,0:T(8,128)S(1)}, f32[1,32,128]{2,1,0:T(8,128)S(1)}, u32[]{:S(2)}, u32[]{:S(2)}) collective-permute-start(f32[1,32,128]{2,1,0:T(8,128)S(1)} %get-tuple-element.30), channel_id=1, source_target_pairs={{0,14},{1,15},{2,4},{3,5},{4,2},{5,3},{6,8},{7,9},{8,6},{9,7},{10,... | collective-permute-start | bytes 49160 | tf_op jit(solution)/shard_map/ppermute | solution.py:395

commit v5 on v4

v5 whole, which is shorter than its diff:
```python
import jax
import jax.numpy as jnp
from jax import lax
from jax.experimental import pallas as pl
from jax.experimental.pallas import tpu as pltpu
from jax.sharding import PartitionSpec as P

OMEGA = 0.8
F32 = jnp.float32
WINDOW = 64
VM = pl.BlockSpec(memory_space=pltpu.VMEM)
SM = pl.BlockSpec(memory_space=pltpu.SMEM)


def shape(*dims):
    return jax.ShapeDtypeStruct(dims, F32)


def call(body, outs, scratch, *args):
    return pl.pallas_call(
        body,
        out_shape=outs,
        in_specs=[SM] + [VM] * (len(args) - 1),
        out_specs=tuple(VM for _ in outs),
        scratch_shapes=[pltpu.VMEM(s, F32) for s in scratch],
        compiler_params=pltpu.CompilerParams(vmem_limit_bytes=16 << 20),
    )(*args)


def iota(rows, axis):
    return lax.broadcasted_iota(jnp.int32, (rows, 128), axis)


def pick(kind):
    i, j = iota(128, 0), iota(128, 1)
    if kind == "pairs":
        at = (i >> 1) == j
    elif kind == "beside":
        at = (i >= 2 * j - 1) & (i <= 2 * j + 2) & (j < 64)
    else:
        at = i == (j >> 1)
    return jnp.where(at, 1.0, 0.0).astype(jnp.bfloat16)


def halves(a):
    high = a.astype(jnp.bfloat16)
    return [high, (a - high.astype(F32)).astype(jnp.bfloat16)]


def dot(*terms):
    left = jnp.concatenate([h for a, _ in terms for h in halves(a)], axis=1)
    right = jnp.concatenate([m for _, m in terms for _ in (0, 1)], axis=0)
    return jnp.dot(left, right, preferred_element_type=F32)


def turn(v, by, axis):
    return pltpu.roll(v, by % v.shape[axis], axis)


def z_sum(v):
    lane = iota(v.shape[0], 1)
    below = jnp.where(lane == 0, 0.0, turn(v, 1, 1))
    return below + jnp.where(lane == 127, 0.0, turn(v, -1, 1))


def beside(ref, k, v, start, rows):
    return ref[k, pl.ds(start - 1, rows)] + ref[k, pl.ds(start + 1, rows)] + z_sum(v)


def windowed(ref, k, v, rows, at):
    below = jnp.where(at == 0, 0.0, ref[k, pl.ds(7, rows)])
    above = jnp.where(at == WINDOW - 1, 0.0, ref[k, pl.ds(9, rows)])
    return below + above + turn(v, 1, 1) + turn(v, -1, 1)


def inside(at, size):
    return (at >= 0) & (at < size)


def every_other(ref, k, start, rows):
    return ref[k, pl.ds(start, rows, stride=2), :]


def row_pairs(ref, k, start, rows):
    return every_other(ref, k, start, rows) + every_other(ref, k, start + 1, rows)


def gather(both, rest, k, at_both, at_rest, rows, at=None):
    below, above = every_other(both, k, at_both - 1, rows), every_other(both, k, at_both + 2, rows)
    if at is not None:
        below = jnp.where(at == 0, 0.0, below)
        above = jnp.where(at == WINDOW // 2 - 1, 0.0, above)
    own = row_pairs(both, k, at_both, rows)
    return row_pairs(rest, k, at_rest, rows) + own + below + above, own


def head_kernel(
    aggs,
    at, b, c, ye, yo,
    p0, vown, wown, b1, c1, edge, se, so,
    v, w, q, bx, cx, own1, rest1,
):
    bi, ai = at[0], at[1]
    x_even, y_even = (bi & 1) == 0, (ai & 1) == 0
    y_lo = jnp.where(ai > 0, OMEGA, 0.0)
    y_hi = jnp.where(ai < aggs - 1, OMEGA, 0.0)
    rows = pl.ds(8, 80)

    def put(p, rows, bb, cc, scale):
        ww = scale / (6.0 + cc)
        vv = ww * bb
        w[p, rows], v[p, rows], bx[p, rows], cx[p, rows] = ww, vv, bb, cc
        return vv, ww

    def planes(n, carry):
        for p in (2 * n, 2 * n + 1):
            vown[p], wown[p] = put(p, pl.ds(16, 64), b[p], c[p], OMEGA)
            lo = [jnp.where(y_even, yo[k, p], ye[k, p]) for k in (0, 1)]
            hi = [jnp.where(y_even, ye[k, p], yo[k, p]) for k in (0, 1)]
            put(p, pl.ds(12, 4), *lo, y_lo)
            put(p, pl.ds(80, 4), *hi, y_hi)
        return carry

    lax.fori_loop(0, 8, planes, 0)

    def smooth(n, carry):
        for p in (1 + 2 * n, 2 + 2 * n):
            vv = v[p, rows]
            near = v[p - 1, rows] + v[p + 1, rows] + beside(v, p, vv, 8, 80)
            qq = 0.4 * vv + w[p, rows] * near
            q[p, rows] = qq
            p0[p] = qq + OMEGA * vv
        return carry

    lax.fori_loop(0, 7, smooth, 0)
    for n, p, inner in ((0, 0, 1), (3, 15, 14)):
        vv, ww = v[p, rows], w[p, rows]
        edge[n] = 0.4 * vv + ww * (v[inner, rows] + beside(v, p, vv, 8, 80))
        edge[n + 1] = ww
        edge[n + 2] = vv

    def sums(k, p):
        cx[k, rows] = cx[p, rows] + cx[p + 1, rows]
        return 0.04 * (bx[p, rows] + bx[p + 1, rows])

    def coarse(k, carry):
        p = 2 * k
        both = q[p, rows] + q[p + 1, rows]
        own1[k, rows] = both
        rest1[k] = sums(k, p) + (both + (q[p - 1, rows] + q[p + 2, rows]))
        return carry

    own1[0, rows] = q[1, rows]
    rest1[0] = sums(0, 0) + (q[1, rows] + q[2, rows])
    lax.fori_loop(1, 7, coarse, 0)
    own1[7, rows] = q[14, rows]
    rest1[7] = sums(7, 14) + (q[14, rows] + q[13, rows])

    pairs, sides = pick("pairs"), pick("beside")

    def products(n, carry):
        ends, mids, csums = [], [], []
        for k in (2 * n, 2 * n + 1):
            end, mid = gather(own1, rest1, k, 8, 0, 40)
            ends.append(end)
            mids.append(mid)
            csums.append(row_pairs(cx, k, 8, 40))
        bb = dot((jnp.concatenate(ends, axis=0), pairs), (jnp.concatenate(mids, axis=0), sides))
        cc = dot((jnp.concatenate(csums, axis=0), pairs))
        for i in (0, 1):
            b1[2 * n + i] = 0.5 * bb[40 * i : 40 * i + 40]
            c1[2 * n + i] = 0.5 * cc[40 * i : 40 * i + 40]
        return carry

    lax.fori_loop(0, 4, products, 0)
    for ref, up in ((se, x_even), (so, jnp.logical_not(x_even))):
        for i in range(3):
            ref[2 * i] = jnp.where(up, edge[3 + i, 0:40], edge[i, 0:40])
            ref[2 * i + 1] = jnp.where(up, edge[3 + i, 40:80], edge[i, 40:80])
            ref[6 + i] = jnp.where(up, b1[5 + i], b1[i]) + turn(jnp.where(up, c1[5 + i], c1[i]), 64, 1)


def mid_kernel(
    blocks, aggs,
    at, b1in, c1in, edge, xe, xo,
    pe, e1out, w1out, bc2, se, so,
    s4, r4, b1, c1, e1, own2, rest2,
):
    bi, ai = at[0], at[1]
    x_even, y_even = (bi & 1) == 0, (ai & 1) == 0
    pairs, sides = pick("pairs"), pick("beside")
    has_lo, has_hi = bi > 0, bi < blocks - 1
    lane1 = iota(40, 1) < 64

    def fetch(lo, n):
        first = x_even if lo else jnp.logical_not(x_even)
        return jnp.where(first, xo[n], xe[n])

    for i, (lo, there) in enumerate(((True, has_lo), (False, has_hi))):
        gb, wb, vb = [
            jnp.where(there, jnp.concatenate([fetch(lo, 2 * n), fetch(lo, 2 * n + 1)], axis=0), 0.0)
            for n in range(3)
        ]
        g, w, v = [edge[3 * i + n] for n in range(3)]
        mine, other = g + w * vb, gb + wb * v
        near, far = (1, 0) if lo else (2, 3)
        pe[near] = mine + OMEGA * v
        pe[far] = other + OMEGA * vb
        s4[2 * i, pl.ds(8, 80)] = mine
        s4[2 * i + 1, pl.ds(8, 80)] = other
        r4[2 * i] = mine + other
        r4[2 * i + 1] = mine + other
        for n in range(3):
            mix = fetch(lo, 6 + n)
            k = n if lo else 11 + n
            b1[k] = jnp.where(lane1, mix, 0.0)
            c1[k] = jnp.where(lane1, turn(mix, -64, 1), 0.0)
    for k in range(8):
        b1[k + 3] = b1in[k]
        c1[k + 3] = c1in[k]
    ends, mids = [], []
    for i in range(4):
        end, mid = gather(s4, r4, i, 8, 0, 40)
        ends.append(end)
        mids.append(mid)
    more = dot((jnp.concatenate(ends, axis=0), pairs), (jnp.concatenate(mids, axis=0), sides))
    for i, k in enumerate((3, 2, 10, 11)):
        b1[k] = b1[k] + 0.5 * more[40 * i : 40 * i + 40]

    row1 = ai * 32 - 4 + iota(40, 0)
    keep1 = inside(row1, 32 * aggs) & lane1
    for k in range(14):
        ok = keep1 & inside(bi * 8 + k - 3, 8 * blocks)
        ww = jnp.where(ok, OMEGA / (6.0 + c1[k]), 0.0)
        ee = jnp.where(ok, ww * b1[k], 0.0)
        e1[k] = ee
        if 0 < k < 13:
            w1out[k - 1], e1out[k - 1] = ww, ee

    at2 = (ai * 16 + iota(16, 0)) & (WINDOW // 2 - 1)
    lane16 = iota(16, 1)
    ends, mids, csums = [], [], []
    for k in range(6):
        p = 1 + 2 * k
        both = e1[p] + e1[p + 1]
        own2[k] = both
        rest2[k] = 0.2 * (b1[p] + b1[p + 1]) + (both + (e1[p - 1] + e1[p + 2]))
        end, mid = gather(own2, rest2, k, 4, 4, 16, at2)
        ends.append(end)
        mids.append(mid)
        csums.append(row_pairs(c1, p, 4, 16) + row_pairs(c1, p + 1, 4, 16))
    bb2 = dot((jnp.concatenate(ends, axis=0), pairs), (jnp.concatenate(mids, axis=0), sides))
    cc2 = dot((jnp.concatenate(csums, axis=0), pairs))
    for k in range(6):
        bb = jnp.where(lane16 < 32, 0.5 * bb2[16 * k : 16 * k + 16], 0.0)
        cc = jnp.where(lane16 < 32, 0.5 * cc2[16 * k : 16 * k + 16], 0.0)
        mix = bb + turn(cc, 32, 1)
        bc2[k] = mix
        for ref, lo_side in ((se, jnp.logical_not(y_even)), (so, y_even)):
            ref[k, 0:5] = jnp.where(lo_side, mix[0:5], mix[11:16])
            for j in (0, 1):
                n = 3 + (2 * k + j) % 8
                ref[k, 5 + j : 6 + j] = jnp.where(lo_side, e1[n, 5:6], e1[n, 34:35])
            ref[k, 7:8] = jnp.zeros((1, 128), F32)


def join_kernel(at, bc2, ye, yo, wide, se, so):
    bi, ai = at[0], at[1]
    x_even, y_even = (bi & 1) == 0, (ai & 1) == 0
    for k in range(6):
        wide[k] = jnp.zeros((32, 128), F32)
        wide[k, 3:8] = jnp.where(y_even, yo[k, 0:5], ye[k, 0:5])
        wide[k, 8:24] = bc2[k]
        wide[k, 24:29] = jnp.where(y_even, ye[k, 0:5], yo[k, 0:5])
    for k in range(5):
        se[k] = jnp.where(x_even, wide[k], wide[k + 1])
        so[k] = jnp.where(x_even, wide[k + 1], wide[k])


def up_kernel(
    blocks, aggs,
    at, p0, pe, vown, wown, e1in, w1, wide, ye, yo, xe, xo,
    out,
    bc, e2, w2, b2, c2, own2, rest2, m2, t2, e1, m1, mf,
):
    bi, ai = at[0], at[1]
    x_even, y_even = (bi & 1) == 0, (ai & 1) == 0
    pairs, sides, copies = pick("pairs"), pick("beside"), pick("copies")

    for k in range(5):
        bc[k] = jnp.where(x_even, xo[k], xe[k])
        bc[9 + k] = jnp.where(x_even, xe[k], xo[k])
    for k in range(4):
        bc[5 + k] = wide[1 + k]

    row2 = ai * 16 - 8 + iota(32, 0)
    lane2 = iota(32, 1) < 32
    keep2 = inside(row2, 16 * aggs) & lane2
    for k in range(14):
        mix = bc[k]
        bb = jnp.where(lane2, mix, 0.0)
        cc = jnp.where(lane2, turn(mix, -32, 1), 0.0)
        ww = jnp.where(keep2 & inside(bi * 4 + k - 5, 4 * blocks), OMEGA / (6.0 + cc), 0.0)
        b2[k], c2[k], w2[k], e2[k] = bb, cc, ww, ww * bb

    row3 = ai * 8 - 4 + iota(16, 0)
    at3 = row3 & (WINDOW // 2 - 1)
    ends, mids, sums = [], [], []
    for j in range(6):
        k = 1 + 2 * j
        both = e2[k] + e2[k + 1]
        own2[j, 8:40] = both
        rest2[j] = 0.2 * (b2[k] + b2[k + 1]) + (both + (e2[k - 1] + e2[k + 2]))
        end, mid = gather(own2, rest2, j, 8, 0, 16, at3)
        ends.append(end)
        mids.append(mid)
        sums.append(row_pairs(c2, k, 0, 16) + row_pairs(c2, k + 1, 0, 16))
    bb3 = dot((jnp.concatenate(ends, axis=0), pairs), (jnp.concatenate(mids, axis=0), sides))
    cc3 = dot((jnp.concatenate(sums, axis=0), pairs))
    keep3 = inside(row3, 8 * aggs) & (iota(16, 1) < 16)
    e3, w3 = [], []
    for j in range(6):
        bb, cc = 0.5 * bb3[16 * j : 16 * j + 16], 0.5 * cc3[16 * j : 16 * j + 16]
        ok = keep3 & inside(bi * 2 + j - 2, 2 * blocks)
        ww = jnp.where(ok, OMEGA / (6.0 + cc), 0.0)
        w3.append(ww)
        e3.append(jnp.where(ok, ww * bb, 0.0))
    solved = []
    for j in range(1, 5):
        v = e3[j]
        near = e3[j - 1] + e3[j + 1] + turn(v, 1, 0) + turn(v, -1, 0) + turn(v, 1, 1) + turn(v, -1, 1)
        solved.append(1.2 * v + w3[j] * near)
    wider = dot((jnp.concatenate(solved, axis=0), copies))
    for k in range(3, 11):
        j = (k - 3) // 2
        for r in (0, 1):
            m2[k, pl.ds(8 + r, 16, stride=2), :] = every_other(e2, k, r, 16) + wider[16 * j : 16 * j + 16]
    at2 = row2 & (WINDOW - 1)
    rows = pl.ds(8, 32)
    solved = []
    for k in range(4, 10):
        v = m2[k, rows]
        near = m2[k - 1, rows] + m2[k + 1, rows] + windowed(m2, k, v, 32, at2)
        solved.append(0.2 * v + e2[k] + w2[k] * near)
    wider = dot((jnp.concatenate(solved, axis=0), copies))
    for k in range(6):
        t2[k] = wider[32 * k : 32 * k + 32]

    for k in range(12):
        e1[k] = e1in[k]
    for n in range(8):
        k, j = n // 2, n % 2
        mine, other = ye[k, 5 + j : 6 + j], yo[k, 5 + j : 6 + j]
        e1[n + 2, 2:3] = jnp.where(y_even, other, mine)
        e1[n + 2, 37:38] = jnp.where(y_even, mine, other)
    for k in range(12):
        for r in (0, 1):
            m1[k, pl.ds(8 + r, 20, stride=2), :] = every_other(e1, k, r, 20) + t2[k // 2, 6:26]
    at1 = (ai * 32 - 4 + iota(40, 0)) & (WINDOW - 1)

    def fine(n, first):
        rows = pl.ds(8, 40)
        solved = []
        for k in (2 * n, 2 * n + 1):
            v = m1[k + 1, rows]
            near = m1[k, rows] + m1[k + 2, rows] + windowed(m1, k + 1, v, 40, at1)
            solved.append(0.2 * v + e1[k + 1] + w1[k + 1] * near)
        wider = dot((jnp.concatenate(solved, axis=0), copies))
        for k, (ref, p) in enumerate(first(4 * n)):
            for r in (0, 1):
                if ref is not None:
                    old = ref[p, pl.ds(r, 40, stride=2), :]
                    i = 40 * (k // 2)
                    mf[4 * n + k, pl.ds(8 + r, 40, stride=2), :] = old + wider[i : i + 40]

    def inner(n, carry):
        fine(n, lambda k: [(p0, k - 2), (p0, k - 1), (p0, k), (p0, k + 1)])
        return carry

    fine(0, lambda k: [(None, 0), (pe, 0), (pe, 1), (p0, 1)])
    lax.fori_loop(1, 4, inner, 0)
    fine(4, lambda k: [(p0, 14), (pe, 2), (pe, 3), (None, 0)])

    def last(n, carry):
        rows = pl.ds(16, 64)
        for k in (2 * n, 2 * n + 1):
            m = mf[k + 2, rows]
            near = mf[k + 1, rows] + mf[k + 3, rows] + beside(mf, k + 2, m, 16, 64)
            out[k] = 0.2 * m + vown[k] + wown[k] * near
        return carry

    lax.fori_loop(0, 8, last, 0)


def swaps(size, apart):
    inner, outer = [], []
    for i in range(size):
        inner.append((i, i ^ apart))
        outer.append((i, (i + apart) % size if i & apart else (i - apart) % size))
    return inner, outer


def shards(b, c):
    blocks, aggs = lax.axis_size("blk"), lax.axis_size("agg")
    bi, ai = lax.axis_index("blk"), lax.axis_index("agg")
    at = jnp.stack([bi, ai]).astype(jnp.int32)
    y_even = (ai & 1) == 0
    near_in, near_out = swaps(blocks, 1)
    side_in, side_out = swaps(aggs, 1)

    first = jnp.stack([b[:, :4], c[:, :4]])
    last = jnp.stack([b[:, 60:], c[:, 60:]])
    ye = lax.ppermute(jnp.where(y_even, last, first), "agg", side_in)
    yo = lax.ppermute(jnp.where(y_even, first, last), "agg", side_out)

    big, mid, own = (16, 96, 128), (12, 40, 128), (16, 64, 128)
    p0, vown, wown, b1, c1, edge, se, so = call(
        lambda *refs: head_kernel(aggs, *refs),
        (shape(16, 80, 128), shape(*own), shape(*own), shape(8, 40, 128), shape(8, 40, 128),
         shape(6, 80, 128), shape(9, 40, 128), shape(9, 40, 128)),
        [big] * 5 + [(8, 96, 128), (8, 80, 128)],
        at, b, c, ye, yo,
    )
    xe = lax.ppermute(se, "blk", near_in)
    xo = lax.ppermute(so, "blk", near_out)
    tall = (14, 40, 128)
    pe, e1, w1, bc2, se, so = call(
        lambda *refs: mid_kernel(blocks, aggs, *refs),
        (shape(4, 80, 128), shape(*mid), shape(*mid), shape(6, 16, 128), shape(6, 8, 128), shape(6, 8, 128)),
        [(4, 96, 128), (4, 80, 128), tall, tall, tall, (6, 40, 128), (6, 40, 128)],
        at, b1, c1, edge, xe, xo,
    )
    ye = lax.ppermute(se, "agg", side_in)
    yo = lax.ppermute(so, "agg", side_out)
    wide, se, so = call(
        join_kernel,
        (shape(6, 32, 128), shape(5, 32, 128), shape(5, 32, 128)),
        [],
        at, bc2, ye, yo,
    )
    xe = lax.ppermute(se, "blk", near_in)
    xo = lax.ppermute(so, "blk", near_out)
    small = (14, 32, 128)
    (out,) = call(
        lambda *refs: up_kernel(blocks, aggs, *refs),
        (shape(*own),),
        [small] * 5 + [(6, 48, 128), (6, 32, 128), (14, 48, 128), (6, 32, 128), mid, (12, 56, 128), (20, 96, 128)],
        at, p0, pe, vown, wown, e1, w1, wide, ye, yo, xe, xo,
    )
    return out


def solution(mesh):
    placed = (P("blk", "agg", None), P("blk", "agg", None))
    return jax.shard_map(
        shards, mesh=mesh, in_specs=placed, out_specs=P("blk", "agg", None), check_vma=False
    )
```

time: 45.5 us -> 39.9 us (0.88)
  waiting for transfers between devices: 18.9 us -> 11 us
  starting transfers between devices: 16.5 us -> 18.1 us
  local copies, waits for them, and re-layouts: 1.18 us -> 2.06 us
    ppermute x4 -> x0, waiting for transfers between devices: 12.9 us -> none  [the longest x1 6.26 us: shards(): xo = lax.ppermute(jnp.where(x_even, first, last), 'blk', near_out)]
    ppermute x4 -> x0, starting transfers between devices: 9.01 us -> none  [the longest x1 6.42 us: shards(): xo = lax.ppermute(jnp.where(x_even, first, last), 'blk', near_out)]
    ppermute x1 -> x2, waiting for transfers between devices: 0.01 us -> 7.18 us  [shards(): xo = lax.ppermute(so, 'blk', near_out)]
    ppermute x1 -> x2, starting transfers between devices: 3.41 us -> 9.52 us  [shards(): xo = lax.ppermute(so, 'blk', near_out)]
    ppermute x1 -> x2, starting transfers between devices: 0.36 us -> 2.2 us  [shards(): xe = lax.ppermute(se, 'blk', near_in)]
    ppermute x1, starting transfers between devices: 1.91 us -> 3.67 us  [shards(): yo = lax.ppermute(so, 'agg', side_out)]
    ppermute x1, starting transfers between devices: 1.4 us -> 2.64 us  [shards(): yo = lax.ppermute(jnp.where(y_even, first, last), 'agg', side_out)]
    ppermute x1, waiting for transfers between devices: 3.48 us -> 2.26 us  [shards(): yo = lax.ppermute(jnp.where(y_even, first, last), 'agg', side_out)]
  transfers between devices with their start and end apart: 10 -> 8, of which waited for: 6 -> 4; matrix products, arithmetic and copies ran while one was open for 0% -> 0% of each run, Pallas kernels for 0% -> 0%
where the time goes in v5:
time: 39.9 us; the launch traced here: 39.7 us
  starting transfers between devices  18.1 us (45%)
  waiting for transfers between devices  11 us (28%)
  Pallas kernels  8.42 us (21%)
  local copies, waits for them, and re-layouts  2.06 us (5%)
    ppermute x2, starting transfers between devices, shards(): xo = lax.ppermute(so, 'blk', near_out)  9.52 us
    pallas_call x4, Pallas kernels, call(): pl.pallas_call(body, out_shape=outs, in_specs=[SM] + [VM] * (len(args) -...  8.42 us
    ppermute x2, waiting for transfers between devices, shards(): xo = lax.ppermute(so, 'blk', near_out)  7.18 us
    ppermute x1, starting transfers between devices, shards(): yo = lax.ppermute(so, 'agg', side_out)  3.67 us
    ppermute x1, starting transfers between devices, shards(): yo = lax.ppermute(jnp.where(y_even, first, last), 'agg', side_out)  2.64 us
    ppermute x1, waiting for transfers between devices, shards(): yo = lax.ppermute(jnp.where(y_even, first, last), 'agg', side_out)  2.26 us
    ppermute x2, starting transfers between devices, shards(): xe = lax.ppermute(se, 'blk', near_in)  2.2 us
    ppermute x1, waiting for transfers between devices, shards(): yo = lax.ppermute(so, 'agg', side_out)  1.52 us
  transfers between devices with their start and end apart: 8, of which 4 were waited for; matrix products, arithmetic and copies ran while one was open for 0% of the time, Pallas kernels for 0%

profile of v5, /device:TPU:0, one launch (start us, length us, event | category | flops | bytes accessed | tf_op | source)
XLA Modules:
  0.0 39.7 jit_solution(14246214164233479959)
XLA Ops:
  0.0 0.0 copy-start
  0.0 1.0 %slice_bitcast_fusion.2 = (f32[1,16,4,128]{3,2,1,0:T(4,128)S(1)}, f32[1,16,4,128]{3,2,1,0:T(4,128)S(1)}, f32[1,16,4,128]{3,2,1,0:T(4,128)S(1)}, f32[1,16,4,128]{3,2,1,0:T(4,128)S(1)}) fusion(f32[16,64,128]{2,1,0:T(8,128)} %refs_2_.1, f32[16,64,128]{2,1,0:T(8,128)} %refs_1_.1), kind=kLoop, calls=%fused_computation.6 | loop fusion | bytes 262144 | tf_op jit(solution)/shard_map/stack | solution.py:412
  1.1 2.6 %collective-permute-start.1 = (f32[2,16,4,128]{3,2,1,0:T(4,128)S(1)}, f32[2,16,4,128]{3,2,1,0:T(4,128)S(1)}, u32[]{:S(2)}, u32[]{:S(2)}) collective-permute-start(f32[2,16,4,128]{3,2,1,0:T(4,128)S(1)} %get-tuple-element.43), channel_id=1, source_target_pairs={{0,112},{16,32},{32,16},{48,64},{64,48},{80,96},{96,80},{112,0},{1... | collective-permute-start | bytes 196616 | tf_op jit(solution)/shard_map/ppermute | solution.py:414
  3.7 0.0 collective-permute-start
  3.7 0.1 pad_add_fusion.refs_0_.at
  3.8 2.3 %collective-permute-done.1.refs_4_ = f32[2,16,4,128]{3,2,1,0:T(4,128)S(1)} collective-permute-done((f32[2,16,4,128]{3,2,1,0:T(4,128)S(1)}, f32[2,16,4,128]{3,2,1,0:T(4,128)S(1)}, u32[]{:S(2)}, u32[]{:S(2)}) %collective-permute-start.1) | collective-permute-done | bytes 65568 | tf_op jit(solution)/shard_map/ppermute | solution.py:414
  6.1 0.0 collective-permute-done.refs_3_
  6.1 0.0 copy-done
  6.1 0.0 copy-start.1
  6.1 1.0 %copy-done.1 = f32[16,64,128]{2,1,0:T(8,128)S(1)} copy-done((f32[16,64,128]{2,1,0:T(8,128)S(1)}, f32[16,64,128]{2,1,0:T(8,128)}, u32[]{:S(2)}) %copy-start.1) | copy-done | bytes 524312
  7.1 2.7 %shard_map.28 = (f32[16,80,128]{2,1,0:T(8,128)S(1)}, f32[16,64,128]{2,1,0:T(8,128)S(1)}, f32[16,64,128]{2,1,0:T(8,128)S(1)}, f32[8,40,128]{2,1,0:T(8,128)S(1)}, ...) custom-call(s32[2]{0:T(128)S(1)} %pad_add_fusion.refs_0_.at, ...), custom_call_target="tpu_custom_call" | custom-call | tf_op jit(solution)/shard_map/pallas_call | solution.py:20
  9.8 2.1 %collective-permute-start.2 = (f32[9,40,128]{2,1,0:T(8,128)S(1)}, f32[9,40,128]{2,1,0:T(8,128)S(1)}, u32[]{:S(2)}, u32[]{:S(2)}) collective-permute-start(f32[9,40,128]{2,1,0:T(8,128)S(1)} %get-tuple-element.26), channel_id=1, source_target_pairs={{0,1},{1,0},{2,3},{3,2},{4,5},{5,4},{6,7},{7,6},{8,9},{9,8},{10,11... | collective-permute-start | bytes 552968 | tf_op jit(solution)/shard_map/ppermute | solution.py:424
  11.9 4.7 %collective-permute-start.3 = (f32[9,40,128]{2,1,0:T(8,128)S(1)}, f32[9,40,128]{2,1,0:T(8,128)S(1)}, u32[]{:S(2)}, u32[]{:S(2)}) collective-permute-start(f32[9,40,128]{2,1,0:T(8,128)S(1)} %get-tuple-element.27), channel_id=1, source_target_pairs={{0,15},{1,2},{2,1},{3,4},{4,3},{5,6},{6,5},{7,8},{8,7},{9,10},{10,... | collective-permute-start | bytes 552968 | tf_op jit(solution)/shard_map/ppermute | solution.py:425
  16.6 0.0 collective-permute-done.2.refs_4_
  16.6 4.1 %collective-permute-done.3.refs_5_ = f32[9,40,128]{2,1,0:T(8,128)S(1)} collective-permute-done((f32[9,40,128]{2,1,0:T(8,128)S(1)}, f32[9,40,128]{2,1,0:T(8,128)S(1)}, u32[]{:S(2)}, u32[]{:S(2)}) %collective-permute-start.3) | collective-permute-done | bytes 184352 | tf_op jit(solution)/shard_map/ppermute | solution.py:425
  20.8 1.1 %shard_map.29 = (f32[4,80,128]{2,1,0:T(8,128)S(1)}, f32[12,40,128]{2,1,0:T(8,128)S(1)}, f32[12,40,128]{2,1,0:T(8,128)S(1)}, f32[6,16,128]{2,1,0:T(8,128)S(1)}, f...) custom-call(s32[2]{0:T(128)S(1)} %pad_add_fusion.refs_0_.at, f32[8,40,128]{2,1,0:T(8,128)S(1)} %get-tuple-element.23.refs_1_, ...), custom_call_target="tpu_custom_call" | custom-call | tf_op jit(solution)/shard_map/pallas_call | solution.py:20
  21.9 0.1 collective-permute-start.4
  22.0 3.7 %collective-permute-start.5 = (f32[6,8,128]{2,1,0:T(8,128)S(1)}, f32[6,8,128]{2,1,0:T(8,128)S(1)}, u32[]{:S(2)}, u32[]{:S(2)}) collective-permute-start(f32[6,8,128]{2,1,0:T(8,128)S(1)} %get-tuple-element.35), channel_id=1, source_target_pairs={{0,112},{16,32},{32,16},{48,64},{64,48},{80,96},{96,80},{112,0},{1... | collective-permute-start | bytes 73736 | tf_op jit(solution)/shard_map/ppermute | solution.py:434
  25.7 0.0 collective-permute-done.4.ye.refs_8_
  25.7 1.5 %collective-permute-done.5.yo.refs_9_ = f32[6,8,128]{2,1,0:T(8,128)S(1)} collective-permute-done((f32[6,8,128]{2,1,0:T(8,128)S(1)}, f32[6,8,128]{2,1,0:T(8,128)S(1)}, u32[]{:S(2)}, u32[]{:S(2)}) %collective-permute-start.5) | collective-permute-done | bytes 24608 | tf_op jit(solution)/shard_map/ppermute | solution.py:434
  27.2 0.6 %shard_map.30 = (f32[6,32,128]{2,1,0:T(8,128)S(1)}, f32[5,32,128]{2,1,0:T(8,128)S(1)}, f32[5,32,128]{2,1,0:T(8,128)S(1)}) custom-call(s32[2]{0:T(128)S(1)} %pad_add_fusion.refs_0_.at, f32[6,16,128]{2,1,0:T(8,128)S(1)} %get-tuple-element.33.bc2, f32[6,8,128]{2,1,0:T(8,128)S(1)} %collective-permute-done.4.ye.refs_8_, ...), custom_call_target="tpu_custom_call" | custom-call | tf_op jit(solution)/shard_map/pallas_call | solution.py:20
  27.8 0.1 collective-permute-start.6
  27.9 4.8 %collective-permute-start.7 = (f32[5,32,128]{2,1,0:T(8,128)S(1)}, f32[5,32,128]{2,1,0:T(8,128)S(1)}, u32[]{:S(2)}, u32[]{:S(2)}) collective-permute-start(f32[5,32,128]{2,1,0:T(8,128)S(1)} %get-tuple-element.38), channel_id=1, source_target_pairs={{0,15},{1,2},{2,1},{3,4},{4,3},{5,6},{6,5},{7,8},{8,7},{9,10},{10,... | collective-permute-start | bytes 245768 | tf_op jit(solution)/shard_map/ppermute | solution.py:442
  32.7 0.0 collective-permute-done.6.refs_10_
  32.7 3.0 %collective-permute-done.7.refs_11_ = f32[5,32,128]{2,1,0:T(8,128)S(1)} collective-permute-done((f32[5,32,128]{2,1,0:T(8,128)S(1)}, f32[5,32,128]{2,1,0:T(8,128)S(1)}, u32[]{:S(2)}, u32[]{:S(2)}) %collective-permute-start.7) | collective-permute-done | bytes 81952 | tf_op jit(solution)/shard_map/ppermute | solution.py:442
  35.7 4.0 %shard_map.31 = f32[16,64,128]{2,1,0:T(8,128)} custom-call(s32[2]{0:T(128)S(1)} %pad_add_fusion.refs_0_.at, f32[16,80,128]{2,1,0:T(8,128)S(1)} %get-tuple-element.22.refs_1_, f32[4,80,128]{2,1,0:T(8,128)S(1)} %get-tuple-element.28.refs_2_, f32[16,64,128]{2,1,0:T(8,128)S(1)} %get-tuple-element.29.refs_3_, f32[16,64,128]{2,1,0:T(8,128)S(1)} %get-tuple-element.30.refs_4_, ...), custom_call_target="tpu_custom_call" | custom-call | tf_op jit(solution)/shard_map/pallas_call | solution.py:20
  (1 shorter events, 0.0 us)
Async XLA Ops:
  0.0 6.1 %copy-start = (f32[16,64,128]{2,1,0:T(8,128)S(1)}, f32[16,64,128]{2,1,0:T(8,128)}, u32[]{:S(2)}) copy-start(f32[16,64,128]{2,1,0:T(8,128)} %refs_1_.1) | copy-start | bytes 1572868
  1.1 5.0 %collective-permute-start.1 = (f32[2,16,4,128]{3,2,1,0:T(4,128)S(1)}, f32[2,16,4,128]{3,2,1,0:T(4,128)S(1)}, u32[]{:S(2)}, u32[]{:S(2)}) collective-permute-start(f32[2,16,4,128]{3,2,1,0:T(4,128)S(1)} %get-tuple-element.43), channel_id=1, source_target_pairs={{0,112},{16,32},{32,16},{48,64},{64,48},{80,96},{96,80},{112,0},{1... | collective-permute-start | bytes 196616 | tf_op jit(solution)/shard_map/ppermute | solution.py:414
  3.7 2.3 %collective-permute-start = (f32[2,16,4,128]{3,2,1,0:T(4,128)S(1)}, f32[2,16,4,128]{3,2,1,0:T(4,128)S(1)}, u32[]{:S(2)}, u32[]{:S(2)}) collective-permute-start(f32[2,16,4,128]{3,2,1,0:T(4,128)S(1)} %get-tuple-element.44), channel_id=1, source_target_pairs={{0,16},{16,0},{32,48},{48,32},{64,80},{80,64},{96,112},{112,96},{1... | collective-permute-start | bytes 196616 | tf_op jit(solution)/shard_map/ppermute | solution.py:413
  6.1 1.0 %copy-start.1 = (f32[16,64,128]{2,1,0:T(8,128)S(1)}, f32[16,64,128]{2,1,0:T(8,128)}, u32[]{:S(2)}) copy-start(f32[16,64,128]{2,1,0:T(8,128)} %refs_2_.1) | copy-start | bytes 1572868
  9.8 6.8 %collective-permute-start.2 = (f32[9,40,128]{2,1,0:T(8,128)S(1)}, f32[9,40,128]{2,1,0:T(8,128)S(1)}, u32[]{:S(2)}, u32[]{:S(2)}) collective-permute-start(f32[9,40,128]{2,1,0:T(8,128)S(1)} %get-tuple-element.26), channel_id=1, source_target_pairs={{0,1},{1,0},{2,3},{3,2},{4,5},{5,4},{6,7},{7,6},{8,9},{9,8},{10,11... | collective-permute-start | bytes 552968 | tf_op jit(solution)/shard_map/ppermute | solution.py:424
  11.9 8.9 %collective-permute-start.3 = (f32[9,40,128]{2,1,0:T(8,128)S(1)}, f32[9,40,128]{2,1,0:T(8,128)S(1)}, u32[]{:S(2)}, u32[]{:S(2)}) collective-permute-start(f32[9,40,128]{2,1,0:T(8,128)S(1)} %get-tuple-element.27), channel_id=1, source_target_pairs={{0,15},{1,2},{2,1},{3,4},{4,3},{5,6},{6,5},{7,8},{8,7},{9,10},{10,... | collective-permute-start | bytes 552968 | tf_op jit(solution)/shard_map/ppermute | solution.py:425
  21.9 3.8 %collective-permute-start.4 = (f32[6,8,128]{2,1,0:T(8,128)S(1)}, f32[6,8,128]{2,1,0:T(8,128)S(1)}, u32[]{:S(2)}, u32[]{:S(2)}) collective-permute-start(f32[6,8,128]{2,1,0:T(8,128)S(1)} %get-tuple-element.34), channel_id=1, source_target_pairs={{0,16},{16,0},{32,48},{48,32},{64,80},{80,64},{96,112},{112,96},{1... | collective-permute-start | bytes 73736 | tf_op jit(solution)/shard_map/ppermute | solution.py:433
  22.0 5.2 %collective-permute-start.5 = (f32[6,8,128]{2,1,0:T(8,128)S(1)}, f32[6,8,128]{2,1,0:T(8,128)S(1)}, u32[]{:S(2)}, u32[]{:S(2)}) collective-permute-start(f32[6,8,128]{2,1,0:T(8,128)S(1)} %get-tuple-element.35), channel_id=1, source_target_pairs={{0,112},{16,32},{32,16},{48,64},{64,48},{80,96},{96,80},{112,0},{1... | collective-permute-start | bytes 73736 | tf_op jit(solution)/shard_map/ppermute | solution.py:434
  27.8 4.9 %collective-permute-start.6 = (f32[5,32,128]{2,1,0:T(8,128)S(1)}, f32[5,32,128]{2,1,0:T(8,128)S(1)}, u32[]{:S(2)}, u32[]{:S(2)}) collective-permute-start(f32[5,32,128]{2,1,0:T(8,128)S(1)} %get-tuple-element.37), channel_id=1, source_target_pairs={{0,1},{1,0},{2,3},{3,2},{4,5},{5,4},{6,7},{7,6},{8,9},{9,8},{10,11... | collective-permute-start | bytes 245768 | tf_op jit(solution)/shard_map/ppermute | solution.py:441
  27.9 7.8 %collective-permute-start.7 = (f32[5,32,128]{2,1,0:T(8,128)S(1)}, f32[5,32,128]{2,1,0:T(8,128)S(1)}, u32[]{:S(2)}, u32[]{:S(2)}) collective-permute-start(f32[5,32,128]{2,1,0:T(8,128)S(1)} %get-tuple-element.38), channel_id=1, source_target_pairs={{0,15},{1,2},{2,1},{3,4},{4,3},{5,6},{6,5},{7,8},{8,7},{9,10},{10,... | collective-permute-start | bytes 245768 | tf_op jit(solution)/shard_map/ppermute | solution.py:442

commit v6 on v5

--- a/solution.py
+++ b/solution.py
@@ -8,6 +8,7 @@
 OMEGA = 0.8
 F32 = jnp.float32
 WINDOW = 64
+STEPS = (4, 7, 3, 2, 4)
 VM = pl.BlockSpec(memory_space=pltpu.VMEM)
 SM = pl.BlockSpec(memory_space=pltpu.SMEM)
 
@@ -16,15 +17,24 @@
     return jax.ShapeDtypeStruct(dims, F32)
 
 
-def call(body, outs, scratch, *args):
+def call(body, outs, scratch, *args, specs=None):
     return pl.pallas_call(
         body,
         out_shape=outs,
-        in_specs=[SM] + [VM] * (len(args) - 1),
+        in_specs=specs or [SM] + [VM] * (len(args) - 1),
         out_specs=tuple(VM for _ in outs),
-        scratch_shapes=[pltpu.VMEM(s, F32) for s in scratch],
+        scratch_shapes=[pltpu.VMEM(s, F32) if isinstance(s, tuple) else s for s in scratch],
         compiler_params=pltpu.CompilerParams(vmem_limit_bytes=16 << 20),
     )(*args)
+
+
+def loop(start, stop, step, body):
+    def trip(n, carry):
+        for i in range(step):
+            body(start + n * step + i)
+        return carry
+
+    lax.fori_loop(0, (stop - start) // step, trip, 0)
 
 
 def iota(rows, axis):
@@ -94,11 +104,38 @@
     return row_pairs(rest, k, at_rest, rows) + own + below + above, own
 
 
+def pack_kernel(b, c, se, so, first, last, sem):
+    copies = []
+    for n, ref in enumerate((b, c)):
+        copies.append(pltpu.make_async_copy(ref.at[:, pl.ds(0, 8)], first.at[n], sem.at[2 * n]))
+        copies.append(pltpu.make_async_copy(ref.at[:, pl.ds(56, 8)], last.at[n], sem.at[2 * n + 1]))
+    for copy in copies:
+        copy.start()
+    y_even = (lax.axis_index("agg") & 1) == 0
+    for copy in copies:
+        copy.wait()
+    for n in (0, 1):
+        se[n] = jnp.where(y_even, last[n, :, 4:8], first[n, :, 0:4])
+        so[n] = jnp.where(y_even, first[n, :, 0:4], last[n, :, 4:8])
+
+
+def load_kernel(b, c, bv, cv, sem):
+    copies = []
+    for n in range(4):
+        part = pl.ds(4 * n, 4)
+        for i, (x, y) in enumerate(((b, bv), (c, cv))):
+            copies.append(pltpu.make_async_copy(x.at[part], y.at[part], sem.at[2 * n + i]))
+    for copy in copies:
+        copy.start()
+    for copy in copies:
+        copy.wait()
+
+
 def head_kernel(
     aggs,
     at, b, c, ye, yo,
-    p0, vown, wown, b1, c1, edge, se, so,
-    v, w, q, bx, cx, own1, rest1,
+    p0, v, w, b1, c1, edge, se, so,
+    q, bx, cx, own1, rest1,
 ):
     bi, ai = at[0], at[1]
     x_even, y_even = (bi & 1) == 0, (ai & 1) == 0
@@ -110,29 +147,24 @@
         ww = scale / (6.0 + cc)
         vv = ww * bb
         w[p, rows], v[p, rows], bx[p, rows], cx[p, rows] = ww, vv, bb, cc
-        return vv, ww
-
-    def planes(n, carry):
-        for p in (2 * n, 2 * n + 1):
-            vown[p], wown[p] = put(p, pl.ds(16, 64), b[p], c[p], OMEGA)
-            lo = [jnp.where(y_even, yo[k, p], ye[k, p]) for k in (0, 1)]
-            hi = [jnp.where(y_even, ye[k, p], yo[k, p]) for k in (0, 1)]
-            put(p, pl.ds(12, 4), *lo, y_lo)
-            put(p, pl.ds(80, 4), *hi, y_hi)
-        return carry
-
-    lax.fori_loop(0, 8, planes, 0)
-
-    def smooth(n, carry):
-        for p in (1 + 2 * n, 2 + 2 * n):
-            vv = v[p, rows]
-            near = v[p - 1, rows] + v[p + 1, rows] + beside(v, p, vv, 8, 80)
-            qq = 0.4 * vv + w[p, rows] * near
-            q[p, rows] = qq
-            p0[p] = qq + OMEGA * vv
-        return carry
-
-    lax.fori_loop(0, 7, smooth, 0)
+
+    def plane(p):
+        put(p, pl.ds(16, 64), b[p], c[p], OMEGA)
+        lo = [jnp.where(y_even, yo[k, p], ye[k, p]) for k in (0, 1)]
+        hi = [jnp.where(y_even, ye[k, p], yo[k, p]) for k in (0, 1)]
+        put(p, pl.ds(12, 4), *lo, y_lo)
+        put(p, pl.ds(80, 4), *hi, y_hi)
+
+    loop(0, 16, STEPS[0], plane)
+
+    def smooth(p):
+        vv = v[p, rows]
+        near = v[p - 1, rows] + v[p + 1, rows] + beside(v, p, vv, 8, 80)
+        qq = 0.4 * vv + w[p, rows] * near
+        q[p, rows] = qq
+        p0[p] = qq + OMEGA * vv
+
+    loop(1, 15, STEPS[1], smooth)
     for n, p, inner in ((0, 0, 1), (3, 15, 14)):
         vv, ww = v[p, rows], w[p, rows]
         edge[n] = 0.4 * vv + ww * (v[inner, rows] + beside(v, p, vv, 8, 80))
@@ -143,22 +175,21 @@
         cx[k, rows] = cx[p, rows] + cx[p + 1, rows]
         return 0.04 * (bx[p, rows] + bx[p + 1, rows])
 
-    def coarse(k, carry):
+    def coarse(k):
         p = 2 * k
         both = q[p, rows] + q[p + 1, rows]
         own1[k, rows] = both
         rest1[k] = sums(k, p) + (both + (q[p - 1, rows] + q[p + 2, rows]))
-        return carry
 
     own1[0, rows] = q[1, rows]
     rest1[0] = sums(0, 0) + (q[1, rows] + q[2, rows])
-    lax.fori_loop(1, 7, coarse, 0)
+    loop(1, 7, STEPS[2], coarse)
     own1[7, rows] = q[14, rows]
     rest1[7] = sums(7, 14) + (q[14, rows] + q[13, rows])
 
     pairs, sides = pick("pairs"), pick("beside")
 
-    def products(n, carry):
+    def products(n):
         ends, mids, csums = [], [], []
         for k in (2 * n, 2 * n + 1):
             end, mid = gather(own1, rest1, k, 8, 0, 40)
@@ -170,21 +201,20 @@
         for i in (0, 1):
             b1[2 * n + i] = 0.5 * bb[40 * i : 40 * i + 40]
             c1[2 * n + i] = 0.5 * cc[40 * i : 40 * i + 40]
-        return carry
-
-    lax.fori_loop(0, 4, products, 0)
+
+    loop(0, 4, STEPS[3], products)
     for ref, up in ((se, x_even), (so, jnp.logical_not(x_even))):
         for i in range(3):
-            ref[2 * i] = jnp.where(up, edge[3 + i, 0:40], edge[i, 0:40])
-            ref[2 * i + 1] = jnp.where(up, edge[3 + i, 40:80], edge[i, 40:80])
-            ref[6 + i] = jnp.where(up, b1[5 + i], b1[i]) + turn(jnp.where(up, c1[5 + i], c1[i]), 64, 1)
+            ref[72 * i : 72 * i + 72] = jnp.where(up, edge[3 + i, 4:76], edge[i, 4:76])
+            mix = jnp.where(up, b1[5 + i], b1[i]) + turn(jnp.where(up, c1[5 + i], c1[i]), 64, 1)
+            ref[216 + 40 * i : 256 + 40 * i] = mix
 
 
 def mid_kernel(
     blocks, aggs,
     at, b1in, c1in, edge, xe, xo,
     pe, e1out, w1out, bc2, se, so,
-    s4, r4, b1, c1, e1, own2, rest2,
+    far, s4, r4, b1, c1, e1, own2, rest2,
 ):
     bi, ai = at[0], at[1]
     x_even, y_even = (bi & 1) == 0, (ai & 1) == 0
@@ -192,26 +222,25 @@
     has_lo, has_hi = bi > 0, bi < blocks - 1
     lane1 = iota(40, 1) < 64
 
-    def fetch(lo, n):
+    def fetch(lo, start, rows):
         first = x_even if lo else jnp.logical_not(x_even)
-        return jnp.where(first, xo[n], xe[n])
+        return jnp.where(first, xo[start : start + rows], xe[start : start + rows])
 
     for i, (lo, there) in enumerate(((True, has_lo), (False, has_hi))):
-        gb, wb, vb = [
-            jnp.where(there, jnp.concatenate([fetch(lo, 2 * n), fetch(lo, 2 * n + 1)], axis=0), 0.0)
-            for n in range(3)
-        ]
+        for n in range(3):
+            far[3 * i + n, 4:76] = jnp.where(there, fetch(lo, 72 * n, 72), 0.0)
+        gb, wb, vb = [far[3 * i + n] for n in range(3)]
         g, w, v = [edge[3 * i + n] for n in range(3)]
         mine, other = g + w * vb, gb + wb * v
-        near, far = (1, 0) if lo else (2, 3)
-        pe[near] = mine + OMEGA * v
-        pe[far] = other + OMEGA * vb
+        here, there = (1, 0) if lo else (2, 3)
+        pe[here] = mine + OMEGA * v
+        pe[there] = other + OMEGA * vb
         s4[2 * i, pl.ds(8, 80)] = mine
         s4[2 * i + 1, pl.ds(8, 80)] = other
         r4[2 * i] = mine + other
         r4[2 * i + 1] = mine + other
         for n in range(3):
-            mix = fetch(lo, 6 + n)
+            mix = fetch(lo, 216 + 40 * n, 40)
             k = n if lo else 11 + n
             b1[k] = jnp.where(lane1, mix, 0.0)
             c1[k] = jnp.where(lane1, turn(mix, -64, 1), 0.0)
@@ -272,34 +301,38 @@
         wide[k, 3:8] = jnp.where(y_even, yo[k, 0:5], ye[k, 0:5])
         wide[k, 8:24] = bc2[k]
         wide[k, 24:29] = jnp.where(y_even, ye[k, 0:5], yo[k, 0:5])
-    for k in range(5):
-        se[k] = jnp.where(x_even, wide[k], wide[k + 1])
-        so[k] = jnp.where(x_even, wide[k + 1], wide[k])
+    for k in range(3):
+        low, high = wide[2 * k], wide[2 * k + 1]
+        if k < 2:
+            low, high = low + turn(high, 64, 1), high + turn(wide[2 * k + 2], 64, 1)
+        se[k] = jnp.where(x_even, low, high)
+        so[k] = jnp.where(x_even, high, low)
 
 
 def up_kernel(
     blocks, aggs,
-    at, p0, pe, vown, wown, e1in, w1, wide, ye, yo, xe, xo,
+    at, p0, pe, v0, w0, e1in, w1, wide, ye, yo, xe, xo,
     out,
-    bc, e2, w2, b2, c2, own2, rest2, m2, t2, e1, m1, mf,
+    e2, w2, b2, c2, own2, rest2, m2, t2, e1, m1, mf,
 ):
     bi, ai = at[0], at[1]
     x_even, y_even = (bi & 1) == 0, (ai & 1) == 0
     pairs, sides, copies = pick("pairs"), pick("beside"), pick("copies")
 
-    for k in range(5):
-        bc[k] = jnp.where(x_even, xo[k], xe[k])
-        bc[9 + k] = jnp.where(x_even, xe[k], xo[k])
-    for k in range(4):
-        bc[5 + k] = wide[1 + k]
+    def source(k):
+        if 5 <= k < 9:
+            return wide[k - 4], 0
+        n = k if k < 5 else k - 9
+        first = x_even if k < 5 else jnp.logical_not(x_even)
+        return jnp.where(first, xo[n // 2], xe[n // 2]), 64 * (n % 2)
 
     row2 = ai * 16 - 8 + iota(32, 0)
     lane2 = iota(32, 1) < 32
     keep2 = inside(row2, 16 * aggs) & lane2
     for k in range(14):
-        mix = bc[k]
-        bb = jnp.where(lane2, mix, 0.0)
-        cc = jnp.where(lane2, turn(mix, -32, 1), 0.0)
+        mix, lane = source(k)
+        bb = jnp.where(lane2, turn(mix, -lane, 1) if lane else mix, 0.0)
+        cc = jnp.where(lane2, turn(mix, -lane - 32, 1), 0.0)
         ww = jnp.where(keep2 & inside(bi * 4 + k - 5, 4 * blocks), OMEGA / (6.0 + cc), 0.0)
         b2[k], c2[k], w2[k], e2[k] = bb, cc, ww, ww * bb
 
@@ -381,15 +414,13 @@
     lax.fori_loop(1, 4, inner, 0)
     fine(4, lambda k: [(p0, 14), (pe, 2), (pe, 3), (None, 0)])
 
-    def last(n, carry):
+    def last(k):
         rows = pl.ds(16, 64)
-        for k in (2 * n, 2 * n + 1):
-            m = mf[k + 2, rows]
-            near = mf[k + 1, rows] + mf[k + 3, rows] + beside(mf, k + 2, m, 16, 64)
-            out[k] = 0.2 * m + vown[k] + wown[k] * near
-        return carry
-
-    lax.fori_loop(0, 8, last, 0)
+        m = mf[k + 2, rows]
+        near = mf[k + 1, rows] + mf[k + 3, rows] + beside(mf, k + 2, m, 16, 64)
+        out[k] = 0.2 * m + v0[k, rows] + w0[k, rows] * near
+
+    loop(0, 16, STEPS[4], last)
 
 
 def swaps(size, apart):
@@ -404,21 +435,35 @@
     blocks, aggs = lax.axis_size("blk"), lax.axis_size("agg")
     bi, ai = lax.axis_index("blk"), lax.axis_index("agg")
     at = jnp.stack([bi, ai]).astype(jnp.int32)
-    y_even = (ai & 1) == 0
     near_in, near_out = swaps(blocks, 1)
     side_in, side_out = swaps(aggs, 1)
 
-    first = jnp.stack([b[:, :4], c[:, :4]])
-    last = jnp.stack([b[:, 60:], c[:, 60:]])
-    ye = lax.ppermute(jnp.where(y_even, last, first), "agg", side_in)
-    yo = lax.ppermute(jnp.where(y_even, first, last), "agg", side_out)
-
-    big, mid, own = (16, 96, 128), (12, 40, 128), (16, 64, 128)
-    p0, vown, wown, b1, c1, edge, se, so = call(
+    hbm = pl.BlockSpec(memory_space=pltpu.HBM)
+    b, c = [pltpu.with_memory_space_constraint(x, pltpu.HBM) for x in (b, c)]
+    own, faces = shape(16, 64, 128), shape(2, 16, 4, 128)
+    se, so = call(
+        pack_kernel,
+        (faces, faces),
+        [(2, 16, 8, 128), (2, 16, 8, 128), pltpu.SemaphoreType.DMA((4,))],
+        b, c,
+        specs=[hbm, hbm],
+    )
+    ye = lax.ppermute(se, "agg", side_in)
+    yo = lax.ppermute(so, "agg", side_out)
+    b, c = call(
+        load_kernel,
+        (own, own),
+        [pltpu.SemaphoreType.DMA((8,))],
+        b, c,
+        specs=[hbm, hbm],
+    )
+
+    big, mid = (16, 96, 128), (12, 40, 128)
+    p0, v, w, b1, c1, edge, se, so = call(
         lambda *refs: head_kernel(aggs, *refs),
-        (shape(16, 80, 128), shape(*own), shape(*own), shape(8, 40, 128), shape(8, 40, 128),
-         shape(6, 80, 128), shape(9, 40, 128), shape(9, 40, 128)),
-        [big] * 5 + [(8, 96, 128), (8, 80, 128)],
+        (shape(16, 80, 128), shape(*big), shape(*big), shape(8, 40, 128), shape(8, 40, 128),
+         shape(6, 80, 128), shape(336, 128), shape(336, 128)),
+        [big] * 3 + [(8, 96, 128), (8, 80, 128)],
         at, b, c, ye, yo,
     )
     xe = lax.ppermute(se, "blk", near_in)
@@ -427,14 +472,14 @@
     pe, e1, w1, bc2, se, so = call(
         lambda *refs: mid_kernel(blocks, aggs, *refs),
         (shape(4, 80, 128), shape(*mid), shape(*mid), shape(6, 16, 128), shape(6, 8, 128), shape(6, 8, 128)),
-        [(4, 96, 128), (4, 80, 128), tall, tall, tall, (6, 40, 128), (6, 40, 128)],
+        [(6, 80, 128), (4, 96, 128), (4, 80, 128), tall, tall, tall, (6, 40, 128), (6, 40, 128)],
         at, b1, c1, edge, xe, xo,
     )
     ye = lax.ppermute(se, "agg", side_in)
     yo = lax.ppermute(so, "agg", side_out)
     wide, se, so = call(
         join_kernel,
-        (shape(6, 32, 128), shape(5, 32, 128), shape(5, 32, 128)),
+        (shape(6, 32, 128), shape(3, 32, 128), shape(3, 32, 128)),
         [],
         at, bc2, ye, yo,
     )
@@ -443,9 +488,9 @@
     small = (14, 32, 128)
     (out,) = call(
         lambda *refs: up_kernel(blocks, aggs, *refs),
-        (shape(*own),),
-        [small] * 5 + [(6, 48, 128), (6, 32, 128), (14, 48, 128), (6, 32, 128), mid, (12, 56, 128), (20, 96, 128)],
-        at, p0, pe, vown, wown, e1, w1, wide, ye, yo, xe, xo,
+        (own,),
+        [small] * 4 + [(6, 48, 128), (6, 32, 128), (14, 48, 128), (6, 32, 128), mid, (12, 56, 128), (20, 96, 128)],
+        at, p0, pe, v, w, e1, w1, wide, ye, yo, xe, xo,
     )
     return out
 

time: 39.9 us -> 37.2 us (0.932)
  waiting for transfers between devices: 11 us -> 8.74 us
  local copies, waits for them, and re-layouts: 2.06 us -> 0 us
  Pallas kernels: 8.42 us -> 9.83 us
    ppermute x1 -> x2, starting transfers between devices: 3.67 us -> 6.5 us  [shards(): yo = lax.ppermute(so, 'agg', side_out)]
    ppermute x2 -> x0, starting transfers between devices: 2.65 us -> none  [the longest x1 2.64 us: shards(): yo = lax.ppermute(jnp.where(y_even, first, last), 'agg', side_out)]
    ppermute x2 -> x0, waiting for transfers between devices: 2.26 us -> none  [the longest x1 2.26 us: shards(): yo = lax.ppermute(jnp.where(y_even, first, last), 'agg', side_out)]
    pallas_call x4 -> x6, Pallas kernels: 8.42 us -> 9.83 us  [call(): pl.pallas_call(body, out_shape=outs, in_specs=specs or [SM] + [VM] * (len...]
    unnamed x4 -> x0, local copies, waits for them, and re-layouts: 1.04 us -> none
    another operation x1 -> x0, local copies, waits for them, and re-layouts: 1.02 us -> none  [shards(): last = jnp.stack([b[:, 60:], c[:, 60:]])]
    ppermute x1 -> x2, waiting for transfers between devices: 1.52 us -> 2.02 us  [shards(): yo = lax.ppermute(so, 'agg', side_out)]
    ppermute x2, waiting for transfers between devices: 7.18 us -> 6.7 us  [shards(): xo = lax.ppermute(so, 'blk', near_out)]
  transfers between devices with their start and end apart: 8 -> 8, of which waited for: 4 -> 4; matrix products, arithmetic and copies ran while one was open for 0% -> 0% of each run, Pallas kernels for 0% -> 4%
where the time goes in v6:
time: 37.2 us; the launch traced here: 37 us
  starting transfers between devices  18.3 us (49%)
  Pallas kernels  9.83 us (26%)
  waiting for transfers between devices  8.74 us (23%)
    pallas_call x6, Pallas kernels, call(): pl.pallas_call(body, out_shape=outs, in_specs=specs or [SM] + [VM] * (len...  9.83 us
    ppermute x2, starting transfers between devices, shards(): xo = lax.ppermute(so, 'blk', near_out)  9.52 us
    ppermute x2, waiting for transfers between devices, shards(): xo = lax.ppermute(so, 'blk', near_out)  6.7 us
    ppermute x2, starting transfers between devices, shards(): yo = lax.ppermute(so, 'agg', side_out)  6.5 us
    ppermute x2, starting transfers between devices, shards(): xe = lax.ppermute(se, 'blk', near_in)  2.08 us
    ppermute x2, waiting for transfers between devices, shards(): yo = lax.ppermute(so, 'agg', side_out)  2.02 us
  transfers between devices with their start and end apart: 8, of which 4 were waited for; matrix products, arithmetic and copies ran while one was open for 0% of the time, Pallas kernels for 4%

profile of v6, /device:TPU:0, one launch (start us, length us, event | category | flops | bytes accessed | tf_op | source)
XLA Modules:
  0.0 37.0 jit_solution(3395116730504844350)
XLA Ops:
  0.0 1.0 %shard_map.29 = (f32[2,16,4,128]{3,2,1,0:T(4,128)S(1)}, f32[2,16,4,128]{3,2,1,0:T(4,128)S(1)}) custom-call(f32[16,64,128]{2,1,0:T(8,128)} %b.3, f32[16,64,128]{2,1,0:T(8,128)} %c.3), custom_call_target="tpu_custom_call" | custom-call | tf_op jit(solution)/shard_map/pallas_call | solution.py:21
  1.0 0.1 collective-permute-start
  1.1 3.2 %collective-permute-start.1 = (f32[2,16,4,128]{3,2,1,0:T(4,128)S(1)}, f32[2,16,4,128]{3,2,1,0:T(4,128)S(1)}, u32[]{:S(2)}, u32[]{:S(2)}) collective-permute-start(f32[2,16,4,128]{3,2,1,0:T(4,128)S(1)} %get-tuple-element.29), channel_id=1, source_target_pairs={{0,112},{16,32},{32,16},{48,64},{64,48},{80,96},{96,80},{112,0},{1... | collective-permute-start | bytes 196616 | tf_op jit(solution)/shard_map/ppermute | solution.py:452
  4.3 1.3 %shard_map.28 = (f32[16,64,128]{2,1,0:T(8,128)S(1)}, f32[16,64,128]{2,1,0:T(8,128)S(1)}) custom-call(f32[16,64,128]{2,1,0:T(8,128)} %b.3, f32[16,64,128]{2,1,0:T(8,128)} %c.3), custom_call_target="tpu_custom_call" | custom-call | tf_op jit(solution)/shard_map/pallas_call | solution.py:21
  5.7 0.1 pad_add_fusion.refs_0_.at
  5.8 0.0 collective-permute-done.refs_3_
  5.8 0.5 %collective-permute-done.1.refs_4_ = f32[2,16,4,128]{3,2,1,0:T(4,128)S(1)} collective-permute-done((f32[2,16,4,128]{3,2,1,0:T(4,128)S(1)}, f32[2,16,4,128]{3,2,1,0:T(4,128)S(1)}, u32[]{:S(2)}, u32[]{:S(2)}) %collective-permute-start.1) | collective-permute-done | bytes 65568 | tf_op jit(solution)/shard_map/ppermute | solution.py:452
  6.3 2.0 %shard_map.30 = (f32[16,80,128]{2,1,0:T(8,128)S(1)}, f32[16,96,128]{2,1,0:T(8,128)S(1)}, f32[16,96,128]{2,1,0:T(8,128)S(1)}, f32[8,40,128]{2,1,0:T(8,128)S(1)}, ...) custom-call(s32[2]{0:T(128)S(1)} %pad_add_fusion.refs_0_.at, ...), custom_call_target="tpu_custom_call" | custom-call | tf_op jit(solution)/shard_map/pallas_call | solution.py:21
  8.3 2.0 %collective-permute-start.2 = (f32[336,128]{1,0:T(8,128)S(1)}, f32[336,128]{1,0:T(8,128)S(1)}, u32[]{:S(2)}, u32[]{:S(2)}) collective-permute-start(f32[336,128]{1,0:T(8,128)S(1)} %get-tuple-element.34), channel_id=1, source_target_pairs={{0,1},{1,0},{2,3},{3,2},{4,5},{5,4},{6,7},{7,6},{8,9},{9,8},{10,11... | collective-permute-start | bytes 516104 | tf_op jit(solution)/shard_map/ppermute | solution.py:469
  10.3 4.7 %collective-permute-start.3 = (f32[336,128]{1,0:T(8,128)S(1)}, f32[336,128]{1,0:T(8,128)S(1)}, u32[]{:S(2)}, u32[]{:S(2)}) collective-permute-start(f32[336,128]{1,0:T(8,128)S(1)} %get-tuple-element.35), channel_id=1, source_target_pairs={{0,15},{1,2},{2,1},{3,4},{4,3},{5,6},{6,5},{7,8},{8,7},{9,10},{10,... | collective-permute-start | bytes 516104 | tf_op jit(solution)/shard_map/ppermute | solution.py:470
  15.0 0.0 collective-permute-done.2.refs_4_
  15.0 4.0 %collective-permute-done.3.refs_5_ = f32[336,128]{1,0:T(8,128)S(1)} collective-permute-done((f32[336,128]{1,0:T(8,128)S(1)}, f32[336,128]{1,0:T(8,128)S(1)}, u32[]{:S(2)}, u32[]{:S(2)}) %collective-permute-start.3) | collective-permute-done | bytes 172064 | tf_op jit(solution)/shard_map/ppermute | solution.py:470
  19.0 1.1 %shard_map.31 = (f32[4,80,128]{2,1,0:T(8,128)S(1)}, f32[12,40,128]{2,1,0:T(8,128)S(1)}, f32[12,40,128]{2,1,0:T(8,128)S(1)}, f32[6,16,128]{2,1,0:T(8,128)S(1)}, f...) custom-call(s32[2]{0:T(128)S(1)} %pad_add_fusion.refs_0_.at, f32[8,40,128]{2,1,0:T(8,128)S(1)} %get-tuple-element.31.refs_1_, ...), custom_call_target="tpu_custom_call" | custom-call | tf_op jit(solution)/shard_map/pallas_call | solution.py:21
  20.1 0.1 collective-permute-start.4
  20.2 3.3 %collective-permute-start.5 = (f32[6,8,128]{2,1,0:T(8,128)S(1)}, f32[6,8,128]{2,1,0:T(8,128)S(1)}, u32[]{:S(2)}, u32[]{:S(2)}) collective-permute-start(f32[6,8,128]{2,1,0:T(8,128)S(1)} %get-tuple-element.43), channel_id=1, source_target_pairs={{0,112},{16,32},{32,16},{48,64},{64,48},{80,96},{96,80},{112,0},{1... | collective-permute-start | bytes 73736 | tf_op jit(solution)/shard_map/ppermute | solution.py:479
  23.5 0.0 collective-permute-done.4.ye.refs_8_
  23.5 1.5 %collective-permute-done.5.yo.refs_9_ = f32[6,8,128]{2,1,0:T(8,128)S(1)} collective-permute-done((f32[6,8,128]{2,1,0:T(8,128)S(1)}, f32[6,8,128]{2,1,0:T(8,128)S(1)}, u32[]{:S(2)}, u32[]{:S(2)}) %collective-permute-start.5) | collective-permute-done | bytes 24608 | tf_op jit(solution)/shard_map/ppermute | solution.py:479
  25.0 0.6 %shard_map.32 = (f32[6,32,128]{2,1,0:T(8,128)S(1)}, f32[3,32,128]{2,1,0:T(8,128)S(1)}, f32[3,32,128]{2,1,0:T(8,128)S(1)}) custom-call(s32[2]{0:T(128)S(1)} %pad_add_fusion.refs_0_.at, f32[6,16,128]{2,1,0:T(8,128)S(1)} %get-tuple-element.41.bc2, f32[6,8,128]{2,1,0:T(8,128)S(1)} %collective-permute-done.4.ye.refs_8_, ...), custom_call_target="tpu_custom_call" | custom-call | tf_op jit(solution)/shard_map/pallas_call | solution.py:21
  25.6 0.1 collective-permute-start.6
  25.7 4.8 %collective-permute-start.7 = (f32[3,32,128]{2,1,0:T(8,128)S(1)}, f32[3,32,128]{2,1,0:T(8,128)S(1)}, u32[]{:S(2)}, u32[]{:S(2)}) collective-permute-start(f32[3,32,128]{2,1,0:T(8,128)S(1)} %get-tuple-element.46), channel_id=1, source_target_pairs={{0,15},{1,2},{2,1},{3,4},{4,3},{5,6},{6,5},{7,8},{8,7},{9,10},{10,... | collective-permute-start | bytes 147464 | tf_op jit(solution)/shard_map/ppermute | solution.py:487
  30.5 0.0 collective-permute-done.6.refs_10_
  30.5 2.7 %collective-permute-done.7.refs_11_ = f32[3,32,128]{2,1,0:T(8,128)S(1)} collective-permute-done((f32[3,32,128]{2,1,0:T(8,128)S(1)}, f32[3,32,128]{2,1,0:T(8,128)S(1)}, u32[]{:S(2)}, u32[]{:S(2)}) %collective-permute-start.7) | collective-permute-done | bytes 49184 | tf_op jit(solution)/shard_map/ppermute | solution.py:487
  33.2 3.8 %shard_map.33 = f32[16,64,128]{2,1,0:T(8,128)} custom-call(s32[2]{0:T(128)S(1)} %pad_add_fusion.refs_0_.at, f32[16,80,128]{2,1,0:T(8,128)S(1)} %get-tuple-element.30.refs_1_, f32[4,80,128]{2,1,0:T(8,128)S(1)} %get-tuple-element.36.refs_2_, f32[16,96,128]{2,1,0:T(8,128)S(1)} %get-tuple-element.37.refs_3_, f32[16,96,128]{2,1,0:T(8,128)S(1)} %get-tuple-element.38.refs_4_, ...), custom_call_target="tpu_custom_call" | custom-call | tf_op jit(solution)/shard_map/pallas_call | solution.py:21
Async XLA Ops:
  1.0 4.8 %collective-permute-start = (f32[2,16,4,128]{3,2,1,0:T(4,128)S(1)}, f32[2,16,4,128]{3,2,1,0:T(4,128)S(1)}, u32[]{:S(2)}, u32[]{:S(2)}) collective-permute-start(f32[2,16,4,128]{3,2,1,0:T(4,128)S(1)} %get-tuple-element.28), channel_id=1, source_target_pairs={{0,16},{16,0},{32,48},{48,32},{64,80},{80,64},{96,112},{112,96},{1... | collective-permute-start | bytes 196616 | tf_op jit(solution)/shard_map/ppermute | solution.py:451
  1.1 5.2 %collective-permute-start.1 = (f32[2,16,4,128]{3,2,1,0:T(4,128)S(1)}, f32[2,16,4,128]{3,2,1,0:T(4,128)S(1)}, u32[]{:S(2)}, u32[]{:S(2)}) collective-permute-start(f32[2,16,4,128]{3,2,1,0:T(4,128)S(1)} %get-tuple-element.29), channel_id=1, source_target_pairs={{0,112},{16,32},{32,16},{48,64},{64,48},{80,96},{96,80},{112,0},{1... | collective-permute-start | bytes 196616 | tf_op jit(solution)/shard_map/ppermute | solution.py:452
  8.3 6.7 %collective-permute-start.2 = (f32[336,128]{1,0:T(8,128)S(1)}, f32[336,128]{1,0:T(8,128)S(1)}, u32[]{:S(2)}, u32[]{:S(2)}) collective-permute-start(f32[336,128]{1,0:T(8,128)S(1)} %get-tuple-element.34), channel_id=1, source_target_pairs={{0,1},{1,0},{2,3},{3,2},{4,5},{5,4},{6,7},{7,6},{8,9},{9,8},{10,11... | collective-permute-start | bytes 516104 | tf_op jit(solution)/shard_map/ppermute | solution.py:469
  10.3 8.7 %collective-permute-start.3 = (f32[336,128]{1,0:T(8,128)S(1)}, f32[336,128]{1,0:T(8,128)S(1)}, u32[]{:S(2)}, u32[]{:S(2)}) collective-permute-start(f32[336,128]{1,0:T(8,128)S(1)} %get-tuple-element.35), channel_id=1, source_target_pairs={{0,15},{1,2},{2,1},{3,4},{4,3},{5,6},{6,5},{7,8},{8,7},{9,10},{10,... | collective-permute-start | bytes 516104 | tf_op jit(solution)/shard_map/ppermute | solution.py:470
  20.1 3.4 %collective-permute-start.4 = (f32[6,8,128]{2,1,0:T(8,128)S(1)}, f32[6,8,128]{2,1,0:T(8,128)S(1)}, u32[]{:S(2)}, u32[]{:S(2)}) collective-permute-start(f32[6,8,128]{2,1,0:T(8,128)S(1)} %get-tuple-element.42), channel_id=1, source_target_pairs={{0,16},{16,0},{32,48},{48,32},{64,80},{80,64},{96,112},{112,96},{1... | collective-permute-start | bytes 73736 | tf_op jit(solution)/shard_map/ppermute | solution.py:478
  20.2 4.8 %collective-permute-start.5 = (f32[6,8,128]{2,1,0:T(8,128)S(1)}, f32[6,8,128]{2,1,0:T(8,128)S(1)}, u32[]{:S(2)}, u32[]{:S(2)}) collective-permute-start(f32[6,8,128]{2,1,0:T(8,128)S(1)} %get-tuple-element.43), channel_id=1, source_target_pairs={{0,112},{16,32},{32,16},{48,64},{64,48},{80,96},{96,80},{112,0},{1... | collective-permute-start | bytes 73736 | tf_op jit(solution)/shard_map/ppermute | solution.py:479
  25.6 4.9 %collective-permute-start.6 = (f32[3,32,128]{2,1,0:T(8,128)S(1)}, f32[3,32,128]{2,1,0:T(8,128)S(1)}, u32[]{:S(2)}, u32[]{:S(2)}) collective-permute-start(f32[3,32,128]{2,1,0:T(8,128)S(1)} %get-tuple-element.45), channel_id=1, source_target_pairs={{0,1},{1,0},{2,3},{3,2},{4,5},{5,4},{6,7},{7,6},{8,9},{9,8},{10,11... | collective-permute-start | bytes 147464 | tf_op jit(solution)/shard_map/ppermute | solution.py:486
  25.7 7.5 %collective-permute-start.7 = (f32[3,32,128]{2,1,0:T(8,128)S(1)}, f32[3,32,128]{2,1,0:T(8,128)S(1)}, u32[]{:S(2)}, u32[]{:S(2)}) collective-permute-start(f32[3,32,128]{2,1,0:T(8,128)S(1)} %get-tuple-element.46), channel_id=1, source_target_pairs={{0,15},{1,2},{2,1},{3,4},{4,3},{5,6},{6,5},{7,8},{8,7},{9,10},{10,... | collective-permute-start | bytes 147464 | tf_op jit(solution)/shard_map/ppermute | solution.py:487

commit v7 on v6

--- a/solution.py
+++ b/solution.py
@@ -10,7 +10,6 @@
 WINDOW = 64
 STEPS = (4, 7, 3, 2, 4)
 VM = pl.BlockSpec(memory_space=pltpu.VMEM)
-SM = pl.BlockSpec(memory_space=pltpu.SMEM)
 
 
 def shape(*dims):
@@ -21,7 +20,7 @@
     return pl.pallas_call(
         body,
         out_shape=outs,
-        in_specs=specs or [SM] + [VM] * (len(args) - 1),
+        in_specs=specs or [VM] * len(args),
         out_specs=tuple(VM for _ in outs),
         scratch_shapes=[pltpu.VMEM(s, F32) if isinstance(s, tuple) else s for s in scratch],
         compiler_params=pltpu.CompilerParams(vmem_limit_bytes=16 << 20),
@@ -133,11 +132,11 @@
 
 def head_kernel(
     aggs,
-    at, b, c, ye, yo,
+    b, c, ye, yo,
     p0, v, w, b1, c1, edge, se, so,
     q, bx, cx, own1, rest1,
 ):
-    bi, ai = at[0], at[1]
+    bi, ai = lax.axis_index("blk"), lax.axis_index("agg")
     x_even, y_even = (bi & 1) == 0, (ai & 1) == 0
     y_lo = jnp.where(ai > 0, OMEGA, 0.0)
     y_hi = jnp.where(ai < aggs - 1, OMEGA, 0.0)
@@ -212,11 +211,11 @@
 
 def mid_kernel(
     blocks, aggs,
-    at, b1in, c1in, edge, xe, xo,
+    b1in, c1in, edge, xe, xo,
     pe, e1out, w1out, bc2, se, so,
     far, s4, r4, b1, c1, e1, own2, rest2,
 ):
-    bi, ai = at[0], at[1]
+    bi, ai = lax.axis_index("blk"), lax.axis_index("agg")
     x_even, y_even = (bi & 1) == 0, (ai & 1) == 0
     pairs, sides = pick("pairs"), pick("beside")
     has_lo, has_hi = bi > 0, bi < blocks - 1
@@ -293,8 +292,8 @@
             ref[k, 7:8] = jnp.zeros((1, 128), F32)
 
 
-def join_kernel(at, bc2, ye, yo, wide, se, so):
-    bi, ai = at[0], at[1]
+def join_kernel(bc2, ye, yo, wide, se, so):
+    bi, ai = lax.axis_index("blk"), lax.axis_index("agg")
     x_even, y_even = (bi & 1) == 0, (ai & 1) == 0
     for k in range(6):
         wide[k] = jnp.zeros((32, 128), F32)
@@ -311,11 +310,11 @@
 
 def up_kernel(
     blocks, aggs,
-    at, p0, pe, v0, w0, e1in, w1, wide, ye, yo, xe, xo,
+    p0, pe, v0, w0, e1in, w1, wide, ye, yo, xe, xo,
     out,
     e2, w2, b2, c2, own2, rest2, m2, t2, e1, m1, mf,
 ):
-    bi, ai = at[0], at[1]
+    bi, ai = lax.axis_index("blk"), lax.axis_index("agg")
     x_even, y_even = (bi & 1) == 0, (ai & 1) == 0
     pairs, sides, copies = pick("pairs"), pick("beside"), pick("copies")
 
@@ -433,8 +432,6 @@
 
 def shards(b, c):
     blocks, aggs = lax.axis_size("blk"), lax.axis_size("agg")
-    bi, ai = lax.axis_index("blk"), lax.axis_index("agg")
-    at = jnp.stack([bi, ai]).astype(jnp.int32)
     near_in, near_out = swaps(blocks, 1)
     side_in, side_out = swaps(aggs, 1)
 
@@ -464,7 +461,7 @@
         (shape(16, 80, 128), shape(*big), shape(*big), shape(8, 40, 128), shape(8, 40, 128),
          shape(6, 80, 128), shape(336, 128), shape(336, 128)),
         [big] * 3 + [(8, 96, 128), (8, 80, 128)],
-        at, b, c, ye, yo,
+        b, c, ye, yo,
     )
     xe = lax.ppermute(se, "blk", near_in)
     xo = lax.ppermute(so, "blk", near_out)
@@ -473,7 +470,7 @@
         lambda *refs: mid_kernel(blocks, aggs, *refs),
         (shape(4, 80, 128), shape(*mid), shape(*mid), shape(6, 16, 128), shape(6, 8, 128), shape(6, 8, 128)),
         [(6, 80, 128), (4, 96, 128), (4, 80, 128), tall, tall, tall, (6, 40, 128), (6, 40, 128)],
-        at, b1, c1, edge, xe, xo,
+        b1, c1, edge, xe, xo,
     )
     ye = lax.ppermute(se, "agg", side_in)
     yo = lax.ppermute(so, "agg", side_out)
@@ -481,7 +478,7 @@
         join_kernel,
         (shape(6, 32, 128), shape(3, 32, 128), shape(3, 32, 128)),
         [],
-        at, bc2, ye, yo,
+        bc2, ye, yo,
     )
     xe = lax.ppermute(se, "blk", near_in)
     xo = lax.ppermute(so, "blk", near_out)
@@ -490,7 +487,7 @@
         lambda *refs: up_kernel(blocks, aggs, *refs),
         (own,),
         [small] * 4 + [(6, 48, 128), (6, 32, 128), (14, 48, 128), (6, 32, 128), mid, (12, 56, 128), (20, 96, 128)],
-        at, p0, pe, v, w, e1, w1, wide, ye, yo, xe, xo,
+        p0, pe, v, w, e1, w1, wide, ye, yo, xe, xo,
     )
     return out
 

time: 37.2 us -> 34.9 us (0.938)
  Pallas kernels: 9.83 us -> 7.61 us
    pallas_call x6, Pallas kernels: 9.83 us -> 7.61 us  [call(): pl.pallas_call(body, out_shape=outs, in_specs=specs or [VM] * len(args),...]
where the time goes in v7:
time: 34.9 us; the launch traced here: 34.8 us
  starting transfers between devices  18.3 us (52%)
  waiting for transfers between devices  8.81 us (25%)
  Pallas kernels  7.61 us (22%)
    ppermute x2, starting transfers between devices, shards(): xo = lax.ppermute(so, 'blk', near_out)  9.52 us
    pallas_call x6, Pallas kernels, call(): pl.pallas_call(body, out_shape=outs, in_specs=specs or [VM] * len(args),...  7.61 us
    ppermute x2, waiting for transfers between devices, shards(): xo = lax.ppermute(so, 'blk', near_out)  6.7 us
    ppermute x2, starting transfers between devices, shards(): yo = lax.ppermute(so, 'agg', side_out)  6.5 us
    ppermute x2, waiting for transfers between devices, shards(): yo = lax.ppermute(so, 'agg', side_out)  2.1 us
    ppermute x2, starting transfers between devices, shards(): xe = lax.ppermute(se, 'blk', near_in)  2.08 us
  transfers between devices with their start and end apart: 8, of which 4 were waited for; matrix products, arithmetic and copies ran while one was open for 0% of the time, Pallas kernels for 4%

profile of v7, /device:TPU:0, one launch (start us, length us, event | category | flops | bytes accessed | tf_op | source)
XLA Modules:
  0.0 34.8 jit_solution(3761720727887865912)
XLA Ops:
  0.0 1.0 %shard_map.29 = (f32[2,16,4,128]{3,2,1,0:T(4,128)S(1)}, f32[2,16,4,128]{3,2,1,0:T(4,128)S(1)}) custom-call(f32[16,64,128]{2,1,0:T(8,128)} %b.3, f32[16,64,128]{2,1,0:T(8,128)} %c.3), custom_call_target="tpu_custom_call" | custom-call | tf_op jit(solution)/shard_map/pallas_call | solution.py:20
  1.0 0.1 collective-permute-start
  1.1 3.2 %collective-permute-start.1 = (f32[2,16,4,128]{3,2,1,0:T(4,128)S(1)}, f32[2,16,4,128]{3,2,1,0:T(4,128)S(1)}, u32[]{:S(2)}, u32[]{:S(2)}) collective-permute-start(f32[2,16,4,128]{3,2,1,0:T(4,128)S(1)} %get-tuple-element.29), channel_id=1, source_target_pairs={{0,112},{16,32},{32,16},{48,64},{64,48},{80,96},{96,80},{112,0},{1... | collective-permute-start | bytes 196616 | tf_op jit(solution)/shard_map/ppermute | solution.py:449
  4.3 1.3 %shard_map.28 = (f32[16,64,128]{2,1,0:T(8,128)S(1)}, f32[16,64,128]{2,1,0:T(8,128)S(1)}) custom-call(f32[16,64,128]{2,1,0:T(8,128)} %b.3, f32[16,64,128]{2,1,0:T(8,128)} %c.3), custom_call_target="tpu_custom_call" | custom-call | tf_op jit(solution)/shard_map/pallas_call | solution.py:20
  5.7 0.0 collective-permute-done.refs_2_
  5.7 0.6 %collective-permute-done.1.refs_3_ = f32[2,16,4,128]{3,2,1,0:T(4,128)S(1)} collective-permute-done((f32[2,16,4,128]{3,2,1,0:T(4,128)S(1)}, f32[2,16,4,128]{3,2,1,0:T(4,128)S(1)}, u32[]{:S(2)}, u32[]{:S(2)}) %collective-permute-start.1) | collective-permute-done | bytes 65568 | tf_op jit(solution)/shard_map/ppermute | solution.py:449
  6.3 1.4 %shard_map.30 = (f32[16,80,128]{2,1,0:T(8,128)S(1)}, f32[16,96,128]{2,1,0:T(8,128)S(1)}, f32[16,96,128]{2,1,0:T(8,128)S(1)}, f32[8,40,128]{2,1,0:T(8,128)S(1)}, ...) custom-call(f32[16,64,128]{2,1,0:T(8,128)S(1)} %get-tuple-element.26.ref, ...), custom_call_target="tpu_custom_call" | custom-call | tf_op jit(solution)/shard_map/pallas_call | solution.py:20
  7.7 2.0 %collective-permute-start.2 = (f32[336,128]{1,0:T(8,128)S(1)}, f32[336,128]{1,0:T(8,128)S(1)}, u32[]{:S(2)}, u32[]{:S(2)}) collective-permute-start(f32[336,128]{1,0:T(8,128)S(1)} %get-tuple-element.34), channel_id=1, source_target_pairs={{0,1},{1,0},{2,3},{3,2},{4,5},{5,4},{6,7},{7,6},{8,9},{9,8},{10,11... | collective-permute-start | bytes 516104 | tf_op jit(solution)/shard_map/ppermute | solution.py:466
  9.7 4.7 %collective-permute-start.3 = (f32[336,128]{1,0:T(8,128)S(1)}, f32[336,128]{1,0:T(8,128)S(1)}, u32[]{:S(2)}, u32[]{:S(2)}) collective-permute-start(f32[336,128]{1,0:T(8,128)S(1)} %get-tuple-element.35), channel_id=1, source_target_pairs={{0,15},{1,2},{2,1},{3,4},{4,3},{5,6},{6,5},{7,8},{8,7},{9,10},{10,... | collective-permute-start | bytes 516104 | tf_op jit(solution)/shard_map/ppermute | solution.py:467
  14.4 0.0 collective-permute-done.2.refs_3_
  14.4 4.0 %collective-permute-done.3.refs_4_ = f32[336,128]{1,0:T(8,128)S(1)} collective-permute-done((f32[336,128]{1,0:T(8,128)S(1)}, f32[336,128]{1,0:T(8,128)S(1)}, u32[]{:S(2)}, u32[]{:S(2)}) %collective-permute-start.3) | collective-permute-done | bytes 172064 | tf_op jit(solution)/shard_map/ppermute | solution.py:467
  18.4 0.6 %shard_map.31 = (f32[4,80,128]{2,1,0:T(8,128)S(1)}, f32[12,40,128]{2,1,0:T(8,128)S(1)}, f32[12,40,128]{2,1,0:T(8,128)S(1)}, f32[6,16,128]{2,1,0:T(8,128)S(1)}, f...) custom-call(f32[8,40,128]{2,1,0:T(8,128)S(1)} %get-tuple-element.31.refs_0_, ...), custom_call_target="tpu_custom_call" | custom-call | tf_op jit(solution)/shard_map/pallas_call | solution.py:20
  19.0 0.1 collective-permute-start.4
  19.1 3.3 %collective-permute-start.5 = (f32[6,8,128]{2,1,0:T(8,128)S(1)}, f32[6,8,128]{2,1,0:T(8,128)S(1)}, u32[]{:S(2)}, u32[]{:S(2)}) collective-permute-start(f32[6,8,128]{2,1,0:T(8,128)S(1)} %get-tuple-element.43), channel_id=1, source_target_pairs={{0,112},{16,32},{32,16},{48,64},{64,48},{80,96},{96,80},{112,0},{1... | collective-permute-start | bytes 73736 | tf_op jit(solution)/shard_map/ppermute | solution.py:476
  22.4 0.0 collective-permute-done.4.ye.refs_7_
  22.4 1.5 %collective-permute-done.5.yo.refs_8_ = f32[6,8,128]{2,1,0:T(8,128)S(1)} collective-permute-done((f32[6,8,128]{2,1,0:T(8,128)S(1)}, f32[6,8,128]{2,1,0:T(8,128)S(1)}, u32[]{:S(2)}, u32[]{:S(2)}) %collective-permute-start.5) | collective-permute-done | bytes 24608 | tf_op jit(solution)/shard_map/ppermute | solution.py:476
  23.9 0.1 shard_map.32
  24.0 0.1 collective-permute-start.6
  24.1 4.8 %collective-permute-start.7 = (f32[3,32,128]{2,1,0:T(8,128)S(1)}, f32[3,32,128]{2,1,0:T(8,128)S(1)}, u32[]{:S(2)}, u32[]{:S(2)}) collective-permute-start(f32[3,32,128]{2,1,0:T(8,128)S(1)} %get-tuple-element.46), channel_id=1, source_target_pairs={{0,15},{1,2},{2,1},{3,4},{4,3},{5,6},{6,5},{7,8},{8,7},{9,10},{10,... | collective-permute-start | bytes 147464 | tf_op jit(solution)/shard_map/ppermute | solution.py:484
  28.9 0.0 collective-permute-done.6.refs_9_
  28.9 2.7 %collective-permute-done.7.refs_10_ = f32[3,32,128]{2,1,0:T(8,128)S(1)} collective-permute-done((f32[3,32,128]{2,1,0:T(8,128)S(1)}, f32[3,32,128]{2,1,0:T(8,128)S(1)}, u32[]{:S(2)}, u32[]{:S(2)}) %collective-permute-start.7) | collective-permute-done | bytes 49184 | tf_op jit(solution)/shard_map/ppermute | solution.py:484
  31.6 3.2 %shard_map.33 = f32[16,64,128]{2,1,0:T(8,128)} custom-call(f32[16,80,128]{2,1,0:T(8,128)S(1)} %get-tuple-element.30.refs_0_, f32[4,80,128]{2,1,0:T(8,128)S(1)} %get-tuple-element.36.refs_1_, f32[16,96,128]{2,1,0:T(8,128)S(1)} %get-tuple-element.37.refs_2_, f32[16,96,128]{2,1,0:T(8,128)S(1)} %get-tuple-element.38.refs_3_, ...), custom_call_target="tpu_custom_call" | custom-call | tf_op jit(solution)/shard_map/pallas_call | solution.py:20
Async XLA Ops:
  1.0 4.7 %collective-permute-start = (f32[2,16,4,128]{3,2,1,0:T(4,128)S(1)}, f32[2,16,4,128]{3,2,1,0:T(4,128)S(1)}, u32[]{:S(2)}, u32[]{:S(2)}) collective-permute-start(f32[2,16,4,128]{3,2,1,0:T(4,128)S(1)} %get-tuple-element.28), channel_id=1, source_target_pairs={{0,16},{16,0},{32,48},{48,32},{64,80},{80,64},{96,112},{112,96},{1... | collective-permute-start | bytes 196616 | tf_op jit(solution)/shard_map/ppermute | solution.py:448
  1.1 5.2 %collective-permute-start.1 = (f32[2,16,4,128]{3,2,1,0:T(4,128)S(1)}, f32[2,16,4,128]{3,2,1,0:T(4,128)S(1)}, u32[]{:S(2)}, u32[]{:S(2)}) collective-permute-start(f32[2,16,4,128]{3,2,1,0:T(4,128)S(1)} %get-tuple-element.29), channel_id=1, source_target_pairs={{0,112},{16,32},{32,16},{48,64},{64,48},{80,96},{96,80},{112,0},{1... | collective-permute-start | bytes 196616 | tf_op jit(solution)/shard_map/ppermute | solution.py:449
  7.7 6.7 %collective-permute-start.2 = (f32[336,128]{1,0:T(8,128)S(1)}, f32[336,128]{1,0:T(8,128)S(1)}, u32[]{:S(2)}, u32[]{:S(2)}) collective-permute-start(f32[336,128]{1,0:T(8,128)S(1)} %get-tuple-element.34), channel_id=1, source_target_pairs={{0,1},{1,0},{2,3},{3,2},{4,5},{5,4},{6,7},{7,6},{8,9},{9,8},{10,11... | collective-permute-start | bytes 516104 | tf_op jit(solution)/shard_map/ppermute | solution.py:466
  9.7 8.7 %collective-permute-start.3 = (f32[336,128]{1,0:T(8,128)S(1)}, f32[336,128]{1,0:T(8,128)S(1)}, u32[]{:S(2)}, u32[]{:S(2)}) collective-permute-start(f32[336,128]{1,0:T(8,128)S(1)} %get-tuple-element.35), channel_id=1, source_target_pairs={{0,15},{1,2},{2,1},{3,4},{4,3},{5,6},{6,5},{7,8},{8,7},{9,10},{10,... | collective-permute-start | bytes 516104 | tf_op jit(solution)/shard_map/ppermute | solution.py:467
  19.0 3.4 %collective-permute-start.4 = (f32[6,8,128]{2,1,0:T(8,128)S(1)}, f32[6,8,128]{2,1,0:T(8,128)S(1)}, u32[]{:S(2)}, u32[]{:S(2)}) collective-permute-start(f32[6,8,128]{2,1,0:T(8,128)S(1)} %get-tuple-element.42), channel_id=1, source_target_pairs={{0,16},{16,0},{32,48},{48,32},{64,80},{80,64},{96,112},{112,96},{1... | collective-permute-start | bytes 73736 | tf_op jit(solution)/shard_map/ppermute | solution.py:475
  19.1 4.8 %collective-permute-start.5 = (f32[6,8,128]{2,1,0:T(8,128)S(1)}, f32[6,8,128]{2,1,0:T(8,128)S(1)}, u32[]{:S(2)}, u32[]{:S(2)}) collective-permute-start(f32[6,8,128]{2,1,0:T(8,128)S(1)} %get-tuple-element.43), channel_id=1, source_target_pairs={{0,112},{16,32},{32,16},{48,64},{64,48},{80,96},{96,80},{112,0},{1... | collective-permute-start | bytes 73736 | tf_op jit(solution)/shard_map/ppermute | solution.py:476
  24.0 4.9 %collective-permute-start.6 = (f32[3,32,128]{2,1,0:T(8,128)S(1)}, f32[3,32,128]{2,1,0:T(8,128)S(1)}, u32[]{:S(2)}, u32[]{:S(2)}) collective-permute-start(f32[3,32,128]{2,1,0:T(8,128)S(1)} %get-tuple-element.45), channel_id=1, source_target_pairs={{0,1},{1,0},{2,3},{3,2},{4,5},{5,4},{6,7},{7,6},{8,9},{9,8},{10,11... | collective-permute-start | bytes 147464 | tf_op jit(solution)/shard_map/ppermute | solution.py:483
  24.1 7.5 %collective-permute-start.7 = (f32[3,32,128]{2,1,0:T(8,128)S(1)}, f32[3,32,128]{2,1,0:T(8,128)S(1)}, u32[]{:S(2)}, u32[]{:S(2)}) collective-permute-start(f32[3,32,128]{2,1,0:T(8,128)S(1)} %get-tuple-element.46), channel_id=1, source_target_pairs={{0,15},{1,2},{2,1},{3,4},{4,3},{5,6},{6,5},{7,8},{8,7},{9,10},{10,... | collective-permute-start | bytes 147464 | tf_op jit(solution)/shard_map/ppermute | solution.py:484

commit v8 on v7

--- a/solution.py
+++ b/solution.py
@@ -8,7 +8,7 @@
 OMEGA = 0.8
 F32 = jnp.float32
 WINDOW = 64
-STEPS = (4, 7, 3, 2, 4)
+STEPS = (4, 7, 3, 2)
 VM = pl.BlockSpec(memory_space=pltpu.VMEM)
 
 
@@ -16,12 +16,12 @@
     return jax.ShapeDtypeStruct(dims, F32)
 
 
-def call(body, outs, scratch, *args, specs=None):
+def call(body, outs, scratch, *args, specs=None, out_specs=None):
     return pl.pallas_call(
         body,
         out_shape=outs,
         in_specs=specs or [VM] * len(args),
-        out_specs=tuple(VM for _ in outs),
+        out_specs=out_specs or tuple(VM for _ in outs),
         scratch_shapes=[pltpu.VMEM(s, F32) if isinstance(s, tuple) else s for s in scratch],
         compiler_params=pltpu.CompilerParams(vmem_limit_bytes=16 << 20),
     )(*args)
@@ -312,7 +312,7 @@
     blocks, aggs,
     p0, pe, v0, w0, e1in, w1, wide, ye, yo, xe, xo,
     out,
-    e2, w2, b2, c2, own2, rest2, m2, t2, e1, m1, mf,
+    e2, w2, b2, c2, own2, rest2, m2, t2, e1, m1, mf, made, sem,
 ):
     bi, ai = lax.axis_index("blk"), lax.axis_index("agg")
     x_even, y_even = (bi & 1) == 0, (ai & 1) == 0
@@ -405,21 +405,23 @@
                     i = 40 * (k // 2)
                     mf[4 * n + k, pl.ds(8 + r, 40, stride=2), :] = old + wider[i : i + 40]
 
-    def inner(n, carry):
-        fine(n, lambda k: [(p0, k - 2), (p0, k - 1), (p0, k), (p0, k + 1)])
-        return carry
-
-    fine(0, lambda k: [(None, 0), (pe, 0), (pe, 1), (p0, 1)])
-    lax.fori_loop(1, 4, inner, 0)
-    fine(4, lambda k: [(p0, 14), (pe, 2), (pe, 3), (None, 0)])
-
-    def last(k):
-        rows = pl.ds(16, 64)
-        m = mf[k + 2, rows]
-        near = mf[k + 1, rows] + mf[k + 3, rows] + beside(mf, k + 2, m, 16, 64)
-        out[k] = 0.2 * m + v0[k, rows] + w0[k, rows] * near
-
-    loop(0, 16, STEPS[4], last)
+    rows = pl.ds(16, 64)
+    writes = []
+    for n in range(5):
+        old = [(p0, 4 * n - 2 + k) for k in range(4)]
+        if n == 0:
+            old[:3] = (None, 0), (pe, 0), (pe, 1)
+        if n == 4:
+            old[1:] = (pe, 2), (pe, 3), (None, 0)
+        fine(n, lambda _: old)
+        for k in range(max(4 * n - 3, 0), min(4 * n + 1, 16)):
+            m = mf[k + 2, rows]
+            near = mf[k + 1, rows] + mf[k + 3, rows] + beside(mf, k + 2, m, 16, 64)
+            made[k] = 0.2 * m + v0[k, rows] + w0[k, rows] * near
+            writes.append(pltpu.make_async_copy(made.at[k], out.at[k], sem.at[k]))
+            writes[-1].start()
+    for copy in writes:
+        copy.wait()
 
 
 def swaps(size, apart):
@@ -486,8 +488,10 @@
     (out,) = call(
         lambda *refs: up_kernel(blocks, aggs, *refs),
         (own,),
-        [small] * 4 + [(6, 48, 128), (6, 32, 128), (14, 48, 128), (6, 32, 128), mid, (12, 56, 128), (20, 96, 128)],
+        [small] * 4 + [(6, 48, 128), (6, 32, 128), (14, 48, 128), (6, 32, 128), mid, (12, 56, 128), (20, 96, 128),
+                       (16, 64, 128), pltpu.SemaphoreType.DMA((16,))],
         p0, pe, v, w, e1, w1, wide, ye, yo, xe, xo,
+        out_specs=(hbm,),
     )
     return out
 

time: 34.9 us -> 33.9 us (0.971)
  Pallas kernels: 7.61 us -> 6.59 us
    pallas_call x6, Pallas kernels: 7.61 us -> 6.59 us  [call(): pl.pallas_call(body, out_shape=outs, in_specs=specs or [VM] * len(args),...]
where the time goes in v8:
time: 33.9 us; the launch traced here: 33.7 us
  starting transfers between devices  18.3 us (54%)
  waiting for transfers between devices  8.81 us (26%)
  Pallas kernels  6.59 us (19%)
    ppermute x2, starting transfers between devices, shards(): xo = lax.ppermute(so, 'blk', near_out)  9.52 us
    ppermute x2, waiting for transfers between devices, shards(): xo = lax.ppermute(so, 'blk', near_out)  6.7 us
    pallas_call x6, Pallas kernels, call(): pl.pallas_call(body, out_shape=outs, in_specs=specs or [VM] * len(args),...  6.59 us
    ppermute x2, starting transfers between devices, shards(): yo = lax.ppermute(so, 'agg', side_out)  6.5 us
    ppermute x2, waiting for transfers between devices, shards(): yo = lax.ppermute(so, 'agg', side_out)  2.1 us
    ppermute x2, starting transfers between devices, shards(): xe = lax.ppermute(se, 'blk', near_in)  2.08 us
  transfers between devices with their start and end apart: 8, of which 4 were waited for; matrix products, arithmetic and copies ran while one was open for 0% of the time, Pallas kernels for 4%

profile of v8, /device:TPU:0, one launch (start us, length us, event | category | flops | bytes accessed | tf_op | source)
XLA Modules:
  0.0 33.7 jit_solution(3650081281254306446)
XLA Ops:
  0.0 1.0 %shard_map.29 = (f32[2,16,4,128]{3,2,1,0:T(4,128)S(1)}, f32[2,16,4,128]{3,2,1,0:T(4,128)S(1)}) custom-call(f32[16,64,128]{2,1,0:T(8,128)} %b.3, f32[16,64,128]{2,1,0:T(8,128)} %c.3), custom_call_target="tpu_custom_call" | custom-call | tf_op jit(solution)/shard_map/pallas_call | solution.py:20
  1.0 0.1 collective-permute-start
  1.1 3.2 %collective-permute-start.1 = (f32[2,16,4,128]{3,2,1,0:T(4,128)S(1)}, f32[2,16,4,128]{3,2,1,0:T(4,128)S(1)}, u32[]{:S(2)}, u32[]{:S(2)}) collective-permute-start(f32[2,16,4,128]{3,2,1,0:T(4,128)S(1)} %get-tuple-element.29), channel_id=1, source_target_pairs={{0,112},{16,32},{32,16},{48,64},{64,48},{80,96},{96,80},{112,0},{1... | collective-permute-start | bytes 196616 | tf_op jit(solution)/shard_map/ppermute | solution.py:451
  4.3 1.3 %shard_map.28 = (f32[16,64,128]{2,1,0:T(8,128)S(1)}, f32[16,64,128]{2,1,0:T(8,128)S(1)}) custom-call(f32[16,64,128]{2,1,0:T(8,128)} %b.3, f32[16,64,128]{2,1,0:T(8,128)} %c.3), custom_call_target="tpu_custom_call" | custom-call | tf_op jit(solution)/shard_map/pallas_call | solution.py:20
  5.7 0.0 collective-permute-done.refs_2_
  5.7 0.6 %collective-permute-done.1.refs_3_ = f32[2,16,4,128]{3,2,1,0:T(4,128)S(1)} collective-permute-done((f32[2,16,4,128]{3,2,1,0:T(4,128)S(1)}, f32[2,16,4,128]{3,2,1,0:T(4,128)S(1)}, u32[]{:S(2)}, u32[]{:S(2)}) %collective-permute-start.1) | collective-permute-done | bytes 65568 | tf_op jit(solution)/shard_map/ppermute | solution.py:451
  6.3 1.4 %shard_map.30 = (f32[16,80,128]{2,1,0:T(8,128)S(1)}, f32[16,96,128]{2,1,0:T(8,128)S(1)}, f32[16,96,128]{2,1,0:T(8,128)S(1)}, f32[8,40,128]{2,1,0:T(8,128)S(1)}, ...) custom-call(f32[16,64,128]{2,1,0:T(8,128)S(1)} %get-tuple-element.26.ref, ...), custom_call_target="tpu_custom_call" | custom-call | tf_op jit(solution)/shard_map/pallas_call | solution.py:20
  7.7 2.0 %collective-permute-start.2 = (f32[336,128]{1,0:T(8,128)S(1)}, f32[336,128]{1,0:T(8,128)S(1)}, u32[]{:S(2)}, u32[]{:S(2)}) collective-permute-start(f32[336,128]{1,0:T(8,128)S(1)} %get-tuple-element.34), channel_id=1, source_target_pairs={{0,1},{1,0},{2,3},{3,2},{4,5},{5,4},{6,7},{7,6},{8,9},{9,8},{10,11... | collective-permute-start | bytes 516104 | tf_op jit(solution)/shard_map/ppermute | solution.py:468
  9.7 4.7 %collective-permute-start.3 = (f32[336,128]{1,0:T(8,128)S(1)}, f32[336,128]{1,0:T(8,128)S(1)}, u32[]{:S(2)}, u32[]{:S(2)}) collective-permute-start(f32[336,128]{1,0:T(8,128)S(1)} %get-tuple-element.35), channel_id=1, source_target_pairs={{0,15},{1,2},{2,1},{3,4},{4,3},{5,6},{6,5},{7,8},{8,7},{9,10},{10,... | collective-permute-start | bytes 516104 | tf_op jit(solution)/shard_map/ppermute | solution.py:469
  14.4 0.0 collective-permute-done.2.refs_3_
  14.4 4.0 %collective-permute-done.3.refs_4_ = f32[336,128]{1,0:T(8,128)S(1)} collective-permute-done((f32[336,128]{1,0:T(8,128)S(1)}, f32[336,128]{1,0:T(8,128)S(1)}, u32[]{:S(2)}, u32[]{:S(2)}) %collective-permute-start.3) | collective-permute-done | bytes 172064 | tf_op jit(solution)/shard_map/ppermute | solution.py:469
  18.4 0.6 %shard_map.31 = (f32[4,80,128]{2,1,0:T(8,128)S(1)}, f32[12,40,128]{2,1,0:T(8,128)S(1)}, f32[12,40,128]{2,1,0:T(8,128)S(1)}, f32[6,16,128]{2,1,0:T(8,128)S(1)}, f...) custom-call(f32[8,40,128]{2,1,0:T(8,128)S(1)} %get-tuple-element.31.refs_0_, ...), custom_call_target="tpu_custom_call" | custom-call | tf_op jit(solution)/shard_map/pallas_call | solution.py:20
  19.0 0.1 collective-permute-start.4
  19.1 3.3 %collective-permute-start.5 = (f32[6,8,128]{2,1,0:T(8,128)S(1)}, f32[6,8,128]{2,1,0:T(8,128)S(1)}, u32[]{:S(2)}, u32[]{:S(2)}) collective-permute-start(f32[6,8,128]{2,1,0:T(8,128)S(1)} %get-tuple-element.43), channel_id=1, source_target_pairs={{0,112},{16,32},{32,16},{48,64},{64,48},{80,96},{96,80},{112,0},{1... | collective-permute-start | bytes 73736 | tf_op jit(solution)/shard_map/ppermute | solution.py:478
  22.4 0.0 collective-permute-done.4.ye.refs_7_
  22.4 1.5 %collective-permute-done.5.yo.refs_8_ = f32[6,8,128]{2,1,0:T(8,128)S(1)} collective-permute-done((f32[6,8,128]{2,1,0:T(8,128)S(1)}, f32[6,8,128]{2,1,0:T(8,128)S(1)}, u32[]{:S(2)}, u32[]{:S(2)}) %collective-permute-start.5) | collective-permute-done | bytes 24608 | tf_op jit(solution)/shard_map/ppermute | solution.py:478
  23.9 0.1 shard_map.32
  24.0 0.1 collective-permute-start.6
  24.1 4.8 %collective-permute-start.7 = (f32[3,32,128]{2,1,0:T(8,128)S(1)}, f32[3,32,128]{2,1,0:T(8,128)S(1)}, u32[]{:S(2)}, u32[]{:S(2)}) collective-permute-start(f32[3,32,128]{2,1,0:T(8,128)S(1)} %get-tuple-element.46), channel_id=1, source_target_pairs={{0,15},{1,2},{2,1},{3,4},{4,3},{5,6},{6,5},{7,8},{8,7},{9,10},{10,... | collective-permute-start | bytes 147464 | tf_op jit(solution)/shard_map/ppermute | solution.py:486
  28.9 0.0 collective-permute-done.6.refs_9_
  28.9 2.7 %collective-permute-done.7.refs_10_ = f32[3,32,128]{2,1,0:T(8,128)S(1)} collective-permute-done((f32[3,32,128]{2,1,0:T(8,128)S(1)}, f32[3,32,128]{2,1,0:T(8,128)S(1)}, u32[]{:S(2)}, u32[]{:S(2)}) %collective-permute-start.7) | collective-permute-done | bytes 49184 | tf_op jit(solution)/shard_map/ppermute | solution.py:486
  31.6 2.2 %shard_map.33 = f32[16,64,128]{2,1,0:T(8,128)} custom-call(f32[16,80,128]{2,1,0:T(8,128)S(1)} %get-tuple-element.30.refs_0_, f32[4,80,128]{2,1,0:T(8,128)S(1)} %get-tuple-element.36.refs_1_, f32[16,96,128]{2,1,0:T(8,128)S(1)} %get-tuple-element.37.refs_2_, f32[16,96,128]{2,1,0:T(8,128)S(1)} %get-tuple-element.38.refs_3_, ...), custom_call_target="tpu_custom_call" | custom-call | tf_op jit(solution)/shard_map/pallas_call | solution.py:20
Async XLA Ops:
  1.0 4.7 %collective-permute-start = (f32[2,16,4,128]{3,2,1,0:T(4,128)S(1)}, f32[2,16,4,128]{3,2,1,0:T(4,128)S(1)}, u32[]{:S(2)}, u32[]{:S(2)}) collective-permute-start(f32[2,16,4,128]{3,2,1,0:T(4,128)S(1)} %get-tuple-element.28), channel_id=1, source_target_pairs={{0,16},{16,0},{32,48},{48,32},{64,80},{80,64},{96,112},{112,96},{1... | collective-permute-start | bytes 196616 | tf_op jit(solution)/shard_map/ppermute | solution.py:450
  1.1 5.2 %collective-permute-start.1 = (f32[2,16,4,128]{3,2,1,0:T(4,128)S(1)}, f32[2,16,4,128]{3,2,1,0:T(4,128)S(1)}, u32[]{:S(2)}, u32[]{:S(2)}) collective-permute-start(f32[2,16,4,128]{3,2,1,0:T(4,128)S(1)} %get-tuple-element.29), channel_id=1, source_target_pairs={{0,112},{16,32},{32,16},{48,64},{64,48},{80,96},{96,80},{112,0},{1... | collective-permute-start | bytes 196616 | tf_op jit(solution)/shard_map/ppermute | solution.py:451
  7.7 6.7 %collective-permute-start.2 = (f32[336,128]{1,0:T(8,128)S(1)}, f32[336,128]{1,0:T(8,128)S(1)}, u32[]{:S(2)}, u32[]{:S(2)}) collective-permute-start(f32[336,128]{1,0:T(8,128)S(1)} %get-tuple-element.34), channel_id=1, source_target_pairs={{0,1},{1,0},{2,3},{3,2},{4,5},{5,4},{6,7},{7,6},{8,9},{9,8},{10,11... | collective-permute-start | bytes 516104 | tf_op jit(solution)/shard_map/ppermute | solution.py:468
  9.7 8.7 %collective-permute-start.3 = (f32[336,128]{1,0:T(8,128)S(1)}, f32[336,128]{1,0:T(8,128)S(1)}, u32[]{:S(2)}, u32[]{:S(2)}) collective-permute-start(f32[336,128]{1,0:T(8,128)S(1)} %get-tuple-element.35), channel_id=1, source_target_pairs={{0,15},{1,2},{2,1},{3,4},{4,3},{5,6},{6,5},{7,8},{8,7},{9,10},{10,... | collective-permute-start | bytes 516104 | tf_op jit(solution)/shard_map/ppermute | solution.py:469
  19.0 3.4 %collective-permute-start.4 = (f32[6,8,128]{2,1,0:T(8,128)S(1)}, f32[6,8,128]{2,1,0:T(8,128)S(1)}, u32[]{:S(2)}, u32[]{:S(2)}) collective-permute-start(f32[6,8,128]{2,1,0:T(8,128)S(1)} %get-tuple-element.42), channel_id=1, source_target_pairs={{0,16},{16,0},{32,48},{48,32},{64,80},{80,64},{96,112},{112,96},{1... | collective-permute-start | bytes 73736 | tf_op jit(solution)/shard_map/ppermute | solution.py:477
  19.1 4.8 %collective-permute-start.5 = (f32[6,8,128]{2,1,0:T(8,128)S(1)}, f32[6,8,128]{2,1,0:T(8,128)S(1)}, u32[]{:S(2)}, u32[]{:S(2)}) collective-permute-start(f32[6,8,128]{2,1,0:T(8,128)S(1)} %get-tuple-element.43), channel_id=1, source_target_pairs={{0,112},{16,32},{32,16},{48,64},{64,48},{80,96},{96,80},{112,0},{1... | collective-permute-start | bytes 73736 | tf_op jit(solution)/shard_map/ppermute | solution.py:478
  24.0 4.9 %collective-permute-start.6 = (f32[3,32,128]{2,1,0:T(8,128)S(1)}, f32[3,32,128]{2,1,0:T(8,128)S(1)}, u32[]{:S(2)}, u32[]{:S(2)}) collective-permute-start(f32[3,32,128]{2,1,0:T(8,128)S(1)} %get-tuple-element.45), channel_id=1, source_target_pairs={{0,1},{1,0},{2,3},{3,2},{4,5},{5,4},{6,7},{7,6},{8,9},{9,8},{10,11... | collective-permute-start | bytes 147464 | tf_op jit(solution)/shard_map/ppermute | solution.py:485
  24.1 7.5 %collective-permute-start.7 = (f32[3,32,128]{2,1,0:T(8,128)S(1)}, f32[3,32,128]{2,1,0:T(8,128)S(1)}, u32[]{:S(2)}, u32[]{:S(2)}) collective-permute-start(f32[3,32,128]{2,1,0:T(8,128)S(1)} %get-tuple-element.46), channel_id=1, source_target_pairs={{0,15},{1,2},{2,1},{3,4},{4,3},{5,6},{6,5},{7,8},{8,7},{9,10},{10,... | collective-permute-start | bytes 147464 | tf_op jit(solution)/shard_map/ppermute | solution.py:486

commit v9 on v8

--- a/solution.py
+++ b/solution.py
@@ -16,13 +16,14 @@
     return jax.ShapeDtypeStruct(dims, F32)
 
 
-def call(body, outs, scratch, *args, specs=None, out_specs=None):
+def call(body, outs, scratch, *args, specs=None, out_specs=None, aliases={}):
     return pl.pallas_call(
         body,
         out_shape=outs,
         in_specs=specs or [VM] * len(args),
         out_specs=out_specs or tuple(VM for _ in outs),
         scratch_shapes=[pltpu.VMEM(s, F32) if isinstance(s, tuple) else s for s in scratch],
+        input_output_aliases=aliases,
         compiler_params=pltpu.CompilerParams(vmem_limit_bytes=16 << 20),
     )(*args)
 
@@ -103,7 +104,7 @@
     return row_pairs(rest, k, at_rest, rows) + own + below + above, own
 
 
-def pack_kernel(b, c, se, so, first, last, sem):
+def pack_kernel(b, c, se, so, sides, first, last, sem):
     copies = []
     for n, ref in enumerate((b, c)):
         copies.append(pltpu.make_async_copy(ref.at[:, pl.ds(0, 8)], first.at[n], sem.at[2 * n]))
@@ -116,9 +117,29 @@
     for n in (0, 1):
         se[n] = jnp.where(y_even, last[n, :, 4:8], first[n, :, 0:4])
         so[n] = jnp.where(y_even, first[n, :, 0:4], last[n, :, 4:8])
-
-
-def load_kernel(b, c, bv, cv, sem):
+    sides[0], sides[1] = first[0], last[0]
+
+
+def smoothed(v, w, q, p0, p, start, rows):
+    at = pl.ds(start, rows)
+    vv = v[p, at]
+    near = v[p - 1, at] + v[p + 1, at] + beside(v, p, vv, start, rows)
+    qq = 0.4 * vv + w[p, at] * near
+    q[p, at] = qq
+    p0[p, pl.ds(start - 8, rows)] = qq + OMEGA * vv
+
+
+def child_sums(q, own1, rest1, k, start, rows, bb, end=None):
+    at, p = pl.ds(start, rows), 2 * k
+    if end is not None:
+        both, outer = q[end[0], at], q[end[1], at]
+    else:
+        both, outer = q[p, at] + q[p + 1, at], q[p - 1, at] + q[p + 2, at]
+    own1[k, at] = both
+    rest1[k, pl.ds(start - 8, rows)] = 0.04 * bb + (both + outer)
+
+
+def own_kernel(b, c, v, w, p0, own1, rest1, c1, q, bv, cv, cs, sem):
     copies = []
     for n in range(4):
         part = pl.ds(4 * n, 4)
@@ -126,15 +147,36 @@
             copies.append(pltpu.make_async_copy(x.at[part], y.at[part], sem.at[2 * n + i]))
     for copy in copies:
         copy.start()
-    for copy in copies:
-        copy.wait()
+    for n in range(4):
+        for copy in copies[2 * n : 2 * n + 2]:
+            copy.wait()
+        for p in range(4 * n, 4 * n + 4):
+            ww = OMEGA / (6.0 + cv[p])
+            w[p, 16:80] = ww
+            v[p, 16:80] = ww * bv[p]
+        for k in (2 * n, 2 * n + 1):
+            cs[k] = cv[2 * k] + cv[2 * k + 1]
+    loop(1, 15, STEPS[1], lambda p: smoothed(v, w, q, p0, p, 24, 48))
+
+    def sums(k, end=None):
+        child_sums(q, own1, rest1, k, 24, 48, bv[2 * k, 8:56] + bv[2 * k + 1, 8:56], end)
+
+    sums(0, (1, 2))
+    loop(1, 7, STEPS[2], sums)
+    sums(7, (14, 13))
+    pairs = pick("pairs")
+    for n in range(2):
+        some = range(4 * n, 4 * n + 4)
+        cc = 0.5 * dot((jnp.concatenate([row_pairs(cs, k, 0, 32) for k in some], axis=0), pairs))
+        for i, k in enumerate(some):
+            c1[k, 4:36] = cc[32 * i : 32 * i + 32]
 
 
 def head_kernel(
     aggs,
-    b, c, ye, yo,
-    p0, v, w, b1, c1, edge, se, so,
-    q, bx, cx, own1, rest1,
+    ye, yo, sides, v_in, w_in, p0_in, own_in, rest_in, c_in,
+    v, w, p0, own1, rest1, c1, b1, edge, se, so,
+    q, bl, bh, cs,
 ):
     bi, ai = lax.axis_index("blk"), lax.axis_index("agg")
     x_even, y_even = (bi & 1) == 0, (ai & 1) == 0
@@ -142,26 +184,32 @@
     y_hi = jnp.where(ai < aggs - 1, OMEGA, 0.0)
     rows = pl.ds(8, 80)
 
-    def put(p, rows, bb, cc, scale):
-        ww = scale / (6.0 + cc)
-        vv = ww * bb
-        w[p, rows], v[p, rows], bx[p, rows], cx[p, rows] = ww, vv, bb, cc
-
-    def plane(p):
-        put(p, pl.ds(16, 64), b[p], c[p], OMEGA)
-        lo = [jnp.where(y_even, yo[k, p], ye[k, p]) for k in (0, 1)]
-        hi = [jnp.where(y_even, ye[k, p], yo[k, p]) for k in (0, 1)]
-        put(p, pl.ds(12, 4), *lo, y_lo)
-        put(p, pl.ds(80, 4), *hi, y_hi)
-
-    loop(0, 16, STEPS[0], plane)
+    def halo(k):
+        csum = []
+        for first, scale, start in ((jnp.logical_not(y_even), y_lo, 12), (y_even, y_hi, 80)):
+            got = []
+            for p in (2 * k, 2 * k + 1):
+                bb, cc = [jnp.where(first, ye[n, p], yo[n, p]) for n in (0, 1)]
+                ww = scale / (6.0 + cc)
+                w[p, pl.ds(start, 4)] = ww
+                v[p, pl.ds(start, 4)] = ww * bb
+                got.append((bb, cc))
+            csum.append(got[0][1] + got[1][1])
+            bsum = got[0][0] + got[1][0]
+            if start == 12:
+                bl[k, 4:8] = bsum
+            else:
+                bh[k, 8:12] = bsum
+        bl[k, 8:16] = sides[0, 2 * k] + sides[0, 2 * k + 1]
+        bh[k, 0:8] = sides[1, 2 * k] + sides[1, 2 * k + 1]
+        cs[k, 0:4] = csum[0]
+        cs[k, 4:8] = csum[1]
+
+    loop(0, 8, STEPS[0], halo)
 
     def smooth(p):
-        vv = v[p, rows]
-        near = v[p - 1, rows] + v[p + 1, rows] + beside(v, p, vv, 8, 80)
-        qq = 0.4 * vv + w[p, rows] * near
-        q[p, rows] = qq
-        p0[p] = qq + OMEGA * vv
+        for start in (8, 72):
+            smoothed(v, w, q, p0, p, start, 16)
 
     loop(1, 15, STEPS[1], smooth)
     for n, p, inner in ((0, 0, 1), (3, 15, 14)):
@@ -170,43 +218,40 @@
         edge[n + 1] = ww
         edge[n + 2] = vv
 
-    def sums(k, p):
-        cx[k, rows] = cx[p, rows] + cx[p + 1, rows]
-        return 0.04 * (bx[p, rows] + bx[p + 1, rows])
-
-    def coarse(k):
-        p = 2 * k
-        both = q[p, rows] + q[p + 1, rows]
-        own1[k, rows] = both
-        rest1[k] = sums(k, p) + (both + (q[p - 1, rows] + q[p + 2, rows]))
-
-    own1[0, rows] = q[1, rows]
-    rest1[0] = sums(0, 0) + (q[1, rows] + q[2, rows])
-    loop(1, 7, STEPS[2], coarse)
-    own1[7, rows] = q[14, rows]
-    rest1[7] = sums(7, 14) + (q[14, rows] + q[13, rows])
-
-    pairs, sides = pick("pairs"), pick("beside")
+    def sums(k, end=None):
+        child_sums(q, own1, rest1, k, 8, 16, bl[k], end)
+        child_sums(q, own1, rest1, k, 72, 16, bh[k], end)
+
+    sums(0, (1, 2))
+    loop(1, 7, STEPS[2], sums)
+    sums(7, (14, 13))
+    pairs, near = pick("pairs"), pick("beside")
+    cc = 0.5 * dot((jnp.concatenate([row_pairs(cs, k, 0, 4) for k in range(8)], axis=0), pairs))
+    for k in range(8):
+        c1[k, 4:36] = c_in[k, 4:36]
+        c1[k, 2:4] = cc[4 * k : 4 * k + 2]
+        c1[k, 36:38] = cc[4 * k + 2 : 4 * k + 4]
 
     def products(n):
-        ends, mids, csums = [], [], []
+        ends, mids = [], []
         for k in (2 * n, 2 * n + 1):
             end, mid = gather(own1, rest1, k, 8, 0, 40)
             ends.append(end)
             mids.append(mid)
-            csums.append(row_pairs(cx, k, 8, 40))
-        bb = dot((jnp.concatenate(ends, axis=0), pairs), (jnp.concatenate(mids, axis=0), sides))
-        cc = dot((jnp.concatenate(csums, axis=0), pairs))
+        bb = dot((jnp.concatenate(ends, axis=0), pairs), (jnp.concatenate(mids, axis=0), near))
         for i in (0, 1):
             b1[2 * n + i] = 0.5 * bb[40 * i : 40 * i + 40]
-            c1[2 * n + i] = 0.5 * cc[40 * i : 40 * i + 40]
 
     loop(0, 4, STEPS[3], products)
     for ref, up in ((se, x_even), (so, jnp.logical_not(x_even))):
         for i in range(3):
             ref[72 * i : 72 * i + 72] = jnp.where(up, edge[3 + i, 4:76], edge[i, 4:76])
-            mix = jnp.where(up, b1[5 + i], b1[i]) + turn(jnp.where(up, c1[5 + i], c1[i]), 64, 1)
-            ref[216 + 40 * i : 256 + 40 * i] = mix
+        for i in (0, 1):
+            mix = jnp.where(up, b1[6 + i], b1[i]) + turn(jnp.where(up, c1[6 + i], c1[i]), 64, 1)
+            ref[216 + 34 * i : 250 + 34 * i] = mix[3:37]
+        third = OMEGA / (6.0 + jnp.where(up, c1[5], c1[2])) * jnp.where(up, b1[5], b1[2])
+        ref[284:301] = third[3:20] + turn(third, 64, 1)[20:37]
+        ref[301:304] = jnp.zeros((3, 128), F32)
 
 
 def mid_kernel(
@@ -238,11 +283,16 @@
         s4[2 * i + 1, pl.ds(8, 80)] = other
         r4[2 * i] = mine + other
         r4[2 * i + 1] = mine + other
-        for n in range(3):
-            mix = fetch(lo, 216 + 40 * n, 40)
-            k = n if lo else 11 + n
-            b1[k] = jnp.where(lane1, mix, 0.0)
-            c1[k] = jnp.where(lane1, turn(mix, -64, 1), 0.0)
+        for n in (0, 1):
+            mix = fetch(lo, 216 + 34 * n, 34)
+            k = 1 + n if lo else 11 + n
+            b1[k, 3:37] = jnp.where(lane1[:34], mix, 0.0)
+            c1[k, 3:37] = jnp.where(lane1[:34], turn(mix, -64, 1), 0.0)
+        k = 0 if lo else 13
+        there = inside(bi * 8 + k - 3, 8 * blocks) & lane1[:17]
+        mix = fetch(lo, 284, 17)
+        for start, part in ((3, mix), (20, turn(mix, -64, 1))):
+            e1[k, start : start + 17] = jnp.where(there & inside(ai * 32 - 4 + start + iota(17, 0), 32 * aggs), part, 0.0)
     for k in range(8):
         b1[k + 3] = b1in[k]
         c1[k + 3] = c1in[k]
@@ -257,13 +307,12 @@
 
     row1 = ai * 32 - 4 + iota(40, 0)
     keep1 = inside(row1, 32 * aggs) & lane1
-    for k in range(14):
+    for k in range(1, 13):
         ok = keep1 & inside(bi * 8 + k - 3, 8 * blocks)
         ww = jnp.where(ok, OMEGA / (6.0 + c1[k]), 0.0)
         ee = jnp.where(ok, ww * b1[k], 0.0)
         e1[k] = ee
-        if 0 < k < 13:
-            w1out[k - 1], e1out[k - 1] = ww, ee
+        w1out[k - 1], e1out[k - 1] = ww, ee
 
     at2 = (ai * 16 + iota(16, 0)) & (WINDOW // 2 - 1)
     lane16 = iota(16, 1)
@@ -439,31 +488,32 @@
 
     hbm = pl.BlockSpec(memory_space=pltpu.HBM)
     b, c = [pltpu.with_memory_space_constraint(x, pltpu.HBM) for x in (b, c)]
-    own, faces = shape(16, 64, 128), shape(2, 16, 4, 128)
-    se, so = call(
+    faces = shape(2, 16, 4, 128)
+    se, so, sides = call(
         pack_kernel,
-        (faces, faces),
+        (faces, faces, shape(2, 16, 8, 128)),
         [(2, 16, 8, 128), (2, 16, 8, 128), pltpu.SemaphoreType.DMA((4,))],
         b, c,
         specs=[hbm, hbm],
     )
     ye = lax.ppermute(se, "agg", side_in)
     yo = lax.ppermute(so, "agg", side_out)
-    b, c = call(
-        load_kernel,
-        (own, own),
-        [pltpu.SemaphoreType.DMA((8,))],
+
+    mid, big = (12, 40, 128), shape(16, 96, 128)
+    fields = (big, big, shape(16, 80, 128), shape(8, 96, 128), shape(8, 80, 128))
+    v, w, p0, own1, rest1, c1 = call(
+        own_kernel,
+        fields + (shape(8, 40, 128),),
+        [(16, 96, 128), (16, 64, 128), (16, 64, 128), (8, 64, 128), pltpu.SemaphoreType.DMA((8,))],
         b, c,
         specs=[hbm, hbm],
     )
-
-    big, mid = (16, 96, 128), (12, 40, 128)
-    p0, v, w, b1, c1, edge, se, so = call(
+    v, w, p0, _, _, c1, b1, edge, se, so = call(
         lambda *refs: head_kernel(aggs, *refs),
-        (shape(16, 80, 128), shape(*big), shape(*big), shape(8, 40, 128), shape(8, 40, 128),
-         shape(6, 80, 128), shape(336, 128), shape(336, 128)),
-        [big] * 3 + [(8, 96, 128), (8, 80, 128)],
-        b, c, ye, yo,
+        fields + (shape(8, 40, 128), shape(8, 40, 128), shape(6, 80, 128), shape(304, 128), shape(304, 128)),
+        [(16, 96, 128), (8, 16, 128), (8, 16, 128), (8, 8, 128)],
+        ye, yo, sides, v, w, p0, own1, rest1, c1,
+        aliases={3 + i: i for i in range(5)},
     )
     xe = lax.ppermute(se, "blk", near_in)
     xo = lax.ppermute(so, "blk", near_out)
@@ -487,7 +537,7 @@
     small = (14, 32, 128)
     (out,) = call(
         lambda *refs: up_kernel(blocks, aggs, *refs),
-        (own,),
+        (shape(16, 64, 128),),
         [small] * 4 + [(6, 48, 128), (6, 32, 128), (14, 48, 128), (6, 32, 128), mid, (12, 56, 128), (20, 96, 128),
                        (16, 64, 128), pltpu.SemaphoreType.DMA((16,))],
         p0, pe, v, w, e1, w1, wide, ye, yo, xe, xo,

time: 33.9 us -> 33.3 us (0.982)
  waiting for transfers between devices: 8.81 us -> 8.05 us
    ppermute x2, waiting for transfers between devices: 2.1 us -> 1.52 us  [shards(): yo = lax.ppermute(so, 'agg', side_out)]
  transfers between devices with their start and end apart: 8 -> 8, of which waited for: 4 -> 3; matrix products, arithmetic and copies ran while one was open for 0% -> 0% of each run, Pallas kernels for 4% -> 6%
where the time goes in v9:
time: 33.3 us; the launch traced here: 33.1 us
  starting transfers between devices  18.1 us (54%)
  waiting for transfers between devices  8.05 us (24%)
  Pallas kernels  6.89 us (21%)
    ppermute x2, starting transfers between devices, shards(): xo = lax.ppermute(so, 'blk', near_out)  9.51 us
    pallas_call x6, Pallas kernels, call(): pl.pallas_call(body, out_shape=outs, in_specs=specs or [VM] * len(args),...  6.89 us
    ppermute x2, waiting for transfers between devices, shards(): xo = lax.ppermute(so, 'blk', near_out)  6.52 us
    ppermute x2, starting transfers between devices, shards(): yo = lax.ppermute(so, 'agg', side_out)  6.3 us
    ppermute x2, starting transfers between devices, shards(): xe = lax.ppermute(se, 'blk', near_in)  2.08 us
    ppermute x2, waiting for transfers between devices, shards(): yo = lax.ppermute(so, 'agg', side_out)  1.52 us
  transfers between devices with their start and end apart: 8, of which 3 were waited for; matrix products, arithmetic and copies ran while one was open for 0% of the time, Pallas kernels for 6%

profile of v9, /device:TPU:0, one launch (start us, length us, event | category | flops | bytes accessed | tf_op | source)
XLA Modules:
  0.0 33.1 jit_solution(2256781999404462475)
XLA Ops:
  0.0 1.0 %shard_map.28 = (f32[2,16,4,128]{3,2,1,0:T(4,128)S(1)}, f32[2,16,4,128]{3,2,1,0:T(4,128)S(1)}, f32[2,16,8,128]{3,2,1,0:T(8,128)S(1)}) custom-call(f32[16,64,128]{2,1,0:T(8,128)} %b.3, f32[16,64,128]{2,1,0:T(8,128)} %c.3), custom_call_target="tpu_custom_call" | custom-call | tf_op jit(solution)/shard_map/pallas_call | solution.py:20
  1.0 0.1 collective-permute-start
  1.1 3.2 %collective-permute-start.1 = (f32[2,16,4,128]{3,2,1,0:T(4,128)S(1)}, f32[2,16,4,128]{3,2,1,0:T(4,128)S(1)}, u32[]{:S(2)}, u32[]{:S(2)}) collective-permute-start(f32[2,16,4,128]{3,2,1,0:T(4,128)S(1)} %get-tuple-element.32), channel_id=1, source_target_pairs={{0,112},{16,32},{32,16},{48,64},{64,48},{80,96},{96,80},{112,0},{1... | collective-permute-start | bytes 196616 | tf_op jit(solution)/shard_map/ppermute | solution.py:500
  4.3 1.9 %shard_map.29 = (f32[16,96,128]{2,1,0:T(8,128)S(1)}, f32[16,96,128]{2,1,0:T(8,128)S(1)}, f32[16,80,128]{2,1,0:T(8,128)S(1)}, f32[8,96,128]{2,1,0:T(8,128)S(1)}, ...) custom-call(f32[16,64,128]{2,1,0:T(8,128)} %b.3, f32[16,64,128]{2,1,0:T(8,128)} %c.3), custom_call_target="tpu_custom_call" | custom-call | tf_op jit(solution)/shard_map/pallas_call | solution.py:20
  6.3 0.0 collective-permute-done.refs_0_
  6.3 0.0 collective-permute-done.1.refs_1_
  6.3 1.1 %shard_map.30 = (f32[16,96,128]{2,1,0:T(8,128)S(1)}, f32[16,96,128]{2,1,0:T(8,128)S(1)}, f32[16,80,128]{2,1,0:T(8,128)S(1)}, f32[8,96,128]{2,1,0:T(8,128)S(1)}, ...) custom-call(f32[2,16,4,128]{3,2,1,0:T(4,128)S(1)} %collective-permut, ...), custom_call_target="tpu_custom_call", output_to_operand_aliasing={{0}: (3, {}), {1}: (4, {}), {2}: (5, {}), {3}: (6, {}), {4}... | custom-call | tf_op jit(solution)/shard_map/pallas_call | solution.py:20
  7.4 2.0 %collective-permute-start.2 = (f32[304,128]{1,0:T(8,128)S(1)}, f32[304,128]{1,0:T(8,128)S(1)}, u32[]{:S(2)}, u32[]{:S(2)}) collective-permute-start(f32[304,128]{1,0:T(8,128)S(1)} %get-tuple-element.44), channel_id=1, source_target_pairs={{0,1},{1,0},{2,3},{3,2},{4,5},{5,4},{6,7},{7,6},{8,9},{9,8},{10,11... | collective-permute-start | bytes 466952 | tf_op jit(solution)/shard_map/ppermute | solution.py:518
  9.4 4.7 %collective-permute-start.3 = (f32[304,128]{1,0:T(8,128)S(1)}, f32[304,128]{1,0:T(8,128)S(1)}, u32[]{:S(2)}, u32[]{:S(2)}) collective-permute-start(f32[304,128]{1,0:T(8,128)S(1)} %get-tuple-element.45), channel_id=1, source_target_pairs={{0,15},{1,2},{2,1},{3,4},{4,3},{5,6},{6,5},{7,8},{8,7},{9,10},{10,... | collective-permute-start | bytes 466952 | tf_op jit(solution)/shard_map/ppermute | solution.py:519
  14.1 0.0 collective-permute-done.2.refs_3_
  14.1 3.8 %collective-permute-done.3.refs_4_ = f32[304,128]{1,0:T(8,128)S(1)} collective-permute-done((f32[304,128]{1,0:T(8,128)S(1)}, f32[304,128]{1,0:T(8,128)S(1)}, u32[]{:S(2)}, u32[]{:S(2)}) %collective-permute-start.3) | collective-permute-done | bytes 155680 | tf_op jit(solution)/shard_map/ppermute | solution.py:519
  18.0 0.6 %shard_map.31 = (f32[4,80,128]{2,1,0:T(8,128)S(1)}, f32[12,40,128]{2,1,0:T(8,128)S(1)}, f32[12,40,128]{2,1,0:T(8,128)S(1)}, f32[6,16,128]{2,1,0:T(8,128)S(1)}, f...) custom-call(f32[8,40,128]{2,1,0:T(8,128)S(1)} %get-tuple-element.41.refs_0_, ...), custom_call_target="tpu_custom_call" | custom-call | tf_op jit(solution)/shard_map/pallas_call | solution.py:20
  18.5 0.1 collective-permute-start.4
  18.6 3.1 %collective-permute-start.5 = (f32[6,8,128]{2,1,0:T(8,128)S(1)}, f32[6,8,128]{2,1,0:T(8,128)S(1)}, u32[]{:S(2)}, u32[]{:S(2)}) collective-permute-start(f32[6,8,128]{2,1,0:T(8,128)S(1)} %get-tuple-element.53), channel_id=1, source_target_pairs={{0,112},{16,32},{32,16},{48,64},{64,48},{80,96},{96,80},{112,0},{1... | collective-permute-start | bytes 73736 | tf_op jit(solution)/shard_map/ppermute | solution.py:528
  21.7 0.0 collective-permute-done.4.ye.refs_7_
  21.7 1.5 %collective-permute-done.5.yo.refs_8_ = f32[6,8,128]{2,1,0:T(8,128)S(1)} collective-permute-done((f32[6,8,128]{2,1,0:T(8,128)S(1)}, f32[6,8,128]{2,1,0:T(8,128)S(1)}, u32[]{:S(2)}, u32[]{:S(2)}) %collective-permute-start.5) | collective-permute-done | bytes 24608 | tf_op jit(solution)/shard_map/ppermute | solution.py:528
  23.2 0.1 shard_map.32
  23.3 0.1 collective-permute-start.6
  23.4 4.8 %collective-permute-start.7 = (f32[3,32,128]{2,1,0:T(8,128)S(1)}, f32[3,32,128]{2,1,0:T(8,128)S(1)}, u32[]{:S(2)}, u32[]{:S(2)}) collective-permute-start(f32[3,32,128]{2,1,0:T(8,128)S(1)} %get-tuple-element.56), channel_id=1, source_target_pairs={{0,15},{1,2},{2,1},{3,4},{4,3},{5,6},{6,5},{7,8},{8,7},{9,10},{10,... | collective-permute-start | bytes 147464 | tf_op jit(solution)/shard_map/ppermute | solution.py:536
  28.2 0.0 collective-permute-done.6.refs_9_
  28.2 2.7 %collective-permute-done.7.refs_10_ = f32[3,32,128]{2,1,0:T(8,128)S(1)} collective-permute-done((f32[3,32,128]{2,1,0:T(8,128)S(1)}, f32[3,32,128]{2,1,0:T(8,128)S(1)}, u32[]{:S(2)}, u32[]{:S(2)}) %collective-permute-start.7) | collective-permute-done | bytes 49184 | tf_op jit(solution)/shard_map/ppermute | solution.py:536
  30.9 2.2 %shard_map.33 = f32[16,64,128]{2,1,0:T(8,128)} custom-call(f32[16,80,128]{2,1,0:T(8,128)S(1)} %get-tuple-element.40.refs_0_, f32[4,80,128]{2,1,0:T(8,128)S(1)} %get-tuple-element.46.refs_1_, f32[16,96,128]{2,1,0:T(8,128)S(1)} %get-tuple-element.47.refs_2_, f32[16,96,128]{2,1,0:T(8,128)S(1)} %get-tuple-element.48.refs_3_, ...), custom_call_target="tpu_custom_call" | custom-call | tf_op jit(solution)/shard_map/pallas_call | solution.py:20
Async XLA Ops:
  1.0 5.3 %collective-permute-start = (f32[2,16,4,128]{3,2,1,0:T(4,128)S(1)}, f32[2,16,4,128]{3,2,1,0:T(4,128)S(1)}, u32[]{:S(2)}, u32[]{:S(2)}) collective-permute-start(f32[2,16,4,128]{3,2,1,0:T(4,128)S(1)} %get-tuple-element.31), channel_id=1, source_target_pairs={{0,16},{16,0},{32,48},{48,32},{64,80},{80,64},{96,112},{112,96},{1... | collective-permute-start | bytes 196616 | tf_op jit(solution)/shard_map/ppermute | solution.py:499
  1.1 5.2 %collective-permute-start.1 = (f32[2,16,4,128]{3,2,1,0:T(4,128)S(1)}, f32[2,16,4,128]{3,2,1,0:T(4,128)S(1)}, u32[]{:S(2)}, u32[]{:S(2)}) collective-permute-start(f32[2,16,4,128]{3,2,1,0:T(4,128)S(1)} %get-tuple-element.32), channel_id=1, source_target_pairs={{0,112},{16,32},{32,16},{48,64},{64,48},{80,96},{96,80},{112,0},{1... | collective-permute-start | bytes 196616 | tf_op jit(solution)/shard_map/ppermute | solution.py:500
  7.4 6.7 %collective-permute-start.2 = (f32[304,128]{1,0:T(8,128)S(1)}, f32[304,128]{1,0:T(8,128)S(1)}, u32[]{:S(2)}, u32[]{:S(2)}) collective-permute-start(f32[304,128]{1,0:T(8,128)S(1)} %get-tuple-element.44), channel_id=1, source_target_pairs={{0,1},{1,0},{2,3},{3,2},{4,5},{5,4},{6,7},{7,6},{8,9},{9,8},{10,11... | collective-permute-start | bytes 466952 | tf_op jit(solution)/shard_map/ppermute | solution.py:518
  9.4 8.6 %collective-permute-start.3 = (f32[304,128]{1,0:T(8,128)S(1)}, f32[304,128]{1,0:T(8,128)S(1)}, u32[]{:S(2)}, u32[]{:S(2)}) collective-permute-start(f32[304,128]{1,0:T(8,128)S(1)} %get-tuple-element.45), channel_id=1, source_target_pairs={{0,15},{1,2},{2,1},{3,4},{4,3},{5,6},{6,5},{7,8},{8,7},{9,10},{10,... | collective-permute-start | bytes 466952 | tf_op jit(solution)/shard_map/ppermute | solution.py:519
  18.5 3.2 %collective-permute-start.4 = (f32[6,8,128]{2,1,0:T(8,128)S(1)}, f32[6,8,128]{2,1,0:T(8,128)S(1)}, u32[]{:S(2)}, u32[]{:S(2)}) collective-permute-start(f32[6,8,128]{2,1,0:T(8,128)S(1)} %get-tuple-element.52), channel_id=1, source_target_pairs={{0,16},{16,0},{32,48},{48,32},{64,80},{80,64},{96,112},{112,96},{1... | collective-permute-start | bytes 73736 | tf_op jit(solution)/shard_map/ppermute | solution.py:527
  18.6 4.6 %collective-permute-start.5 = (f32[6,8,128]{2,1,0:T(8,128)S(1)}, f32[6,8,128]{2,1,0:T(8,128)S(1)}, u32[]{:S(2)}, u32[]{:S(2)}) collective-permute-start(f32[6,8,128]{2,1,0:T(8,128)S(1)} %get-tuple-element.53), channel_id=1, source_target_pairs={{0,112},{16,32},{32,16},{48,64},{64,48},{80,96},{96,80},{112,0},{1... | collective-permute-start | bytes 73736 | tf_op jit(solution)/shard_map/ppermute | solution.py:528
  23.3 4.9 %collective-permute-start.6 = (f32[3,32,128]{2,1,0:T(8,128)S(1)}, f32[3,32,128]{2,1,0:T(8,128)S(1)}, u32[]{:S(2)}, u32[]{:S(2)}) collective-permute-start(f32[3,32,128]{2,1,0:T(8,128)S(1)} %get-tuple-element.55), channel_id=1, source_target_pairs={{0,1},{1,0},{2,3},{3,2},{4,5},{5,4},{6,7},{7,6},{8,9},{9,8},{10,11... | collective-permute-start | bytes 147464 | tf_op jit(solution)/shard_map/ppermute | solution.py:535
  23.4 7.5 %collective-permute-start.7 = (f32[3,32,128]{2,1,0:T(8,128)S(1)}, f32[3,32,128]{2,1,0:T(8,128)S(1)}, u32[]{:S(2)}, u32[]{:S(2)}) collective-permute-start(f32[3,32,128]{2,1,0:T(8,128)S(1)} %get-tuple-element.56), channel_id=1, source_target_pairs={{0,15},{1,2},{2,1},{3,4},{4,3},{5,6},{6,5},{7,8},{8,7},{9,10},{10,... | collective-permute-start | bytes 147464 | tf_op jit(solution)/shard_map/ppermute | solution.py:536
